TPU v7x, 32 devices: a whole 2x2x4 slice. The times are simulated.
32 devices in a mesh: dp: 16 (over z, y, core), seq: 2 (over x).
Axes of the slice: x: 2, y: 2, z: 4, core: 2. Of those that a mesh axis runs over, the one named last changes fastest.
Arguments:
- images: bfloat16 [48, 640, 512], P('dp', 'seq'), may hold values from -6 to 6
- cotangent: bfloat16 [48, 640, 512], P('dp', 'seq'), may hold values from -8 to 8
- lengths: int32 [48], P('dp'), may hold values from 320 to 640, as said below
- routes: int32 [16, 3, 2, 320, 2], P('dp', None, 'seq'), may hold values from 0 to 15, all different within a row; in each aligned block of 320 rows (0 to 319, 320 to 639, ..., all dimensions but the last counted through in order) at most 50 rows name the same one
- attn_norm_gain: bfloat16 [512], P('dp'), may hold values from 0.5 to 1.5
- attn_norm_bias: bfloat16 [512], P('dp'), may hold values from -1.25 to 1.25
- qkv_weight: bfloat16 [512, 1536], P('dp'), may hold values from -0.375 to 0.375
- query_value_bias: bfloat16 [2, 512], P(None, 'dp'), may hold values from -1.25 to 1.25
- proj_weight: bfloat16 [512, 512], P('dp'), may hold values from -0.75 to 0.75
- proj_bias: bfloat16 [512], P('dp'), may hold values from -1.25 to 1.25
- moe_norm_gain: bfloat16 [512], P('dp'), may hold values from 0.5 to 1.5
- moe_norm_bias: bfloat16 [512], P('dp'), may hold values from -1.25 to 1.25
- router_weight: bfloat16 [512, 16], P('dp'), may hold values from -0.25 to 0.25
- up_weight: bfloat16 [16, 512, 2048], P('dp'), may hold values from -0.25 to 0.25
- up_bias: bfloat16 [16, 2048], P('dp'), may hold values from -3 to 3
- down_weight: bfloat16 [16, 2048, 512], P('dp'), may hold values from -1 to 1
- down_bias: bfloat16 [16, 512], P('dp'), may hold values from -6 to 6
Outputs:
- block_out: bfloat16 [48, 640, 512], P('dp', 'seq')
- input_grad: bfloat16 [48, 640, 512], P('dp', 'seq')
- grad_attn_norm_gain: float32 [512], P('dp')
- grad_attn_norm_bias: float32 [512], P('dp')
- grad_qkv_weight: float32 [512, 1536], P('dp')
- grad_query_value_bias: float32 [2, 512], P(None, 'dp')
- grad_proj_weight: float32 [512, 512], P('dp')
- grad_proj_bias: float32 [512], P('dp')
- grad_moe_norm_gain: float32 [512], P('dp')
- grad_moe_norm_bias: float32 [512], P('dp')
- grad_router_weight: float32 [512, 16], P('dp')
- grad_up_weight: float32 [16, 512, 2048], P('dp')
- grad_up_bias: float32 [16, 2048], P('dp')
- grad_down_weight: float32 [16, 2048, 512], P('dp')
- grad_down_bias: float32 [16, 512], P('dp')
Inputs may be any that keep to these rules, and one draw needn't show every extreme that they name: `lengths`: real tokens of each image; its later slots are pads, masked as keys; some image is full and some has half of its slots. `routes`: the 2 experts of a row differ; in each aligned block of 320 rows (one group) no expert is named by more than 50 rows, a bound that some block reaches.
All inputs are finite; a program needn't handle non-finite values.
Results may differ from a plain program's by a relative error of at most 0.023.
Values may be sent and summed in bfloat16 or wider, within the bound.
No kernel may reach another device: no remote copies, remote signals or barrier semaphores. Data moves between devices by JAX's collectives and lax.ppermute only.
A program may use at most 192 MiB of HBM per device.

v0:
```python
import jax
import jax.numpy as jnp
from jax import lax
from jax.sharding import PartitionSpec as P

HD = 64
TOP = 2
MICRO = 3


def layer_norm(values, gain_vec, shift_vec):
    average = jnp.mean(values, axis=-1, keepdims=True)
    centred = values - average
    spread = jnp.mean(centred * centred, axis=-1, keepdims=True)
    return centred * lax.rsqrt(spread + 1e-06) * gain_vec + shift_vec


def exact_gelu(values):
    return jax.nn.gelu(values, approximate=False)


def slot_places(expert_ids, experts, capacity):
    row_count = expert_ids.shape[0]
    flattened = expert_ids.reshape(-1)
    onehot = (flattened[:, None] == jnp.arange(experts, dtype=jnp.int32)[None, :]).astype(jnp.int32)
    before = jnp.cumsum(onehot, axis=0) - onehot
    within = jnp.sum(before * onehot, axis=1)
    places = flattened * capacity + within
    owners = jnp.arange(flattened.shape[0], dtype=jnp.int32) // expert_ids.shape[1]
    slot_table = jnp.full((experts * capacity,), row_count, jnp.int32).at[places].set(owners)
    return (places, slot_table)


def masked_scores(queries, keys_in, key_valid):
    scores = jnp.einsum(
        "nqhd,nkhd->nhqk", queries, keys_in, preferred_element_type=jnp.float32
    ) * HD ** (-0.5)
    return jnp.where(key_valid[:, None, None, :], scores, -1e30)


def attention_forward(queries, keys_in, values, key_valid):
    scores = masked_scores(queries, keys_in, key_valid)
    highest = jnp.max(scores, axis=-1, keepdims=True)
    exp_scores = jnp.exp(scores - highest)
    row_totals = jnp.sum(exp_scores, axis=-1, keepdims=True)
    attn_probs = (exp_scores / row_totals).astype(jnp.bfloat16)
    attended = jnp.einsum("nhqk,nkhd->nqhd", attn_probs, values, preferred_element_type=jnp.float32)
    return (attended.astype(jnp.bfloat16), highest + jnp.log(row_totals))


def attention_backward(queries, keys_in, values, key_valid, log_total, grad_attended):
    score_scale = HD ** (-0.5)
    scores = masked_scores(queries, keys_in, key_valid)
    attn_probs = jnp.exp(scores - log_total)
    grad_values = jnp.einsum(
        "nhqk,nqhd->nkhd",
        attn_probs.astype(jnp.bfloat16),
        grad_attended,
        preferred_element_type=jnp.float32,
    )
    grad_probs = jnp.einsum(
        "nqhd,nkhd->nhqk", grad_attended, values, preferred_element_type=jnp.float32
    )
    inner_sum = jnp.sum(attn_probs * grad_probs, axis=-1, keepdims=True)
    grad_scores = (attn_probs * (grad_probs - inner_sum)).astype(jnp.bfloat16)
    grad_queries = (
        jnp.einsum("nhqk,nkhd->nqhd", grad_scores, keys_in, preferred_element_type=jnp.float32)
        * score_scale
    )
    grad_keys = (
        jnp.einsum("nhqk,nqhd->nkhd", grad_scores, queries, preferred_element_type=jnp.float32)
        * score_scale
    )
    return jnp.stack([grad_queries, grad_keys, grad_values], axis=2).astype(jnp.bfloat16)


def on_device(
    images,
    cotangent,
    lengths,
    routes,
    attn_norm_gain,
    attn_norm_bias,
    qkv_weight,
    query_value_bias,
    proj_weight,
    proj_bias,
    moe_norm_gain,
    moe_norm_bias,
    router_weight,
    up_weight,
    up_bias,
    down_weight,
    down_bias,
):
    seq_count = lax.axis_size("seq")
    dp_count = lax.axis_size("dp")
    per_batch = images.shape[0] // MICRO
    local_len = images.shape[1]
    model_width = images.shape[2]
    tokens = per_batch * local_len
    full_len = local_len * seq_count
    experts = router_weight.shape[1]
    capacity = (5 * tokens * TOP + 4 * experts - 1) // (4 * experts)
    head_cols = model_width // seq_count
    heads_here = head_cols // HD
    local_experts = up_weight.shape[0]
    up_shift = up_bias.astype(jnp.float32)[None, :, None, :]
    down_shift = down_bias.astype(jnp.float32)[None, :, None, :]

    def fetch():
        return (
            lax.all_gather(attn_norm_gain, "dp", axis=0, tiled=True),
            lax.all_gather(attn_norm_bias, "dp", axis=0, tiled=True),
            lax.all_gather(qkv_weight, "dp", axis=0, tiled=True),
            lax.all_gather(query_value_bias, "dp", axis=1, tiled=True),
            lax.all_gather(proj_weight, "dp", axis=0, tiled=True),
            lax.all_gather(proj_bias, "dp", axis=0, tiled=True),
            lax.all_gather(moe_norm_gain, "dp", axis=0, tiled=True),
            lax.all_gather(moe_norm_bias, "dp", axis=0, tiled=True),
            lax.all_gather(router_weight, "dp", axis=0, tiled=True),
        )

    def expert_up(received):
        return (
            jnp.einsum("njcd,jdf->njcf", received, up_weight, preferred_element_type=jnp.float32)
            + up_shift
        )

    dense_totals = None
    expert_totals = None
    out_blocks = []
    grad_blocks = []
    for micro_step in range(MICRO):
        low_first = micro_step * per_batch
        weights_now = fetch()
        (
            gain_first,
            shift_first,
            qkv_full,
            qv_full,
            proj_full,
            proj_shift,
            gain_second,
            shift_second,
            router_full,
        ) = weights_now
        span_in = images[low_first : low_first + per_batch]
        inputs_flat = span_in.reshape(tokens, model_width).astype(jnp.float32)
        normed_one = layer_norm(
            inputs_flat, gain_first.astype(jnp.float32), shift_first.astype(jnp.float32)
        ).astype(jnp.bfloat16)
        qkv_bias = jnp.concatenate(
            [qv_full[0], jnp.zeros((model_width,), jnp.bfloat16), qv_full[1]]
        ).astype(jnp.float32)
        projected = (
            jnp.dot(normed_one, qkv_full, preferred_element_type=jnp.float32) + qkv_bias
        ).astype(jnp.bfloat16)
        by_heads = lax.all_to_all(
            projected.reshape(per_batch, local_len, 3, model_width),
            "seq",
            split_axis=3,
            concat_axis=1,
            tiled=True,
        )
        queries = by_heads[:, :, 0].reshape(per_batch, full_len, heads_here, HD)
        keys_in = by_heads[:, :, 1].reshape(per_batch, full_len, heads_here, HD)
        values = by_heads[:, :, 2].reshape(per_batch, full_len, heads_here, HD)
        lengths_now = lengths[low_first : low_first + per_batch]
        key_valid = jnp.arange(full_len, dtype=jnp.int32)[None, :] < lengths_now[:, None]
        attended, log_total = attention_forward(queries, keys_in, values, key_valid)
        by_tokens = lax.all_to_all(
            attended.reshape(per_batch, full_len, head_cols),
            "seq",
            split_axis=1,
            concat_axis=2,
            tiled=True,
        )
        attended_tok = by_tokens.reshape(tokens, model_width)
        branch = jnp.dot(
            attended_tok, proj_full, preferred_element_type=jnp.float32
        ) + proj_shift.astype(jnp.float32)
        middle = inputs_flat + branch
        normed_two = layer_norm(
            middle, gain_second.astype(jnp.float32), shift_second.astype(jnp.float32)
        ).astype(jnp.bfloat16)
        logits = jnp.dot(normed_two, router_full, preferred_element_type=jnp.float32)
        gate_probs = jax.nn.softmax(logits, axis=-1)
        expert_ids = routes[0, micro_step, 0]
        places, slot_table = slot_places(expert_ids, experts, capacity)
        padded = jnp.concatenate([normed_two, jnp.zeros((1, model_width), jnp.bfloat16)], axis=0)
        send_rows = padded[slot_table].reshape(dp_count, local_experts, capacity, model_width)
        expert_received = lax.all_to_all(send_rows, "dp", split_axis=0, concat_axis=0, tiled=True)
        pre_act = expert_up(expert_received)
        active = exact_gelu(pre_act).astype(jnp.bfloat16)
        result = (
            jnp.einsum("njcf,jfd->njcd", active, down_weight, preferred_element_type=jnp.float32)
            + down_shift
        )
        result_low = result.astype(jnp.bfloat16)
        outputs = (expert_received, result_low)
        received, result_low = outputs
        returned = lax.all_to_all(
            result_low, "dp", split_axis=0, concat_axis=0, tiled=True
        ).reshape(experts * capacity, model_width)
        picked = returned[places].reshape(tokens, TOP, model_width).astype(jnp.float32)
        gate_now = jnp.take_along_axis(gate_probs, expert_ids, axis=1)
        mixture = jnp.sum(gate_now[:, :, None] * picked, axis=1)
        out_blocks.append(
            (middle + mixture).astype(jnp.bfloat16).reshape(per_batch, local_len, model_width)
        )
        weights_back = fetch()
        (
            gain_first,
            shift_first,
            qkv_full,
            qv_full,
            proj_full,
            proj_shift,
            gain_second,
            shift_second,
            router_full,
        ) = weights_back
        grad_out_flat = (
            cotangent[low_first : low_first + per_batch]
            .reshape(tokens, model_width)
            .astype(jnp.float32)
        )
        grad_gate = jnp.sum(grad_out_flat[:, None, :] * picked, axis=2)
        grad_picked = (gate_now[:, :, None] * grad_out_flat[:, None, :]).astype(jnp.bfloat16)
        grad_rows = (
            jnp.zeros((experts * capacity, model_width), jnp.bfloat16)
            .at[places]
            .set(grad_picked.reshape(tokens * TOP, model_width))
        )
        grad_result = lax.all_to_all(
            grad_rows.reshape(dp_count, local_experts, capacity, model_width),
            "dp",
            split_axis=0,
            concat_axis=0,
            tiled=True,
        )
        pre_act = expert_up(received)
        active = exact_gelu(pre_act).astype(jnp.bfloat16)
        grad_active = jnp.einsum(
            "njcd,jfd->njcf", grad_result, down_weight, preferred_element_type=jnp.float32
        )
        step_down = jnp.einsum(
            "njcf,njcd->jfd", active, grad_result, preferred_element_type=jnp.float32
        )
        step_down_shift = jnp.sum(grad_result.astype(jnp.float32), axis=(0, 2))
        gelu_pull = jax.vjp(exact_gelu, pre_act)[1]
        grad_pre = gelu_pull(grad_active)[0].astype(jnp.bfloat16)
        step_up = jnp.einsum(
            "njcd,njcf->jdf", received, grad_pre, preferred_element_type=jnp.float32
        )
        step_up_shift = jnp.sum(grad_pre.astype(jnp.float32), axis=(0, 2))
        grad_sent = jnp.einsum(
            "njcf,jdf->njcd", grad_pre, up_weight, preferred_element_type=jnp.float32
        )
        grad_back = lax.all_to_all(
            grad_sent.astype(jnp.bfloat16), "dp", split_axis=0, concat_axis=0, tiled=True
        ).reshape(experts * capacity, model_width)
        grad_from_experts = jnp.sum(
            grad_back[places].reshape(tokens, TOP, model_width).astype(jnp.float32), axis=1
        )
        chosen = (
            expert_ids[:, :, None] == jnp.arange(experts, dtype=jnp.int32)[None, None, :]
        ).astype(jnp.float32)
        grad_probs = jnp.sum(chosen * grad_gate[:, :, None], axis=1)
        grad_logits = gate_probs * (
            grad_probs - jnp.sum(gate_probs * grad_probs, axis=1, keepdims=True)
        )
        grad_logits = grad_logits.astype(jnp.bfloat16)
        step_router = jnp.einsum(
            "td,te->de", normed_two, grad_logits, preferred_element_type=jnp.float32
        )
        grad_normed_two = grad_from_experts + jnp.einsum(
            "te,de->td", grad_logits, router_full, preferred_element_type=jnp.float32
        )
        norm_pull = jax.vjp(
            layer_norm, middle, gain_second.astype(jnp.float32), shift_second.astype(jnp.float32)
        )[1]
        grad_middle_norm, step_gain_second, step_shift_second = norm_pull(grad_normed_two)
        grad_middle = grad_out_flat + grad_middle_norm
        grad_branch = grad_middle.astype(jnp.bfloat16)
        step_proj = jnp.einsum(
            "td,te->de", attended_tok, grad_branch, preferred_element_type=jnp.float32
        )
        step_proj_shift = jnp.sum(grad_branch.astype(jnp.float32), axis=0)
        grad_attended = jnp.einsum(
            "te,de->td", grad_branch, proj_full, preferred_element_type=jnp.float32
        )
        grad_heads = lax.all_to_all(
            grad_attended.astype(jnp.bfloat16).reshape(per_batch, local_len, model_width),
            "seq",
            split_axis=2,
            concat_axis=1,
            tiled=True,
        )
        stacked = attention_backward(
            queries,
            keys_in,
            values,
            key_valid,
            log_total,
            grad_heads.reshape(per_batch, full_len, heads_here, HD),
        )
        grad_projected = lax.all_to_all(
            stacked.reshape(per_batch, full_len, 3, head_cols),
            "seq",
            split_axis=1,
            concat_axis=3,
            tiled=True,
        ).reshape(tokens, 3 * model_width)
        step_qkv = jnp.einsum(
            "td,te->de", normed_one, grad_projected, preferred_element_type=jnp.float32
        )
        column_sums = jnp.sum(grad_projected.astype(jnp.float32), axis=0)
        step_qv = jnp.stack([column_sums[:model_width], column_sums[2 * model_width :]])
        grad_normed_one = jnp.einsum(
            "te,de->td", grad_projected, qkv_full, preferred_element_type=jnp.float32
        )
        first_pull = jax.vjp(
            layer_norm, inputs_flat, gain_first.astype(jnp.float32), shift_first.astype(jnp.float32)
        )[1]
        grad_inputs_norm, step_gain_first, step_shift_first = first_pull(grad_normed_one)
        grad_blocks.append(
            (grad_middle + grad_inputs_norm)
            .astype(jnp.bfloat16)
            .reshape(per_batch, local_len, model_width)
        )
        dense_step = (
            step_gain_first,
            step_shift_first,
            step_qkv,
            step_qv,
            step_proj,
            step_proj_shift,
            step_gain_second,
            step_shift_second,
            step_router,
        )
        expert_step = (step_up, step_up_shift, step_down, step_down_shift)
        if dense_totals is None:
            dense_totals = dense_step
            expert_totals = expert_step
        else:
            dense_totals = jax.tree.map(
                lambda first_term, second_term: first_term + second_term, dense_totals, dense_step
            )
            expert_totals = jax.tree.map(
                lambda first_term, second_term: first_term + second_term, expert_totals, expert_step
            )
    (
        total_gain_first,
        total_shift_first,
        total_qkv,
        total_qv,
        total_proj,
        total_proj_shift,
        total_gain_second,
        total_shift_second,
        total_router,
    ) = dense_totals
    total_up, total_up_shift, total_down, total_down_shift = expert_totals
    dense_shards = (
        lax.psum_scatter(
            total_gain_first.astype(jnp.bfloat16), "dp", scatter_dimension=0, tiled=True
        ).astype(jnp.float32),
        lax.psum_scatter(
            total_shift_first.astype(jnp.bfloat16), "dp", scatter_dimension=0, tiled=True
        ).astype(jnp.float32),
        lax.psum_scatter(
            total_qkv.astype(jnp.bfloat16), "dp", scatter_dimension=0, tiled=True
        ).astype(jnp.float32),
        lax.psum_scatter(
            total_qv.astype(jnp.bfloat16), "dp", scatter_dimension=1, tiled=True
        ).astype(jnp.float32),
        lax.psum_scatter(
            total_proj.astype(jnp.bfloat16), "dp", scatter_dimension=0, tiled=True
        ).astype(jnp.float32),
        lax.psum_scatter(
            total_proj_shift.astype(jnp.bfloat16), "dp", scatter_dimension=0, tiled=True
        ).astype(jnp.float32),
        lax.psum_scatter(
            total_gain_second.astype(jnp.bfloat16), "dp", scatter_dimension=0, tiled=True
        ).astype(jnp.float32),
        lax.psum_scatter(
            total_shift_second.astype(jnp.bfloat16), "dp", scatter_dimension=0, tiled=True
        ).astype(jnp.float32),
        lax.psum_scatter(
            total_router.astype(jnp.bfloat16), "dp", scatter_dimension=0, tiled=True
        ).astype(jnp.float32),
    )
    (
        shard_gain_first,
        shard_shift_first,
        shard_qkv,
        shard_qv,
        shard_proj,
        shard_proj_shift,
        shard_gain_second,
        shard_shift_second,
        shard_router,
    ) = dense_shards
    summed = (
        lax.psum(shard_gain_first.astype(jnp.bfloat16), "seq").astype(jnp.float32),
        lax.psum(shard_shift_first.astype(jnp.bfloat16), "seq").astype(jnp.float32),
        lax.psum(shard_qkv.astype(jnp.bfloat16), "seq").astype(jnp.float32),
        lax.psum(shard_qv.astype(jnp.bfloat16), "seq").astype(jnp.float32),
        lax.psum(shard_proj.astype(jnp.bfloat16), "seq").astype(jnp.float32),
        lax.psum(shard_proj_shift.astype(jnp.bfloat16), "seq").astype(jnp.float32),
        lax.psum(shard_gain_second.astype(jnp.bfloat16), "seq").astype(jnp.float32),
        lax.psum(shard_shift_second.astype(jnp.bfloat16), "seq").astype(jnp.float32),
        lax.psum(shard_router.astype(jnp.bfloat16), "seq").astype(jnp.float32),
        lax.psum(total_up.astype(jnp.bfloat16), "seq").astype(jnp.float32),
        lax.psum(total_up_shift.astype(jnp.bfloat16), "seq").astype(jnp.float32),
        lax.psum(total_down.astype(jnp.bfloat16), "seq").astype(jnp.float32),
        lax.psum(total_down_shift.astype(jnp.bfloat16), "seq").astype(jnp.float32),
    )
    (
        final_gain_first,
        final_shift_first,
        final_qkv,
        final_qv,
        final_proj,
        final_proj_shift,
        final_gain_second,
        final_shift_second,
        final_router,
        final_up,
        final_up_shift,
        final_down,
        final_down_shift,
    ) = summed
    return (
        jnp.concatenate(out_blocks, axis=0),
        jnp.concatenate(grad_blocks, axis=0),
        final_gain_first,
        final_shift_first,
        final_qkv,
        final_qv,
        final_proj,
        final_proj_shift,
        final_gain_second,
        final_shift_second,
        final_router,
        final_up,
        final_up_shift,
        final_down,
        final_down_shift,
    )


def solution(mesh):
    return jax.shard_map(
        on_device,
        mesh=mesh,
        in_specs=(
            P("dp", "seq", None),
            P("dp", "seq", None),
            P("dp"),
            P("dp", None, "seq", None, None),
            P("dp"),
            P("dp"),
            P("dp", None),
            P(None, "dp"),
            P("dp", None),
            P("dp"),
            P("dp"),
            P("dp"),
            P("dp", None),
            P("dp", None, None),
            P("dp", None),
            P("dp", None, None),
            P("dp", None),
        ),
        out_specs=(
            P("dp", "seq", None),
            P("dp", "seq", None),
            P("dp"),
            P("dp"),
            P("dp", None),
            P(None, "dp"),
            P("dp", None),
            P("dp"),
            P("dp"),
            P("dp"),
            P("dp", None),
            P("dp", None, None),
            P("dp", None),
            P("dp", None, None),
            P("dp", None),
        ),
        check_vma=False,
    )
```

profile of v0, /device:TPU:0, one launch (start us, length us, event | category | flops | bytes accessed | tf_op | source)
XLA Modules:
  0.0 1329.0 jit_solution(16141388931027853948)
XLA Ops:
  15.4 35.9 %all-reduce.14 = (bf16[512]{0:T(512)(128)(2,1)S(1)}, bf16[512]{0:T(512)(128)(2,1)S(1)}, bf16[512]{0:T(512)(128)(2,1)S(1)}, bf16[512]{0:T(512)(128)(2,1)S(1)}, bf16[512]{0:T(512)(128)(2,1)S(1)}) all-reduce(bf16[512]{0:T(512)(128)(2,1)S(1)} %dynamic-update-slice.1, ...), channel_id=1, replica_groups=mesh['dp'=16,'seq'=2] {'dp'}, use_global_device_ids=true, to_apply=%add.4 | all-reduce | flops 2560 | bytes 10240
  51.4 17.4 %all-gather = bf16[16,32,2]{1,2,0:T(2,128)(2,1)S(1)} all-gather(bf16[1,32,2]{1,2,0:T(2,128)(2,1)} %bitcast.1216), channel_id=1, replica_groups=mesh['dp'=16,'seq'=2] {'dp'}, dimensions={0}, use_global_device_ids=true | all-gather | bytes 2176 | tf_op jit(solution)/shard_map/all_gather | solution.py:116
  68.9 19.4 %all-gather.1 = bf16[16,32,16]{1,2,0:T(8,128)(2,1)S(1)} all-gather(bf16[1,32,16]{1,2,0:T(8,128)(2,1)} %bitcast.1212), channel_id=1, replica_groups=mesh['dp'=16,'seq'=2] {'dp'}, dimensions={0}, use_global_device_ids=true | all-gather | bytes 17408 | tf_op jit(solution)/shard_map/all_gather | solution.py:121
  110.6 4.7 all-to-all-start.4
  122.3 13.0 all-to-all-done.4
  135.3 4.6 all-to-all-start.8
  140.0 18.9 %all_gather.22 = bf16[512,512]{1,0:T(8,128)(2,1)S(1)} all-gather(bf16[32,512]{1,0:T(8,128)(2,1)S(1)} %copy-done.134), channel_id=1, replica_groups=mesh['dp'=16,'seq'=2] {'dp'}, dimensions={0}, use_global_device_ids=true | all-gather | bytes 557056 | tf_op jit(solution)/shard_map/all_gather | solution.py:117
  158.9 5.2 copy.466
  169.8 5.0 copy.467
  212.5 4.5 all-to-all-start.5
  231.1 5.4 gather_fusion.11
  237.0 9.6 scatter_custom_fusion.5
  266.1 7.8 all-to-all-done.20
  273.9 6.3 all-to-all-start.6
  288.4 5.4 gather_fusion.10
  294.2 9.6 scatter_custom_fusion.4
  306.0 6.1 all-to-all-start.16
  329.2 6.9 fusion.128
  336.1 6.0 all-to-all-start.10
  342.1 19.0 %fusion.174 = bf16[16,1,50,512]{3,2,1,0:T(8,128)(2,1)} fusion(bf16[1,2048,512]{2,1,0:T(8,128)(2,1)S(1)} %copy-done, f32[512]{0:T(512)S(1)} %bitcast.1213, f32[16,50,2048]{2,1,0:T(8,128)} %fusion.128, f32[2048]{0:T(1024)S(1)} %bitcast.1202), kind=kOutput, calls=%fused_computation.224 | convolution fusion | flops 1786675200 | bytes 9480192 | tf_op jit(solution)/shard_map/njcf,jfd->njcd/dot_general | solution.py:197
  363.8 6.5 all-to-all-start.7
  370.3 21.2 %convert_reduce_fusion.1 = (f32[2048]{0:T(1024)}, bf16[16,1,50,2048]{3,2,0,1:T(8,128)(2,1)S(1)}) fusion(bf16[1,2048,512]{2,1,0:T(8,128)(2,1)S(1)} %copy-done, bf16[16,1,50,512]{3,2,1,0:T(8,128)(2,1)} %all-to-all-done.16, f32[2048]{0:T(1024)S(1)} %bitcast.1203, f32[16,50,2048]{2,1,0:T(8,128)} %fusion.128), kind=kOutput, calls=%fused_computation.76 | convolution fusion | flops 1800599552 | bytes 12763136 | tf_op jit(solution)/shard_map/njcd,jfd->njcf/dot_general | solution.py:245
  391.5 5.1 fusion.126
  399.7 6.1 all-to-all-start.17
  405.9 19.0 %fusion.177 = bf16[16,1,50,512]{3,2,1,0:T(8,128)(2,1)} fusion(bf16[1,2048,512]{2,1,0:T(8,128)(2,1)S(1)} %copy-done, f32[512]{0:T(512)S(1)} %bitcast.1214, f32[16,50,2048]{2,1,0:T(8,128)} %fusion.126, f32[2048]{0:T(1024)S(1)} %bitcast.1204), kind=kOutput, calls=%fused_computation.225 | convolution fusion | flops 1786675200 | bytes 9480192 | tf_op jit(solution)/shard_map/njcf,jfd->njcd/dot_general | solution.py:197
  426.7 6.1 all-to-all-start.11
  432.8 21.2 %convert_reduce_fusion = (f32[2048]{0:T(1024)}, bf16[16,1,50,2048]{3,2,0,1:T(8,128)(2,1)S(1)}) fusion(bf16[1,2048,512]{2,1,0:T(8,128)(2,1)S(1)} %copy-done, bf16[16,1,50,512]{3,2,1,0:T(8,128)(2,1)} %all-to-all-done.20, f32[2048]{0:T(1024)S(1)} %bitcast.1205, f32[16,50,2048]{2,1,0:T(8,128)} %fusion.126), kind=kOutput, calls=%fused_computation.75 | convolution fusion | flops 1800599552 | bytes 12763136 | tf_op jit(solution)/shard_map/njcd,jfd->njcf/dot_general | solution.py:245
  458.9 6.2 all-to-all-start.21
  471.9 4.6 multiply_reduce_fusion.4
  491.7 4.6 multiply_reduce_fusion.3
  551.9 4.9 fusion.196
  556.8 7.1 multiply_reduce_fusion
  576.5 4.8 fusion.193
  581.3 6.9 multiply_reduce_fusion.1
  595.8 4.8 pad_maximum_fusion.2
  605.2 6.0 multiply_convert_fusion.1
  619.2 4.8 pad_maximum_fusion.1
  668.9 4.6 all-to-all-start
  673.6 20.5 %fusion.208 = f32[2048,512,1]{1,0,2:T(8,128)} fusion(bf16[16,1,50,512]{3,2,1,0:T(8,128)(2,1)} %all-to-all-done.16, f32[16,50,2048]{2,1,0:T(8,128)} %fusion.128, f32[2048]{0:T(1024)S(1)} %bitcast.1206), kind=kOutput, calls=%fused_computation.294 | convolution fusion | flops 1785856000 | bytes 11575296 | tf_op jit(solution)/shard_map/njcf,njcd->jfd/dot_general | solution.py:248
  694.1 5.0 copy.465
  718.2 6.7 fusion.84
  738.2 6.1 all-to-all-start.2
  744.4 6.7 fusion.80
  751.4 5.4 gather_fusion.9
  757.9 8.9 scatter_custom_fusion.3
  768.0 6.2 all-to-all-start.12
  781.1 17.5 %fusion.171 = bf16[16,1,50,512]{3,2,1,0:T(8,128)(2,1)} fusion(bf16[1,2048,512]{2,1,0:T(8,128)(2,1)S(1)} %copy-done, f32[512]{0:T(512)S(1)} %bitcast.1215, f32[16,50,2048]{2,1,0:T(8,128)S(1)} %fusion.130, f32[2048]{0:T(1024)S(1)} %bitcast.1207), kind=kOutput, calls=%fused_computation.223 | convolution fusion | flops 1786675200 | bytes 9480192 | tf_op jit(solution)/shard_map/njcf,jfd->njcd/dot_general | solution.py:197
  798.6 6.1 all-to-all-start.3
  804.8 20.9 %convert_reduce_fusion.2 = (f32[2048]{0:T(1024)}, bf16[16,1,50,2048]{3,2,0,1:T(8,128)(2,1)S(1)}) fusion(bf16[1,2048,512]{2,1,0:T(8,128)(2,1)S(1)} %copy-done, bf16[16,1,50,512]{3,2,1,0:T(8,128)(2,1)S(1)} %all-to-all-done.12, f32[2048]{0:T(1024)S(1)} %bitcast.1208, f32[16,50,2048]{2,1,0:T(8,128)} %copy-done.204), kind=kOutput, calls=%fused_computation.77 | convolution fusion | flops 1800599552 | bytes 12763136 | tf_op jit(solution)/shard_map/njcd,jfd->njcf/dot_general | solution.py:245
  830.6 6.4 all-to-all-start.13
  847.3 4.6 multiply_reduce_fusion.5
  853.0 4.8 all-to-all-done.13
  886.8 7.1 all-to-all-done.14
  900.6 6.9 multiply_reduce_fusion.2
  928.8 20.3 %fusion.211 = f32[2048,512,1]{1,0,2:T(8,128)} fusion(bf16[16,1,50,512]{3,2,1,0:T(8,128)(2,1)} %copy-done.34, f32[16,50,2048]{2,1,0:T(8,128)} %copy-done.204, f32[2048]{0:T(1024)S(1)} %bitcast.1209), kind=kOutput, calls=%fused_computation.297 | convolution fusion | flops 1785856000 | bytes 11575296 | tf_op jit(solution)/shard_map/njcf,njcd->jfd/dot_general | solution.py:248
  964.4 21.1 %fusion.105 = bf16[1,2048,512]{2,1,0:T(8,128)(2,1)} fusion(f32[2048,512,1]{1,0,2:T(8,128)} %fusion.208, f32[2048,512,1]{1,0,2:T(8,128)} %fusion.211, bf16[16,1,50,512]{3,2,1,0:T(8,128)(2,1)} %all-to-all-done.20, f32[16,50,2048]{2,1,0:T(8,128)} %fusion.126, f32[2048]{0:T(1024)S(1)} %bitcast.1210), kind=kOutput, calls=%fused_computation.180 | convolution fusion | flops 1789001728 | bytes 17866752 | tf_op jit(solution)/shard_map/njcf,njcd->jfd/dot_general | solution.py:248
  996.1 8.6 fusion.111
  1004.7 21.0 %reduce-scatter.9.cloned.1.call-done = bf16[32,1536]{1,0:T(8,128)(2,1)} async-done(((bf16[512,1536]{1,0:T(8,128)(2,1)}), bf16[32,1536]{1,0:T(8,128)(2,1)}) %reduce-scatter.9.cloned.1.call-update) | async-done | bytes 98320 | tf_op jit(solution)/shard_map/reduce_scatter | solution.py:374
  1029.5 54.9 %reduce-scatter.15.cloned.1.call-done = bf16[32,16]{1,0:T(8,128)(2,1)} async-done(((bf16[512,16]{1,0:T(8,128)(2,1)}), bf16[32,16]{1,0:T(8,128)(2,1)}) %reduce-scatter.15.cloned.1.call-update) | async-done | bytes 1040
  1090.3 30.0 %all-reduce.13 = (bf16[512]{0:T(512)(128)(2,1)S(1)}, bf16[512]{0:T(512)(128)(2,1)S(1)}, bf16[512]{0:T(512)(128)(2,1)S(1)}, bf16[512]{0:T(512)(128)(2,1)S(1)}, bf16[512]{0:T(512)(128)(2,1)S(1)}) all-reduce(bf16[512]{0:T(512)(128)(2,1)S(1)} %add_convert_fusion.15, ...), channel_id=2, replica_groups=mesh['dp'=16,'seq'=2] {'dp'}, use_global_device_ids=true, to_apply=%region_72.74.clone | all-reduce | flops 2560 | bytes 10240
  1124.1 18.8 %reduce-scatter.13.cloned.1.call-done = bf16[32,2]{1,0:T(8,128)(2,1)} async-done(((bf16[512,2]{1,0:T(8,128)(2,1)}), bf16[32,2]{1,0:T(8,128)(2,1)}) %reduce-scatter.13.cloned.1.call-update) | async-done | bytes 144
  1143.8 57.9 %reduce-scatter.11.cloned.1.call-done = bf16[32,512]{1,0:T(8,128)(2,1)} async-done(((bf16[512,512]{1,0:T(8,128)(2,1)}), bf16[32,512]{1,0:T(8,128)(2,1)}) %reduce-scatter.11.cloned.1.call-update) | async-done | bytes 32784 | tf_op jit(solution)/shard_map/reduce_scatter | solution.py:380
  1201.6 9.8 all-reduce.15
  1216.9 96.3 %all-reduce.19.cloned.1.call-done = (bf16[32,1536]{1,0:T(8,128)(2,1)}, bf16[1,512,2048]{2,1,0:T(8,128)(2,1)}, bf16[1,2048,512]{2,1,0:T(8,128)(2,1)}) async-done(((bf16[32,1536]{1,0:T(8,128)(2,1)}, bf16[1,512,2048]{2,1,0:T(8,128)(2,1)}, bf16[1,2048,512]{2,1,0:T(8,128)(2,1)}), (bf16[32,1536]{1,0:T(8,128)(2,1)}, bf16[1,512,2048]{2,1,0:T(8,128)(2,1)}, ...) | async-done | bytes 4292624 | tf_op jit(solution)/shard_map/psum | solution.py:410
  (839 shorter events, 475.5 us)
Async XLA Ops:
  7.2 334.9 %copy-start = (bf16[1,2048,512]{2,1,0:T(8,128)(2,1)S(1)}, bf16[1,2048,512]{2,1,0:T(8,128)(2,1)}, u32[]{:S(2)}) copy-start(bf16[1,2048,512]{2,1,0:T(8,128)(2,1)} %param.34) | copy-start | bytes 6291460
  7.2 91.2 %copy-start.191 = (s32[3]{0:T(128)S(1)}, s32[3]{0:T(128)}, u32[]{:S(2)}) copy-start(s32[3]{0:T(128)} %param.21) | copy-start | bytes 40
  7.2 93.3 %copy-start.8 = (bf16[3,320,512]{2,1,0:T(8,128)(2,1)S(1)}, bf16[3,320,512]{2,1,0:T(8,128)(2,1)}, u32[]{:S(2)}) copy-start(bf16[3,320,512]{2,1,0:T(8,128)(2,1)} %param.19) | copy-start | bytes 2949124
  7.2 94.5 %all-gather.4.cloned.1.call-start = ((), (), s32[]{:S(2)}) async-start(), calls=%async_computation.28 | async-start | bytes 1671168 | tf_op jit(solution)/shard_map/all_gather | solution.py:115
  51.3 64.0 %copy-start.123 = (f32[512]{0:T(512)}, f32[512]{0:T(512)S(1)}, u32[]{:S(2)}) copy-start(f32[512]{0:T(512)S(1)} %convert_element_type.598) | copy-start | bytes 6148
  51.3 64.0 %copy-start.92 = (f32[512]{0:T(512)}, f32[512]{0:T(512)S(1)}, u32[]{:S(2)}) copy-start(f32[512]{0:T(512)S(1)} %convert_element_type.597) | copy-start | bytes 6148
  51.4 178.0 %copy-start.83 = (f32[512]{0:T(512)}, f32[512]{0:T(512)S(1)}, u32[]{:S(2)}) copy-start(f32[512]{0:T(512)S(1)} %convert_element_type.607) | copy-start | bytes 6148
  51.4 176.2 %copy-start.126 = (f32[512]{0:T(512)}, f32[512]{0:T(512)S(1)}, u32[]{:S(2)}) copy-start(f32[512]{0:T(512)S(1)} %convert_element_type.606) | copy-start | bytes 6148
  51.4 178.0 %copy-start.162 = (f32[512]{0:T(512)}, f32[512]{0:T(512)S(1)}, u32[]{:S(2)}) copy-start(f32[512]{0:T(512)S(1)} %convert_element_type.608) | copy-start | bytes 6148
  88.4 199.7 %copy-start.68 = (bf16[512,16]{0,1:T(8,128)(2,1)}, bf16[512,16]{0,1:T(8,128)(2,1)S(1)}, u32[]{:S(2)}) copy-start(bf16[512,16]{0,1:T(8,128)(2,1)S(1)} %reshape.1577) | copy-start | bytes 49156
  110.6 24.8 %all-to-all-start.4 = ((bf16[1,320,3,512]{1,2,0,3:T(4,128)(2,1)}), bf16[1,320,3,512]{1,2,0,3:T(4,128)(2,1)}, u32[]{:S(2)}, u32[]{:S(2)}) async-start(bf16[1,320,3,512]{1,2,0,3:T(4,128)(2,1)} %copy.381), calls=%async_computation.4 | async-start | bytes 3145728 | tf_op jit(solution)/shard_map/all_to_all | solution.py:159
  135.3 34.5 %all-to-all-start.8 = ((bf16[1,320,3,512]{1,2,0,3:T(4,128)(2,1)}), bf16[1,320,3,512]{1,2,0,3:T(4,128)(2,1)}, u32[]{:S(2)}, u32[]{:S(2)}) async-start(bf16[1,320,3,512]{1,2,0,3:T(4,128)(2,1)} %copy.395), calls=%async_computation.8 | async-start | bytes 3145728 | tf_op jit(solution)/shard_map/all_to_all | solution.py:159
  158.9 68.7 %copy-start.5 = (bf16[512,512]{1,0:T(8,128)(2,1)}, bf16[512,512]{1,0:T(8,128)(2,1)S(1)}, u32[]{:S(2)}) copy-start(bf16[512,512]{1,0:T(8,128)(2,1)S(1)} %all_gather.22) | copy-start | bytes 1572868
  166.5 34.5 %copy-start.37 = (bf16[1,640,1,256]{1,3,2,0:T(8,128)(2,1)}, bf16[1,640,1,256]{1,3,2,0:T(8,128)(2,1)S(1)}, u32[]{:S(2)}) copy-start(bf16[1,640,1,256]{1,3,2,0:T(8,128)(2,1)S(1)} %copy.386) | copy-start | bytes 983044
  167.8 33.2 %copy-start.39 = (bf16[1,640,1,256]{1,3,2,0:T(8,128)(2,1)}, bf16[1,640,1,256]{1,3,2,0:T(8,128)(2,1)S(1)}, u32[]{:S(2)}) copy-start(bf16[1,640,1,256]{1,3,2,0:T(8,128)(2,1)S(1)} %copy.385) | copy-start | bytes 983044
  196.9 15.6 %all-to-all-start.9 = ((bf16[2,2,40960]{2,1,0:T(2,128)(2,1)}), bf16[2,2,40960]{2,1,0:T(2,128)(2,1)}, u32[]{:S(2)}, u32[]{:S(2)}) async-start(bf16[2,2,40960]{2,1,0:T(2,128)(2,1)} %reshape.1643), calls=%async_computation.9 | async-start | bytes 655360 | tf_op jit(solution)/shard_map/all_to_all | solution.py:172
  212.5 11.6 all-to-all-start.5
  248.8 25.1 %all-to-all-start.20 = ((bf16[16,1,50,512]{3,2,1,0:T(8,128)(2,1)}), bf16[16,1,50,512]{3,2,1,0:T(8,128)(2,1)}, u32[]{:S(2)}, u32[]{:S(2)}) async-start(bf16[16,1,50,512]{3,2,1,0:T(8,128)(2,1)} %bitcast.1127), calls=%async_computation.20 | async-start | bytes 1835008 | tf_op jit(solution)/shard_map/all_to_all | solution.py:236
  253.7 70.2 %copy-start.19 = (s32[1,1,1,320,2]{4,3,2,1,0:T(8,128)}, s32[1,1,1,320,2]{4,3,2,1,0:T(8,128)S(1)}, u32[]{:S(2)}) copy-start(s32[1,1,1,320,2]{4,3,2,1,0:T(8,128)S(1)} %copy.481) | copy-start | bytes 7684
  273.9 32.1 %all-to-all-start.6 = ((bf16[16,1,50,512]{3,2,1,0:T(8,128)(2,1)}), bf16[16,1,50,512]{3,2,1,0:T(8,128)(2,1)}, u32[]{:S(2)}, u32[]{:S(2)}) async-start(bf16[16,1,50,512]{3,2,1,0:T(8,128)(2,1)} %bitcast.1126), calls=%async_computation.6 | async-start | bytes 1835008 | tf_op jit(solution)/shard_map/all_to_all | solution.py:193
  293.9 30.7 %copy-start.29 = (bf16[320,512]{1,0:T(8,128)(2,1)S(1)}, bf16[320,512]{1,0:T(8,128)(2,1)}, u32[]{:S(2)}) copy-start(bf16[320,512]{1,0:T(8,128)(2,1)} %copy-done.28) | copy-start | bytes 983044
  306.0 30.1 %all-to-all-start.16 = ((bf16[16,1,50,512]{3,2,1,0:T(8,128)(2,1)}), bf16[16,1,50,512]{3,2,1,0:T(8,128)(2,1)}, u32[]{:S(2)}, u32[]{:S(2)}) async-start(bf16[16,1,50,512]{3,2,1,0:T(8,128)(2,1)} %bitcast.1128), calls=%async_computation.16 | async-start | bytes 1835008 | tf_op jit(solution)/shard_map/all_to_all | solution.py:236
  316.3 89.5 %copy-start.196 = (f32[1,512]{1,0:T(1,128)}, f32[1,512]{1,0:T(1,128)S(1)}, u32[]{:S(2)}) copy-start(f32[1,512]{1,0:T(1,128)S(1)} %add.641) | copy-start | bytes 6148
  336.1 26.8 %all-to-all-start.10 = ((bf16[16,1,50,512]{3,2,1,0:T(8,128)(2,1)}), bf16[16,1,50,512]{3,2,1,0:T(8,128)(2,1)S(1)}, u32[]{:S(2)}, u32[]{:S(2)}) async-start(bf16[16,1,50,512]{3,2,1,0:T(8,128)(2,1)} %bitcast.83), calls=%async_computation.10 | async-start | bytes 1835008 | tf_op jit(solution)/shard_map/all_to_all | solution.py:193
  363.8 35.9 %all-to-all-start.7 = ((bf16[16,1,50,512]{3,2,1,0:T(8,128)(2,1)}), bf16[16,1,50,512]{3,2,1,0:T(8,128)(2,1)S(1)}, u32[]{:S(2)}, u32[]{:S(2)}) async-start(bf16[16,1,50,512]{3,2,1,0:T(8,128)(2,1)} %fusion.174), calls=%async_computation.7 | async-start | bytes 1835008 | tf_op jit(solution)/shard_map/all_to_all | solution.py:203
  399.7 27.0 %all-to-all-start.17 = ((bf16[16,1,50,512]{3,2,1,0:T(8,128)(2,1)}), bf16[16,1,50,512]{3,2,1,0:T(8,128)(2,1)}, u32[]{:S(2)}, u32[]{:S(2)}) async-start(bf16[16,1,50,512]{3,2,1,0:T(8,128)(2,1)} %fusion.161), calls=%async_computation.17 | async-start | bytes 1835008 | tf_op jit(solution)/shard_map/all_to_all | solution.py:261
  426.7 32.2 %all-to-all-start.11 = ((bf16[16,1,50,512]{3,2,1,0:T(8,128)(2,1)}), bf16[16,1,50,512]{3,2,1,0:T(8,128)(2,1)S(1)}, u32[]{:S(2)}, u32[]{:S(2)}) async-start(bf16[16,1,50,512]{3,2,1,0:T(8,128)(2,1)} %fusion.177), calls=%async_computation.11 | async-start | bytes 1835008 | tf_op jit(solution)/shard_map/all_to_all | solution.py:203
  458.9 38.7 %all-to-all-start.21 = ((bf16[16,1,50,512]{3,2,1,0:T(8,128)(2,1)}), bf16[16,1,50,512]{3,2,1,0:T(8,128)(2,1)}, u32[]{:S(2)}, u32[]{:S(2)}) async-start(bf16[16,1,50,512]{3,2,1,0:T(8,128)(2,1)} %fusion.156), calls=%async_computation.21 | async-start | bytes 1835008 | tf_op jit(solution)/shard_map/all_to_all | solution.py:261
  529.4 11.6 all-to-all-start.22
  541.0 30.4 %all-to-all-start.18 = ((bf16[2,2,40960]{2,1,0:T(2,128)(2,1)}), bf16[2,2,40960]{2,1,0:T(2,128)(2,1)}, u32[]{:S(2)}, u32[]{:S(2)}) async-start(bf16[2,2,40960]{2,1,0:T(2,128)(2,1)} %reshape.1647), calls=%async_computation.18 | async-start | bytes 655360 | tf_op jit(solution)/shard_map/all_to_all | solution.py:294
  600.7 23.3 %all-to-all-start.23 = ((bf16[1,640,3,256]{3,2,0,1:T(4,128)(2,1)}), bf16[1,640,3,256]{3,2,0,1:T(4,128)(2,1)}, u32[]{:S(2)}, u32[]{:S(2)}) async-start(bf16[1,640,3,256]{3,2,0,1:T(4,128)(2,1)} %pad_maximum_fusion.2), calls=%async_computation.23 | async-start | bytes 2621440 | tf_op jit(solution)/shard_map/all_to_all | solution.py:309
  623.9 22.0 %all-to-all-start.19 = ((bf16[1,640,3,256]{3,2,0,1:T(4,128)(2,1)}), bf16[1,640,3,256]{3,2,0,1:T(4,128)(2,1)}, u32[]{:S(2)}, u32[]{:S(2)}) async-start(bf16[1,640,3,256]{3,2,0,1:T(4,128)(2,1)} %pad_maximum_fusion.1), calls=%async_computation.19 | async-start | bytes 2621440 | tf_op jit(solution)/shard_map/all_to_all | solution.py:309
  668.9 25.1 %all-to-all-start = ((bf16[1,320,3,512]{1,2,0,3:T(4,128)(2,1)}), bf16[1,320,3,512]{1,2,0,3:T(4,128)(2,1)}, u32[]{:S(2)}, u32[]{:S(2)}) async-start(bf16[1,320,3,512]{1,2,0,3:T(4,128)(2,1)} %copy.366), calls=%async_computation | async-start | bytes 3145728 | tf_op jit(solution)/shard_map/all_to_all | solution.py:159
  714.6 12.3 all-to-all-start.1
  738.2 29.7 %all-to-all-start.2 = ((bf16[16,1,50,512]{3,2,1,0:T(8,128)(2,1)}), bf16[16,1,50,512]{3,2,1,0:T(8,128)(2,1)}, u32[]{:S(2)}, u32[]{:S(2)}) async-start(bf16[16,1,50,512]{3,2,1,0:T(8,128)(2,1)} %bitcast.1129), calls=%async_computation.2 | async-start | bytes 1835008 | tf_op jit(solution)/shard_map/all_to_all | solution.py:193
  768.0 30.7 %all-to-all-start.12 = ((bf16[16,1,50,512]{3,2,1,0:T(8,128)(2,1)}), bf16[16,1,50,512]{3,2,1,0:T(8,128)(2,1)S(1)}, u32[]{:S(2)}, u32[]{:S(2)}) async-start(bf16[16,1,50,512]{3,2,1,0:T(8,128)(2,1)} %bitcast.1130), calls=%async_computation.12 | async-start | bytes 1835008 | tf_op jit(solution)/shard_map/all_to_all | solution.py:236
  798.6 32.0 %all-to-all-start.3 = ((bf16[16,1,50,512]{3,2,1,0:T(8,128)(2,1)}), bf16[16,1,50,512]{3,2,1,0:T(8,128)(2,1)}, u32[]{:S(2)}, u32[]{:S(2)}) async-start(bf16[16,1,50,512]{3,2,1,0:T(8,128)(2,1)} %fusion.171), calls=%async_computation.3 | async-start | bytes 1835008 | tf_op jit(solution)/shard_map/all_to_all | solution.py:203
  830.6 27.3 %all-to-all-start.13 = ((bf16[16,1,50,512]{3,2,1,0:T(8,128)(2,1)}), bf16[16,1,50,512]{3,2,1,0:T(8,128)(2,1)}, u32[]{:S(2)}, u32[]{:S(2)}) async-start(bf16[16,1,50,512]{3,2,1,0:T(8,128)(2,1)} %fusion.166), calls=%async_computation.13 | async-start | bytes 1835008 | tf_op jit(solution)/shard_map/all_to_all | solution.py:261
  883.3 10.6 all-to-all-start.14
  924.2 24.9 %all-to-all-start.15 = ((bf16[1,640,3,256]{3,2,0,1:T(4,128)(2,1)}), bf16[1,640,3,256]{3,2,0,1:T(4,128)(2,1)}, u32[]{:S(2)}, u32[]{:S(2)}) async-start(bf16[1,640,3,256]{3,2,0,1:T(4,128)(2,1)} %pad_maximum_fusion), calls=%async_computation.15 | async-start | bytes 2621440 | tf_op jit(solution)/shard_map/all_to_all | solution.py:309
  928.7 97.0 %reduce-scatter.9.cloned.1.call-start = ((), (), s32[]{:S(2)}) async-start(), calls=%async_computation.29 | async-start | bytes 1671168 | tf_op jit(solution)/shard_map/reduce_scatter | solution.py:374
  964.3 120.1 %reduce-scatter.15.cloned.1.call-start = ((), (), s32[]{:S(2)}) async-start(), calls=%async_computation.32 | async-start | bytes 139264
  990.8 152.2 %reduce-scatter.13.cloned.1.call-start = ((), (), s32[]{:S(2)}) async-start(), calls=%async_computation.31 | async-start | bytes 139264
  993.1 208.5 %reduce-scatter.11.cloned.1.call-start = ((), (), s32[]{:S(2)}) async-start(), calls=%async_computation.30 | async-start | bytes 557056 | tf_op jit(solution)/shard_map/reduce_scatter | solution.py:380
  995.9 31.3 %copy-start.174 = (f32[512]{0:T(512)S(1)}, f32[512]{0:T(512)}, u32[]{:S(2)}) copy-start(f32[512]{0:T(512)} %convert_reduce_fusion.6) | copy-start | bytes 6148
  996.0 31.3 %copy-start.175 = (f32[512]{0:T(512)S(1)}, f32[512]{0:T(512)}, u32[]{:S(2)}) copy-start(f32[512]{0:T(512)} %convert_reduce_fusion.7) | copy-start | bytes 6148
  996.0 31.3 %copy-start.177 = (f32[2048]{0:T(1024)S(1)}, f32[2048]{0:T(1024)}, u32[]{:S(2)}) copy-start(f32[2048]{0:T(1024)} %get-tuple-element.162) | copy-start | bytes 24580
  996.0 31.3 %copy-start.178 = (f32[2048]{0:T(1024)S(1)}, f32[2048]{0:T(1024)}, u32[]{:S(2)}) copy-start(f32[2048]{0:T(1024)} %get-tuple-element.158) | copy-start | bytes 24580
  996.0 31.3 %copy-start.179 = (f32[2048]{0:T(1024)S(1)}, f32[2048]{0:T(1024)}, u32[]{:S(2)}) copy-start(f32[2048]{0:T(1024)} %get-tuple-element.160) | copy-start | bytes 24580
  996.0 31.3 %copy-start.65 = (bf16[1,320,512]{2,1,0:T(8,128)(2,1)S(1)}, bf16[1,320,512]{2,1,0:T(8,128)(2,1)}, u32[]{:S(2)}) copy-start(bf16[1,320,512]{2,1,0:T(8,128)(2,1)} %get-tuple-element.105) | copy-start | bytes 983044
  996.0 33.4 %copy-start.187 = (f32[512]{0:T(512)S(1)}, f32[512]{0:T(512)}, u32[]{:S(2)}) copy-start(f32[512]{0:T(512)} %get-tuple-element.50) | copy-start | bytes 6148
  996.0 33.4 %copy-start.188 = (f32[512]{0:T(512)S(1)}, f32[512]{0:T(512)}, u32[]{:S(2)}) copy-start(f32[512]{0:T(512)} %get-tuple-element.122) | copy-start | bytes 6148
  996.0 33.4 %copy-start.190 = (f32[512]{0:T(512)S(1)}, f32[512]{0:T(512)}, u32[]{:S(2)}) copy-start(f32[512]{0:T(512)} %get-tuple-element.49) | copy-start | bytes 6148
  996.0 33.4 %copy-start.185 = (f32[512]{0:T(512)S(1)}, f32[512]{0:T(512)}, u32[]{:S(2)}) copy-start(f32[512]{0:T(512)} %get-tuple-element.26) | copy-start | bytes 6148
  996.1 33.4 %copy-start.186 = (f32[512]{0:T(512)S(1)}, f32[512]{0:T(512)}, u32[]{:S(2)}) copy-start(f32[512]{0:T(512)} %get-tuple-element.124) | copy-start | bytes 6148
  996.1 33.4 %copy-start.189 = (f32[512]{0:T(512)S(1)}, f32[512]{0:T(512)}, u32[]{:S(2)}) copy-start(f32[512]{0:T(512)} %get-tuple-element.24) | copy-start | bytes 6148
  996.1 33.4 %copy-start.172 = (f32[512]{0:T(512)S(1)}, f32[512]{0:T(512)}, u32[]{:S(2)}) copy-start(f32[512]{0:T(512)} %get-tuple-element.80) | copy-start | bytes 6148
  996.1 33.4 %copy-start.173 = (f32[512]{0:T(512)S(1)}, f32[512]{0:T(512)}, u32[]{:S(2)}) copy-start(f32[512]{0:T(512)} %get-tuple-element.97) | copy-start | bytes 6148
  996.1 317.2 %all-reduce.19.cloned.1.call-start = ((), (), s32[]{:S(2)}) async-start(), calls=%async_computation.33 | async-start | bytes 8585216 | tf_op jit(solution)/shard_map/psum | solution.py:410
  1025.7 62.6 %copy-start.181 = (f32[320]{0:T(512)S(1)}, f32[320]{0:T(512)}, u32[]{:S(2)}) copy-start(f32[320]{0:T(512)} %copy-done.180) | copy-start | bytes 3844
  1025.7 62.7 %copy-start.192 = (f32[512]{0:T(512)S(1)}, f32[512]{0:T(512)}, u32[]{:S(2)}) copy-start(f32[512]{0:T(512)} %get-tuple-element.45) | copy-start | bytes 6148
  1025.7 62.7 %copy-start.165 = (f32[320]{0:T(512)S(1)}, f32[320]{0:T(512)}, u32[]{:S(2)}) copy-start(f32[320]{0:T(512)} %copy-done.164) | copy-start | bytes 3844
  1025.7 95.0 %copy-start.147 = (f32[320]{0:T(512)S(1)}, f32[320]{0:T(512)}, u32[]{:S(2)}) copy-start(f32[320]{0:T(512)} %copy-done.146) | copy-start | bytes 3844
  1025.8 95.0 %copy-start.149 = (f32[320]{0:T(512)S(1)}, f32[320]{0:T(512)}, u32[]{:S(2)}) copy-start(f32[320]{0:T(512)} %copy-done.148) | copy-start | bytes 3844
  (176 other events, 2156.4 us)
Sparse Core Ops, SparseCore 0:
  10.3 42.4 all-gather.3
  964.4 61.2 reduce-scatter.8
  1029.8 54.6 reduce-scatter.14
  1088.3 54.6 reduce-scatter.12
  1146.4 55.1 reduce-scatter.10
  1204.1 109.1 all-reduce.18
where the time goes:
time: 1340 us; the launch traced here: 1330 us
  matrix products  329 us (25%)
  waiting for transfers between devices  289 us (22%)
  local copies, waits for them, and re-layouts  277 us (21%)
  other arithmetic  159 us (12%)
  blocking collectives  131 us (10%)
  starting transfers between devices  124 us (9%)
  between operations  19.6 us (1%)
    psum x1, waiting for transfers between devices, on_device(): lax.psum(shard_qkv.astype(jnp.bfloat16), 'seq').astype(jnp.float32)  96.3 us
    unnamed x8, waiting for transfers between devices  74.5 us
    unnamed x2, blocking collectives  66 us
    dot_general x3, matrix products, on_device(): jnp.einsum('njcd,jfd->njcf', grad_result, down_weight, preferred_element_...  63.3 us
    dot_general x3, matrix products, on_device(): jnp.einsum('njcf,njcd->jfd', active, grad_result, preferred_element_type=...  61.9 us
    reduce_scatter x1, waiting for transfers between devices, on_device(): lax.psum_scatter(total_proj.astype(jnp.bfloat16), 'dp', scatter_dimension...  57.9 us
    dot_general x3, matrix products, on_device(): jnp.einsum('njcf,jfd->njcd', active, down_weight, preferred_element_type=...  55.5 us
    unnamed x477, local copies, waits for them, and re-layouts  53 us
  transfers between devices with their start and end apart: 30, of which 12 were waited for; matrix products, arithmetic and copies ran while one was open for 37% of the time, Pallas kernels for 0%

commit v1 on v0

v1 whole, which is shorter than its diff:
```python
import functools

import jax
import jax.numpy as jnp
from jax import lax
from jax.experimental import pallas as pl
from jax.experimental.pallas import tpu as pltpu
from jax.sharding import PartitionSpec as P

HD = 64
TOP = 2
MICRO = 3
BF = jnp.bfloat16
F32 = jnp.float32
EPS = 1e-06
LANES = 128
VEC = 7
FF_BLOCK = 512
VMEM_LIMIT = 60 * 1024 * 1024


def mm(left, right):
    return jnp.dot(left, right, preferred_element_type=F32)


def mm_nt(left, right):
    return lax.dot_general(
        left, right, (((1,), (1,)), ((), ())), preferred_element_type=F32
    )


def iota(shape, dim):
    return lax.broadcasted_iota(jnp.int32, shape, dim)


def norm_parts(values):
    average = jnp.mean(values, axis=-1, keepdims=True)
    centred = values - average
    spread = jnp.mean(centred * centred, axis=-1, keepdims=True)
    scale = lax.rsqrt(spread + EPS)
    return centred * scale, scale


def norm_pull(unit, scale, gain, cotangent):
    inner = cotangent * gain
    mean_inner = jnp.mean(inner, axis=-1, keepdims=True)
    mean_unit = jnp.mean(inner * unit, axis=-1, keepdims=True)
    return scale * (inner - mean_inner - unit * mean_unit)


def misc_rows(w_ref, start):
    return jnp.transpose(w_ref[:, start : start + LANES].astype(F32))


def place_kernel(experts, room, cols_ref, rows_ref, dy_ref, send_ref, prow_ref, pcol_ref):
    tokens = cols_ref.shape[1]
    slots = experts * room
    first_row = rows_ref[0, 0:1, :]
    second_row = rows_ref[0, 1:2, :]
    hot_first = (iota((experts, tokens), 0) == first_row).astype(F32)
    hot_second = (iota((experts, tokens), 0) == second_row).astype(F32)
    earlier = (iota((tokens, tokens), 0) < iota((tokens, tokens), 1)).astype(BF)
    before = mm((hot_first + hot_second).astype(BF), earlier)
    in_first = jnp.sum(before * hot_first, axis=0, keepdims=True).astype(jnp.int32)
    in_second = jnp.sum((before + hot_first) * hot_second, axis=0, keepdims=True).astype(jnp.int32)
    place_first = first_row * room + in_first
    place_second = second_row * room + in_second
    prow_ref[0:1, :] = place_first
    prow_ref[1:2, :] = place_second
    slot_of = iota((slots, tokens), 0)
    hot = jnp.where((slot_of == place_first) | (slot_of == place_second), 1.0, 0.0).astype(BF)
    flat = dy_ref[...].reshape(tokens, dy_ref.shape[-1])
    rows = mm(hot, flat)
    for e in range(experts):
        send_ref[e] = rows[e * room : (e + 1) * room].astype(BF)
    first_col = cols_ref[0, :, 0:1]
    second_col = cols_ref[0, :, 1:2]
    hot_first = (iota((tokens, experts), 1) == first_col).astype(F32)
    hot_second = (iota((tokens, experts), 1) == second_col).astype(F32)
    later = (iota((tokens, tokens), 1) < iota((tokens, tokens), 0)).astype(BF)
    before = mm(later, (hot_first + hot_second).astype(BF))
    in_first = jnp.sum(before * hot_first, axis=1, keepdims=True).astype(jnp.int32)
    in_second = jnp.sum((before + hot_first) * hot_second, axis=1, keepdims=True).astype(jnp.int32)
    lane = iota((tokens, 8), 1)
    table = jnp.zeros((tokens, 8), jnp.int32)
    for at, col in enumerate(
        (
            first_col * room + in_first,
            second_col * room + in_second,
            first_col,
            second_col,
            in_first,
            in_second,
        )
    ):
        table = jnp.where(lane == at, col, table)
    pcol_ref[...] = table


def forward_kernel(
    cfg,
    mb,
    meta_ref,
    len_ref,
    own_ref,
    oth_ref,
    w_ref,
    prow_ref,
    send_ref,
    middle_ref,
    gate_ref,
    second_ref,
    oT_ref,
    q_ref,
    k_ref,
    v_ref,
    lse_ref,
    n1T_ref,
    att_ref,
    logs_ref,
):
    images, local_len, seq_count, width, experts, room = cfg
    full_len = local_len * seq_count
    tokens = images * local_len
    slots = experts * room
    misc_at = 4 * width
    rows = misc_rows(w_ref, misc_at)

    def vec(j):
        return rows[experts + j : experts + j + 1, :]

    here = meta_ref[1]
    lane = iota((1, LANES), 1)
    low_half = (lane < HD).astype(BF)
    high_half = (lane >= HD).astype(BF)
    for b in range(images):
        blocks = [own_ref[b]] + [oth_ref[j, b] for j in range(seq_count - 1)]
        full = jnp.concatenate(blocks, axis=0).astype(F32)
        unit, _ = norm_parts(full)
        normed = (unit * vec(0) + vec(1)).astype(BF)
        n1T_ref[:, b * full_len : (b + 1) * full_len] = jnp.transpose(normed)
        span = slice(b * local_len, (b + 1) * local_len)
        wide = slice(b * full_len, (b + 1) * full_len)
        queries = (mm(normed[:local_len], w_ref[:, :width]) + vec(2)).astype(BF)
        q_ref[span, :] = queries * jnp.asarray(HD**-0.5, BF)
        k_ref[wide, :] = mm(normed, w_ref[:, width : 2 * width]).astype(BF)
        v_ref[wide, :] = (mm(normed, w_ref[:, 2 * width : 3 * width]) + vec(3)).astype(BF)
        kpos = iota((1, full_len), 1)
        shift = jnp.zeros((1, full_len), jnp.int32)
        for j in range(seq_count):
            origin = lax.rem(here + j, seq_count) * local_len - j * local_len
            shift = jnp.where(kpos >= j * local_len, origin, shift)
        valid = (kpos + shift) < len_ref[mb * images + b]
        logs_ref[...] = jnp.zeros_like(logs_ref)

        def heads(blk, carry):
            at = pl.ds(pl.multiple_of(blk * LANES, LANES), LANES)
            q_blk = q_ref[span, at]
            k_blk = k_ref[wide, at]
            v_blk = v_ref[wide, at]
            outs = []
            for side, keep in enumerate((low_half, high_half)):
                scores = mm_nt(q_blk * keep, k_blk)
                scores = jnp.where(valid, scores, -1e30)
                highest = jnp.max(scores, axis=1, keepdims=True)
                powers = jnp.exp(scores - highest)
                total = jnp.sum(powers, axis=1, keepdims=True)
                probs = (powers * (1.0 / total)).astype(BF)
                outs.append(mm(probs, v_blk))
                logs_ref[...] = jnp.where(
                    lane == 2 * blk + side, highest + jnp.log(total), logs_ref[...]
                )
            att_ref[span, at] = jnp.where(lane < HD, outs[0], outs[1]).astype(BF)
            return carry

        lax.fori_loop(0, width // LANES, heads, 0)
        lse_ref[b * 8 : b * 8 + 8, :] = jnp.transpose(logs_ref[...])[0:8, :]
    attended = att_ref[...]
    oT_ref[...] = jnp.transpose(attended)
    branch = mm(attended, w_ref[:, 3 * width : 4 * width]) + vec(4)
    middle = own_ref[...].reshape(tokens, width).astype(F32) + branch
    middle_ref[...] = middle
    unit, _ = norm_parts(middle)
    second = (unit * vec(5) + vec(6)).astype(BF)
    second_ref[...] = second
    gate_ref[...] = gates(mm(second, w_ref[:, misc_at : misc_at + LANES]), experts)
    slot_of = iota((slots, tokens), 0)
    hot = jnp.where(
        (slot_of == prow_ref[0:1, :]) | (slot_of == prow_ref[1:2, :]), 1.0, 0.0
    ).astype(BF)
    sent = mm(hot, second)
    for e in range(experts):
        send_ref[e] = sent[e * room : (e + 1) * room].astype(BF)


def gates(logits, experts):
    real = iota((1, LANES), 1) < experts
    logits = jnp.where(real, logits, -1e30)
    powers = jnp.where(real, jnp.exp(logits - jnp.max(logits, axis=1, keepdims=True)), 0.0)
    return powers / jnp.sum(powers, axis=1, keepdims=True)


def expert_kernel(cfg, first, *refs):
    groups, room, capacity, width = cfg
    meta_ref, buf_ref, dyb_ref, wm_ref, up_ref, ub_ref, down_ref, db_ref = refs[:8]
    refs = refs[8:]
    if not first:
        gup_in, gdn_in, gb_in, gdb_in = refs[:4]
        refs = refs[4:]
    (
        r_ref,
        dbuf_ref,
        gup_ref,
        gdn_ref,
        gb_ref,
        gdb_ref,
        flat_s,
        flatT_s,
        dr_s,
        drT_s,
        racc_s,
        dacc_s,
    ) = refs
    slots = groups * room
    step = pl.program_id(0)
    experts = groups

    @pl.when(step == 0)
    def _():
        flat = buf_ref[...].astype(F32).reshape(slots, width).astype(BF)
        flat_s[...] = flat
        flatT_s[...] = jnp.transpose(flat)
        gate = gates(mm(flat, wm_ref[...]), experts)
        mine = iota((1, LANES), 1) == meta_ref[0]
        mine_gate = jnp.sum(jnp.where(mine, gate, 0.0), axis=1, keepdims=True)
        dr = (dyb_ref[...].astype(F32).reshape(slots, width) * mine_gate).astype(BF)
        dr_s[...] = dr
        drT_s[...] = jnp.transpose(dr)
        shift_sum = jnp.sum(dr.astype(F32), axis=0, keepdims=True)
        gdb_ref[...] = shift_sum if first else gdb_in[...] + shift_sum
        racc_s[...] = jnp.zeros_like(racc_s)
        dacc_s[...] = jnp.zeros_like(dacc_s)

    flat = flat_s[...]
    dr = dr_s[...]
    hidden = mm(flat, up_ref[0]) + ub_ref[...].astype(F32)
    half_erf = 0.5 * lax.erf(hidden * (0.5**0.5)) + 0.5
    active = (hidden * half_erf).astype(BF)
    slope = half_erf + hidden * (jnp.exp(-0.5 * hidden * hidden) * 0.3989422804014327)
    racc_s[...] += mm(active, down_ref[0])
    grad_pre = mm_nt(dr, down_ref[0]) * slope
    low_pre = grad_pre.astype(BF)
    dacc_s[...] += mm_nt(low_pre, up_ref[0])
    gup = mm(flatT_s[...], low_pre)
    gdn = mm(drT_s[...], active)
    gbias = jnp.sum(low_pre.astype(F32), axis=0, keepdims=True)
    if first:
        gup_ref[...] = gup
        gdn_ref[...] = gdn
        gb_ref[...] = gbias
    else:
        gup_ref[...] = gup_in[...] + gup
        gdn_ref[...] = gdn_in[...] + gdn
        gb_ref[...] = gb_in[...] + gbias

    @pl.when(step == pl.num_programs(0) - 1)
    def _():
        result = (racc_s[...] + db_ref[...].astype(F32)).astype(BF)
        for e in range(groups):
            r_ref[e] = result[e * room : (e + 1) * room]
        dy = dyb_ref[...].astype(F32).reshape(slots, width)
        dgate = jnp.sum(dy * result.astype(F32), axis=1, keepdims=True).reshape(groups, room, 1)
        spread = jnp.where(
            iota((groups, room, LANES), 2) == iota((groups, room, LANES), 1), dgate, 0.0
        )
        as_row = jnp.sum(spread, axis=1, keepdims=True)
        high = as_row.astype(BF).astype(F32)
        tail = jnp.zeros((groups, 1, width - 2 * LANES), F32)
        as_row = jnp.concatenate([high, as_row - high, tail], axis=2)
        back = dacc_s[...].reshape(groups, room, width)
        back = jnp.where(iota((groups, room, 1), 1) == capacity, as_row, back).astype(BF)
        for e in range(groups):
            dbuf_ref[e] = back[e]


def backward_kernel(cfg, mb, first, *refs):
    images, local_len, seq_count, width, experts, room, capacity = cfg
    (
        meta_ref,
        len_ref,
        dback_ref,
        pcol_ref,
        gate_ref,
        middle_ref,
        second_ref,
        dy_ref,
        oT_ref,
        w_ref,
        q_ref,
        k_ref,
        v_ref,
        lse_ref,
        n1T_ref,
    ) = refs[:15]
    refs = refs[15:]
    if not first:
        g_in, mrow_in = refs[:2]
        refs = refs[2:]
    down_own, down_oth, dm_ref, g_ref, mrow_ref, do_s, dqT_s, dkv_s = refs
    full_len = local_len * seq_count
    tokens = images * local_len
    slots = experts * room
    misc_at = 4 * width
    rows = misc_rows(w_ref, misc_at)
    here = meta_ref[1]

    def vec(j):
        return rows[experts + j : experts + j + 1, :]

    dback = dback_ref[...].astype(F32)
    back_rows = dback.reshape(slots, width).astype(BF)
    slot_of = iota((tokens, slots), 1)
    hot = jnp.where(
        (slot_of == pcol_ref[:, 0:1]) | (slot_of == pcol_ref[:, 1:2]), 1.0, 0.0
    ).astype(BF)
    from_experts = mm(hot, back_rows)
    spare = jnp.where(iota((experts, room, 1), 1) == capacity, dback[:, :, : 2 * LANES], 0.0)
    spare = jnp.sum(spare, axis=1)
    spare = jnp.concatenate(
        [spare, jnp.zeros((LANES - experts, 2 * LANES), F32)], axis=0
    ).astype(BF)
    lane = iota((tokens, LANES), 1)
    pulled = jnp.zeros((tokens, LANES), F32)
    for k in range(TOP):
        within = jnp.where(lane == pcol_ref[:, 4 + k : 5 + k], 1.0, 0.0).astype(BF)
        found = mm_nt(jnp.concatenate([within, within], axis=1), spare)
        pulled = pulled + jnp.where(lane == pcol_ref[:, 2 + k : 3 + k], found, 0.0)
    gate = gate_ref[...]
    dlogit = gate * (pulled - jnp.sum(gate * pulled, axis=1, keepdims=True))
    dlogit_low = dlogit.astype(BF)
    mrow_ref[...] = mm(jnp.transpose(dlogit_low.astype(F32)).astype(BF), second_ref[...])
    dn2 = from_experts + mm_nt(dlogit_low, w_ref[:, misc_at : misc_at + LANES])
    unit, scale = norm_parts(middle_ref[...])
    dy = dy_ref[...].reshape(tokens, width).astype(F32)
    dm = dy + norm_pull(unit, scale, vec(5), dn2)
    dm_ref[...] = dm
    da = dm.astype(BF)
    gproj = mm(oT_ref[...], da)
    proj = slice(3 * width, 4 * width)
    if first:
        g_ref[:, proj] = gproj
    else:
        g_ref[:, proj] = g_in[:, proj] + gproj
    do_s[...] = mm_nt(da, w_ref[:, proj]).astype(BF)
    half_lane = iota((1, LANES), 1)
    low_half = (half_lane < HD).astype(BF)
    high_half = (half_lane >= HD).astype(BF)
    gqkv = [None, None]
    bias_q = jnp.zeros((1, width), F32)
    bias_v = jnp.zeros((1, width), F32)
    for b in range(images):
        span = slice(b * local_len, (b + 1) * local_len)
        wide = slice(b * full_len, (b + 1) * full_len)
        kpos = iota((full_len, 1), 0)
        shift = jnp.zeros((full_len, 1), jnp.int32)
        for j in range(seq_count):
            origin = lax.rem(here + j, seq_count) * local_len - j * local_len
            shift = jnp.where(kpos >= j * local_len, origin, shift)
        valid = (kpos + shift) < len_ref[mb * images + b]

        def heads(blk, carry):
            at = pl.ds(pl.multiple_of(blk * LANES, LANES), LANES)
            q_blk = q_ref[span, at]
            k_blk = k_ref[wide, at]
            v_blk = v_ref[wide, at]
            do_blk = do_s[span, at]
            kT_blk = jnp.transpose(k_blk)
            dvs = []
            dks = []
            dqs = []
            for side, keep in enumerate((low_half, high_half)):
                scores = mm_nt(k_blk, q_blk * keep)
                logs = lse_ref[pl.ds(b * 8 + 2 * blk + side, 1), :]
                probs = jnp.where(valid, jnp.exp(scores - logs), 0.0)
                dprobs = mm_nt(v_blk, do_blk * keep)
                inner = jnp.sum(probs * dprobs, axis=0, keepdims=True)
                dscores = (probs * (dprobs - inner)).astype(BF)
                dvs.append(mm(probs.astype(BF), do_blk))
                dks.append(mm(dscores, q_blk))
                dqs.append(mm(kT_blk[side * HD : (side + 1) * HD], dscores))
            dqT_s[pl.ds(pl.multiple_of(blk * LANES, LANES), HD), :] = dqs[0]
            dqT_s[pl.ds(pl.multiple_of(blk * LANES + HD, HD), HD), :] = dqs[1]
            left = half_lane < HD
            dkv_s[:, at] = jnp.where(left, dks[0], dks[1]).astype(BF)
            vat = pl.ds(pl.multiple_of(width + blk * LANES, LANES), LANES)
            dkv_s[:, vat] = jnp.where(left, dvs[0], dvs[1]).astype(BF)
            return carry

        lax.fori_loop(0, width // LANES, heads, 0)
        dq = (jnp.transpose(dqT_s[...]) * HD**-0.5).astype(BF)
        dkv = dkv_s[...]
        part_q = mm(n1T_ref[:, b * full_len : b * full_len + local_len], dq)
        part_kv = mm(n1T_ref[:, wide], dkv)
        gqkv[0] = part_q if b == 0 else gqkv[0] + part_q
        gqkv[1] = part_kv if b == 0 else gqkv[1] + part_kv
        bias_q = bias_q + jnp.sum(dq.astype(F32), axis=0, keepdims=True)
        bias_v = bias_v + jnp.sum(dkv[:, width:].astype(F32), axis=0, keepdims=True)
        down = mm_nt(dkv, w_ref[:, width : 3 * width])
        down_own[span, :] = mm_nt(dq, w_ref[:, :width])
        down_own[span, :] += down[:local_len]
        for j in range(seq_count - 1):
            down_oth[j, span, :] = down[(j + 1) * local_len : (j + 2) * local_len].astype(BF)
    if first:
        g_ref[:, :width] = gqkv[0]
        g_ref[:, width : 3 * width] = gqkv[1]
    else:
        g_ref[:, :width] = g_in[:, :width] + gqkv[0]
        g_ref[:, width : 3 * width] = g_in[:, width : 3 * width] + gqkv[1]
    row = iota((LANES, 1), 0)
    mrow = jnp.where(row < experts, mrow_ref[...], 0.0)
    sums = (
        bias_q,
        bias_v,
        jnp.sum(da.astype(F32), axis=0, keepdims=True),
        jnp.sum(dn2 * unit, axis=0, keepdims=True),
        jnp.sum(dn2, axis=0, keepdims=True),
    )
    for j, value in enumerate(sums):
        mrow = jnp.where(row == experts + 2 + j, value, mrow)
    mrow_ref[...] = mrow if first else mrow_in[...] + mrow


def input_kernel(cfg, own_ref, got_ref, x_ref, dm_ref, wm_ref, mrow_in, out_ref, mrow_ref):
    images, local_len, seq_count, width, experts = cfg
    tokens = images * local_len
    rows = jnp.transpose(wm_ref[...].astype(F32))
    dn1 = own_ref[...]
    for j in range(seq_count - 1):
        dn1 = dn1 + got_ref[j].astype(F32)
    unit, scale = norm_parts(x_ref[...].reshape(tokens, width).astype(F32))
    grad = dm_ref[...] + norm_pull(unit, scale, rows[experts : experts + 1, :], dn1)
    out_ref[...] = grad.astype(BF).reshape(images, local_len, width)
    row = iota((LANES, 1), 0)
    mrow = jnp.where(row == experts, jnp.sum(dn1 * unit, axis=0, keepdims=True), 0.0)
    mrow = jnp.where(row == experts + 1, jnp.sum(dn1, axis=0, keepdims=True), mrow)
    mrow_ref[...] = mrow_in[...] + mrow


def mix_kernel(cfg, back_ref, pcol_ref, gate_ref, middle_ref, out_ref):
    images, local_len, width, experts, room = cfg
    tokens = images * local_len
    slots = experts * room
    back = back_ref[...].astype(F32).reshape(slots, width).astype(BF)
    slot_of = iota((tokens, slots), 1)
    lane = iota((tokens, LANES), 1)
    gate = gate_ref[...]
    total = middle_ref[...]
    for k in range(TOP):
        hot = jnp.where(slot_of == pcol_ref[:, k : k + 1], 1.0, 0.0).astype(BF)
        chosen = jnp.where(lane == pcol_ref[:, 2 + k : 3 + k], gate, 0.0)
        total = total + jnp.sum(chosen, axis=1, keepdims=True) * mm(hot, back)
    out_ref[...] = total.astype(BF).reshape(images, local_len, width)


def sum_kernel(gup_ref, gdn_ref, got_up, got_dn, up_ref, dn_ref):
    up_ref[0] = gup_ref[...] + got_up[...].astype(F32)
    dn_ref[0] = jnp.transpose(gdn_ref[...] + got_dn[...].astype(F32))


def whole_spec():
    return pl.BlockSpec(memory_space=pltpu.VMEM)


def smem_spec():
    return pl.BlockSpec(memory_space=pltpu.SMEM)


def params():
    return pltpu.CompilerParams(vmem_limit_bytes=VMEM_LIMIT)


def struct(shape, kind):
    return jax.ShapeDtypeStruct(shape, kind)


def on_device(
    images,
    cotangent,
    lengths,
    routes,
    attn_norm_gain,
    attn_norm_bias,
    qkv_weight,
    query_value_bias,
    proj_weight,
    proj_bias,
    moe_norm_gain,
    moe_norm_bias,
    router_weight,
    up_weight,
    up_bias,
    down_weight,
    down_bias,
):
    seq_count = lax.axis_size("seq")
    dp_count = lax.axis_size("dp")
    count = images.shape[0] // MICRO
    local_len = images.shape[1]
    width = images.shape[2]
    tokens = count * local_len
    full_len = local_len * seq_count
    experts = router_weight.shape[1]
    hidden = up_weight.shape[2]
    capacity = (5 * tokens * TOP + 4 * experts - 1) // (4 * experts)
    room = (capacity + 1 + 7) // 8 * 8
    slots = experts * room
    assert up_weight.shape[0] == 1 and experts == dp_count
    assert experts + VEC <= LANES and capacity <= LANES
    meta = jnp.stack([lax.axis_index("dp"), lax.axis_index("seq")]).astype(jnp.int32)

    shard = router_weight.shape[0]
    pieces = [
        qkv_weight,
        proj_weight,
        router_weight,
        attn_norm_gain[:, None],
        attn_norm_bias[:, None],
        query_value_bias[0][:, None],
        query_value_bias[1][:, None],
        proj_bias[:, None],
        moe_norm_gain[:, None],
        moe_norm_bias[:, None],
        jnp.zeros((shard, LANES - experts - VEC), BF),
    ]
    packed = lax.all_gather(jnp.concatenate(pieces, axis=1), "dp", axis=0, tiled=True)
    packed_width = 4 * width + LANES

    others = jnp.stack(
        [
            lax.ppermute(
                images, "seq", [((i + j) % seq_count, i) for i in range(seq_count)]
            )
            for j in range(1, seq_count)
        ]
    )
    cols = routes.reshape(MICRO, tokens, TOP)
    rows = jnp.swapaxes(cols, 1, 2)

    def exchange(array):
        return lax.all_to_all(array, "dp", split_axis=0, concat_axis=0, tiled=True)

    def token_spec(mb):
        return pl.BlockSpec((count, local_len, width), lambda i: (mb, 0, 0))

    def full(shape):
        return pl.BlockSpec(shape, lambda i: (0,) * len(shape))

    misc_spec = pl.BlockSpec((width, LANES), lambda i: (0, 4 * width // LANES))
    moved = struct((experts, room, width), BF)

    def place(mb):
        return pl.pallas_call(
            functools.partial(place_kernel, experts, room),
            grid=(1,),
            in_specs=[
                pl.BlockSpec((1, tokens, TOP), lambda i: (mb, 0, 0)),
                pl.BlockSpec((1, TOP, tokens), lambda i: (mb, 0, 0)),
                token_spec(mb),
            ],
            out_specs=[
                full((experts, room, width)),
                full((TOP, tokens)),
                full((tokens, 8)),
            ],
            out_shape=[
                moved,
                struct((TOP, tokens), jnp.int32),
                struct((tokens, 8), jnp.int32),
            ],
            compiler_params=params(),
            name="place",
        )(cols, rows, cotangent)

    def forward(mb, prow):
        cfg = (count, local_len, seq_count, width, experts, room)
        outs = [
            ((experts, room, width), BF),
            ((tokens, width), F32),
            ((tokens, LANES), F32),
            ((tokens, width), BF),
            ((width, tokens), BF),
            ((tokens, width), BF),
            ((count * full_len, width), BF),
            ((count * full_len, width), BF),
            ((count * 8, local_len), F32),
            ((width, count * full_len), BF),
        ]
        return pl.pallas_call(
            functools.partial(forward_kernel, cfg, mb),
            grid=(1,),
            in_specs=[
                smem_spec(),
                smem_spec(),
                token_spec(mb),
                pl.BlockSpec((seq_count - 1, count, local_len, width), lambda i: (0, mb, 0, 0)),
                full((width, packed_width)),
                full((TOP, tokens)),
            ],
            out_specs=[full(s) for s, _ in outs],
            out_shape=[struct(s, k) for s, k in outs],
            scratch_shapes=[
                pltpu.VMEM((tokens, width), BF),
                pltpu.VMEM((local_len, LANES), F32),
            ],
            compiler_params=params(),
            name="forward",
        )(meta, lengths, images, others, packed, prow)

    def expert(buf, dyb, totals):
        first = totals is None
        cfg = (experts, room, capacity, width)
        wide = lambda: pl.BlockSpec((width, FF_BLOCK), lambda i: (0, i))
        thin = lambda: pl.BlockSpec((1, FF_BLOCK), lambda i: (0, i))
        in_specs = [
            smem_spec(),
            full((experts, room, width)),
            full((experts, room, width)),
            misc_spec,
            pl.BlockSpec((1, width, FF_BLOCK), lambda i: (0, 0, i)),
            thin(),
            pl.BlockSpec((1, FF_BLOCK, width), lambda i: (0, i, 0)),
            full((1, width)),
        ]
        total_specs = [wide(), wide(), thin(), full((1, width))]
        args = [meta, buf, dyb, packed, up_weight, up_bias, down_weight, down_bias]
        aliases = {}
        if not first:
            aliases = {len(args) + j: 2 + j for j in range(4)}
            in_specs += total_specs
            args += list(totals)
        outs = pl.pallas_call(
            functools.partial(expert_kernel, cfg, first),
            grid=(hidden // FF_BLOCK,),
            in_specs=in_specs,
            out_specs=[full((experts, room, width))] * 2 + total_specs,
            out_shape=[
                moved,
                moved,
                struct((width, hidden), F32),
                struct((width, hidden), F32),
                struct((1, hidden), F32),
                struct((1, width), F32),
            ],
            scratch_shapes=[
                pltpu.VMEM((slots, width), BF),
                pltpu.VMEM((width, slots), BF),
                pltpu.VMEM((slots, width), BF),
                pltpu.VMEM((width, slots), BF),
                pltpu.VMEM((slots, width), F32),
                pltpu.VMEM((slots, width), F32),
            ],
            input_output_aliases=aliases,
            compiler_params=params(),
            name="expert",
        )(*args)
        return outs[0], outs[1], tuple(outs[2:])

    def backward(mb, dback, pcol, saved, totals):
        first = totals is None
        cfg = (count, local_len, seq_count, width, experts, room, capacity)
        middle, gate, second, oT, q, k, v, lse, n1T = saved
        args = [
            meta,
            lengths,
            dback,
            pcol,
            gate,
            middle,
            second,
            cotangent,
            oT,
            packed,
            q,
            k,
            v,
            lse,
            n1T,
        ]
        in_specs = [smem_spec(), smem_spec()]
        in_specs += [token_spec(mb) if a is cotangent else full(a.shape) for a in args[2:]]
        aliases = {}
        if not first:
            aliases = {len(args) + j: 3 + j for j in range(2)}
            in_specs += [full(a.shape) for a in totals]
            args += list(totals)
        outs = [
            ((tokens, width), F32),
            ((seq_count - 1, tokens, width), BF),
            ((tokens, width), F32),
            ((width, 4 * width), F32),
            ((LANES, width), F32),
        ]
        return pl.pallas_call(
            functools.partial(backward_kernel, cfg, mb, first),
            grid=(1,),
            in_specs=in_specs,
            out_specs=[full(s) for s, _ in outs],
            out_shape=[struct(s, t) for s, t in outs],
            scratch_shapes=[
                pltpu.VMEM((tokens, width), BF),
                pltpu.VMEM((width, local_len), F32),
                pltpu.VMEM((full_len, 2 * width), BF),
            ],
            input_output_aliases=aliases,
            compiler_params=params(),
            name="backward",
        )(*args)

    def finish(mb, own, got, dm, mrow):
        cfg = (count, local_len, seq_count, width, experts)
        return pl.pallas_call(
            functools.partial(input_kernel, cfg),
            grid=(1,),
            in_specs=[
                full((tokens, width)),
                full((seq_count - 1, tokens, width)),
                token_spec(mb),
                full((tokens, width)),
                misc_spec,
                full((LANES, width)),
            ],
            out_specs=[full((count, local_len, width)), full((LANES, width))],
            out_shape=[struct((count, local_len, width), BF), struct((LANES, width), F32)],
            compiler_params=params(),
            name="finish",
        )(own, got, images, dm, packed, mrow)

    def mix(back, pcol, gate, middle):
        cfg = (count, local_len, width, experts, room)
        args = (back, pcol, gate, middle)
        return pl.pallas_call(
            functools.partial(mix_kernel, cfg),
            grid=(1,),
            in_specs=[full(a.shape) for a in args],
            out_specs=full((count, local_len, width)),
            out_shape=struct((count, local_len, width), BF),
            compiler_params=params(),
            name="mix",
        )(*args)

    placed = [place(mb) for mb in range(MICRO)]
    dyb = [exchange(p[0]) for p in placed]
    saved = []
    bufs = []
    for mb in range(MICRO):
        outs = forward(mb, placed[mb][1])
        bufs.append(exchange(outs[0]))
        saved.append(outs[1:])
    totals = None
    results = []
    dbacks = []
    for mb in range(MICRO):
        result, dback, totals = expert(bufs[mb], dyb[mb], totals)
        results.append(result)
        dbacks.append(exchange(dback))
    dense = None
    mrows = []
    grads = []
    for mb in range(MICRO):
        own, oth, dm, *dense = backward(mb, dbacks[mb], placed[mb][2], saved[mb], dense)
        got = jnp.stack(
            [
                lax.ppermute(
                    oth[j - 1], "seq", [(i, (i + j) % seq_count) for i in range(seq_count)]
                )
                for j in range(1, seq_count)
            ]
        )
        grad, dense[1] = finish(mb, own, got, dm, dense[1])
        grads.append(grad)
    out_blocks = []
    for mb in range(MICRO):
        back = exchange(results[mb])
        out_blocks.append(mix(back, placed[mb][2], saved[mb][1], saved[mb][0]))

    gup, gdn, gbias, gdbias = totals
    swap = [(i, (i + 1) % seq_count) for i in range(seq_count)]

    def seq_sum(value):
        if seq_count == 2:
            return value + lax.ppermute(value.astype(BF), "seq", swap).astype(F32)
        return lax.psum(value.astype(BF), "seq").astype(F32)

    if seq_count == 2:
        got_up = lax.ppermute(gup.astype(BF), "seq", swap)
        got_dn = lax.ppermute(gdn.astype(BF), "seq", swap)
        wide = lambda: pl.BlockSpec((width, FF_BLOCK), lambda i: (0, i))
        final_up, final_down = pl.pallas_call(
            sum_kernel,
            grid=(hidden // FF_BLOCK,),
            in_specs=[wide(), wide(), wide(), wide()],
            out_specs=[
                pl.BlockSpec((1, width, FF_BLOCK), lambda i: (0, 0, i)),
                pl.BlockSpec((1, FF_BLOCK, width), lambda i: (0, i, 0)),
            ],
            out_shape=[struct((1, width, hidden), F32), struct((1, hidden, width), F32)],
            compiler_params=params(),
            name="sum_experts",
        )(gup, gdn, got_up, got_dn)
    else:
        final_up = seq_sum(gup)[None]
        final_down = jnp.swapaxes(seq_sum(gdn), 0, 1)[None]
    biases = seq_sum(jnp.concatenate([gbias, gdbias], axis=1))
    final_up_shift = biases[:, :hidden]
    final_down_shift = biases[:, hidden:]

    grand = jnp.concatenate([dense[0], jnp.transpose(dense[1])], axis=1).astype(BF)
    shards = lax.psum_scatter(grand, "dp", scatter_dimension=0, tiled=True)
    shards = seq_sum(shards.astype(F32))
    misc = 4 * width + experts
    return (
        jnp.concatenate(out_blocks, axis=0),
        jnp.concatenate(grads, axis=0),
        shards[:, misc],
        shards[:, misc + 1],
        shards[:, : 3 * width],
        jnp.stack([shards[:, misc + 2], shards[:, misc + 3]]),
        shards[:, 3 * width : 4 * width],
        shards[:, misc + 4],
        shards[:, misc + 5],
        shards[:, misc + 6],
        shards[:, 4 * width : misc],
        final_up,
        final_up_shift,
        final_down,
        final_down_shift,
    )


def solution(mesh):
    return jax.shard_map(
        on_device,
        mesh=mesh,
        in_specs=(
            P("dp", "seq", None),
            P("dp", "seq", None),
            P("dp"),
            P("dp", None, "seq", None, None),
            P("dp"),
            P("dp"),
            P("dp", None),
            P(None, "dp"),
            P("dp", None),
            P("dp"),
            P("dp"),
            P("dp"),
            P("dp", None),
            P("dp", None, None),
            P("dp", None),
            P("dp", None, None),
            P("dp", None),
        ),
        out_specs=(
            P("dp", "seq", None),
            P("dp", "seq", None),
            P("dp"),
            P("dp"),
            P("dp", None),
            P(None, "dp"),
            P("dp", None),
            P("dp"),
            P("dp"),
            P("dp"),
            P("dp", None),
            P("dp", None, None),
            P("dp", None),
            P("dp", None, None),
            P("dp", None),
        ),
        check_vma=False,
    )
```

time: 1340 us -> 531 us (0.40)
  matrix products: 329 us -> 0 us
  local copies, waits for them, and re-layouts: 277 us -> 18.7 us
  Pallas kernels: 0 us -> 177 us
  other arithmetic: 159 us -> 13.7 us
  blocking collectives: 131 us -> 28.6 us
  waiting for transfers between devices: 289 us -> 188 us
  starting transfers between devices: 124 us -> 81.1 us
    dot_general x63 -> x0, matrix products: 329 us -> none  [the longest x3 63.3 us: on_device(): jnp.einsum('njcd,jfd->njcf', grad_result, down_weight, preferred_element_...]
    pallas_call x0 -> x19, Pallas kernels: none -> 177 us  [the longest x3 58.4 us: expert(): pl.pallas_call(functools.partial(expert_kernel, cfg, first), grid=(hidden...]
    ppermute x0 -> x8, waiting for transfers between devices: none -> 115 us  [the longest x2 71.2 us: seq_sum(): return value + lax.ppermute(value.astype(BF), 'seq', swap).astype(F32)]
    psum x1 -> x0, waiting for transfers between devices: 96.3 us -> none  [on_device(): lax.psum(shard_qkv.astype(jnp.bfloat16), 'seq').astype(jnp.float32)]
    reduce_scatter x2 -> x1, waiting for transfers between devices: 78.8 us -> 0.01 us  [on_device(): shards = lax.psum_scatter(grand, 'dp', scatter_dimension=0, tiled=True)]
    unnamed x8 -> x2, waiting for transfers between devices: 74.5 us -> 0.03 us
    unnamed x2 -> x0, blocking collectives: 66 us -> none
    all_gather x3 -> x0, blocking collectives: 55.7 us -> none  [the longest x1 19.4 us: fetch(): lax.all_gather(router_weight, 'dp', axis=0, tiled=True)]
  transfers between devices with their start and end apart: 30 -> 21, of which waited for: 12 -> 13; matrix products, arithmetic and copies ran while one was open for 37% -> 4% of each run, Pallas kernels for 0% -> 33%
where the time goes in v1:
time: 531 us; the launch traced here: 521 us
  waiting for transfers between devices  188 us (35%)
  Pallas kernels  177 us (33%)
  starting transfers between devices  81.1 us (15%)
  blocking collectives  28.6 us (5%)
  local copies, waits for them, and re-layouts  18.7 us (4%)
  between operations  14.7 us (3%)
  other arithmetic  13.7 us (3%)
    all_to_all x11, waiting for transfers between devices, exchange(): return lax.all_to_all(array, 'dp', split_axis=0, concat_axis=0, tiled=True)  73 us
    ppermute x2, waiting for transfers between devices, seq_sum(): return value + lax.ppermute(value.astype(BF), 'seq', swap).astype(F32)  71.2 us
    all_to_all x11, starting transfers between devices, exchange(): return lax.all_to_all(array, 'dp', split_axis=0, concat_axis=0, tiled=True)  69.7 us
    pallas_call x3, Pallas kernels, expert(): pl.pallas_call(functools.partial(expert_kernel, cfg, first), grid=(hidden...  58.4 us
    pallas_call x3, Pallas kernels, backward(): pl.pallas_call(functools.partial(backward_kernel, cfg, mb, first), grid=(...  50.3 us
    pallas_call x3, Pallas kernels, forward(): pl.pallas_call(functools.partial(forward_kernel, cfg, mb), grid=(1,), in_...  33.1 us
    all_to_all x1, blocking collectives, exchange(): return lax.all_to_all(array, 'dp', split_axis=0, concat_axis=0, tiled=True)  28.6 us
    ppermute x1, waiting for transfers between devices, on_device(): lax.ppermute(images, 'seq', [((i + j) % seq_count, i) for i in range(seq_...  21.9 us
  transfers between devices with their start and end apart: 21, of which 13 were waited for; matrix products, arithmetic and copies ran while one was open for 4% of the time, Pallas kernels for 33%

profile of v1, /device:TPU:0, one launch (start us, length us, event | category | flops | bytes accessed | tf_op | source)
XLA Modules:
  0.0 521.4 jit_solution(9362318435879142408)
XLA Ops:
  7.2 1.7 copy.65.cols_ref
  8.9 2.9 place.5
  11.8 7.5 %all-to-all-start.7 = ((bf16[16,56,512]{2,1,0:T(8,128)(2,1)}), bf16[16,56,512]{2,1,0:T(8,128)(2,1)S(1)}, u32[]{:S(2)}, u32[]{:S(2)}) async-start(bf16[16,56,512]{2,1,0:T(8,128)(2,1)} %get-tuple-element.115), calls=%async_computation.7 | async-start | bytes 1835008 | tf_op jit(solution)/shard_map/all_to_all | solution.py:550
  24.8 1.6 concatenate.24
  26.5 2.9 place.4
  29.4 10.8 %all-to-all-done.7.refs_2_ = bf16[16,56,512]{2,1,0:T(8,128)(2,1)S(1)} async-done(((bf16[16,56,512]{2,1,0:T(8,128)(2,1)}), bf16[16,56,512]{2,1,0:T(8,128)(2,1)S(1)}, u32[]{:S(2)}, u32[]{:S(2)}) %all-to-all-start.7) | async-done | bytes 917536 | tf_op jit(solution)/shard_map/all_to_all | solution.py:550
  40.2 9.2 %all-to-all-start.4 = ((bf16[16,56,512]{2,1,0:T(8,128)(2,1)}), bf16[16,56,512]{2,1,0:T(8,128)(2,1)S(1)}, u32[]{:S(2)}, u32[]{:S(2)}) async-start(bf16[16,56,512]{2,1,0:T(8,128)(2,1)} %get-tuple-element.104), calls=%async_computation.4 | async-start | bytes 1835008 | tf_op jit(solution)/shard_map/all_to_all | solution.py:550
  49.3 2.9 place.3
  52.2 26.8 %all-to-all-done.4.refs_2_ = bf16[16,56,512]{2,1,0:T(8,128)(2,1)S(1)} async-done(((bf16[16,56,512]{2,1,0:T(8,128)(2,1)}), bf16[16,56,512]{2,1,0:T(8,128)(2,1)S(1)}, u32[]{:S(2)}, u32[]{:S(2)}) %all-to-all-start.4) | async-done | bytes 917536 | tf_op jit(solution)/shard_map/all_to_all | solution.py:550
  79.0 0.9 copy-done.7
  80.0 6.1 %all-to-all-start.1 = ((bf16[16,56,512]{2,1,0:T(8,128)(2,1)}), bf16[16,56,512]{2,1,0:T(8,128)(2,1)}, u32[]{:S(2)}, u32[]{:S(2)}) async-start(bf16[16,56,512]{2,1,0:T(8,128)(2,1)} %get-tuple-element.97), calls=%async_computation.1 | async-start | bytes 1835008 | tf_op jit(solution)/shard_map/all_to_all | solution.py:550
  86.1 1.6 collective-permute-start
  88.2 21.9 %collective-permute-done = bf16[3,320,512]{2,1,0:T(8,128)(2,1)S(1)} collective-permute-done((bf16[3,320,512]{2,1,0:T(8,128)(2,1)S(1)}, bf16[3,320,512]{2,1,0:T(8,128)(2,1)S(1)}, u32[]{:S(2)}, u32[]{:S(2)}) %collective-permute-start) | collective-permute-done | bytes 983072 | tf_op jit(solution)/shard_map/ppermute | solution.py:540
  110.2 0.9 copy-done.2
  111.1 11.0 %forward.3 = (bf16[16,56,512]{2,1,0:T(8,128)(2,1)}, f32[320,512]{1,0:T(8,128)}, f32[320,128]{1,0:T(8,128)}, bf16[320,512]{1,0:T(8,128)(2,1)}, bf16[512,320]{1,0:...) custom-call(s32[2]{0:T(128)} %pad_add_fusion.meta_ref.refs_0_, ...), custom_call_target="tpu_custom_call" | custom-call | tf_op jit(solution)/shard_map/forward/pallas_call | solution.py:598
  122.2 5.7 %all-to-all-start = ((bf16[16,56,512]{2,1,0:T(8,128)(2,1)}), bf16[16,56,512]{2,1,0:T(8,128)(2,1)S(1)}, u32[]{:S(2)}, u32[]{:S(2)}) async-start(bf16[16,56,512]{2,1,0:T(8,128)(2,1)} %get-tuple-element.96), calls=%async_computation | async-start | bytes 1835008 | tf_op jit(solution)/shard_map/all_to_all | solution.py:550
  127.9 11.0 %forward.4 = (bf16[16,56,512]{2,1,0:T(8,128)(2,1)}, f32[320,512]{1,0:T(8,128)}, f32[320,128]{1,0:T(8,128)}, bf16[320,512]{1,0:T(8,128)(2,1)}, bf16[512,320]{1,0:...) custom-call(s32[2]{0:T(128)} %pad_add_fusion.meta_ref.refs_0_, ...), custom_call_target="tpu_custom_call" | custom-call | tf_op jit(solution)/shard_map/forward/pallas_call | solution.py:598
  138.9 9.8 %all-to-all-done.refs_1_ = bf16[16,56,512]{2,1,0:T(8,128)(2,1)S(1)} async-done(((bf16[16,56,512]{2,1,0:T(8,128)(2,1)}), bf16[16,56,512]{2,1,0:T(8,128)(2,1)S(1)}, u32[]{:S(2)}, u32[]{:S(2)}) %all-to-all-start) | async-done | bytes 917536 | tf_op jit(solution)/shard_map/all_to_all | solution.py:550
  148.7 6.4 %all-to-all-start.3 = ((bf16[16,56,512]{2,1,0:T(8,128)(2,1)}), bf16[16,56,512]{2,1,0:T(8,128)(2,1)S(1)}, u32[]{:S(2)}, u32[]{:S(2)}) async-start(bf16[16,56,512]{2,1,0:T(8,128)(2,1)} %get-tuple-element.103), calls=%async_computation.3 | async-start | bytes 1835008 | tf_op jit(solution)/shard_map/all_to_all | solution.py:550
  155.1 11.0 %forward.5 = (bf16[16,56,512]{2,1,0:T(8,128)(2,1)}, f32[320,512]{1,0:T(8,128)}, f32[320,128]{1,0:T(8,128)}, bf16[320,512]{1,0:T(8,128)(2,1)}, bf16[512,320]{1,0:...) custom-call(s32[2]{0:T(128)} %pad_add_fusion.meta_ref.refs_0_, ...), custom_call_target="tpu_custom_call" | custom-call | tf_op jit(solution)/shard_map/forward/pallas_call | solution.py:598
  166.1 9.7 %all-to-all-done.3.refs_1_ = bf16[16,56,512]{2,1,0:T(8,128)(2,1)S(1)} async-done(((bf16[16,56,512]{2,1,0:T(8,128)(2,1)}), bf16[16,56,512]{2,1,0:T(8,128)(2,1)S(1)}, u32[]{:S(2)}, u32[]{:S(2)}) %all-to-all-start.3) | async-done | bytes 917536 | tf_op jit(solution)/shard_map/all_to_all | solution.py:550
  175.8 6.1 %all-to-all-start.6 = ((bf16[16,56,512]{2,1,0:T(8,128)(2,1)}), bf16[16,56,512]{2,1,0:T(8,128)(2,1)S(1)}, u32[]{:S(2)}, u32[]{:S(2)}) async-start(bf16[16,56,512]{2,1,0:T(8,128)(2,1)} %get-tuple-element.114), calls=%async_computation.6 | async-start | bytes 1835008 | tf_op jit(solution)/shard_map/all_to_all | solution.py:550
  181.9 18.7 %expert.3 = (bf16[16,56,512]{2,1,0:T(8,128)(2,1)}, bf16[16,56,512]{2,1,0:T(8,128)(2,1)}, f32[512,2048]{1,0:T(8,128)}, f32[512,2048]{1,0:T(8,128)}, f32[1,2048]{1,0:T(1,128)}, /*index=5*/f32[1,512]{1,0:T(1,128)}) custom-call(s32[2]{0:T(128)} %pad_add_fusion.meta_ref.refs_0_, bf16[16,56,512]{2,1,0:T(8,128)(2,1)} %copy-done.9, ...), custom_call_target="tpu_custom_call" | custom-call | tf_op jit(solution)/shard_map/expert/pallas_call | solution.py:641
  200.7 2.0 all-to-all-done.6.refs_1_
  202.7 6.6 %all-to-all-start.9 = ((bf16[16,56,512]{2,1,0:T(8,128)(2,1)}), bf16[16,56,512]{2,1,0:T(8,128)(2,1)S(1)}, u32[]{:S(2)}, u32[]{:S(2)}) async-start(bf16[16,56,512]{2,1,0:T(8,128)(2,1)} %get-tuple-element.124), calls=%async_computation.9 | async-start | bytes 1835008 | tf_op jit(solution)/shard_map/all_to_all | solution.py:550
  209.3 19.9 %expert.4 = (bf16[16,56,512]{2,1,0:T(8,128)(2,1)}, bf16[16,56,512]{2,1,0:T(8,128)(2,1)}, f32[512,2048]{1,0:T(8,128)}, f32[512,2048]{1,0:T(8,128)}, f32[1,2048]{1,0:T(1,128)}, /*index=5*/f32[1,512]{1,0:T(1,128)}) custom-call(s32[2]{0:T(128)} %pad_add_fusion.meta_ref.refs_0_, ...), custom_call_target="tpu_custom_call", output_to_operand_aliasing={{2}: (8, {}), {3}: (9, {}), {4}: (10, {}), {5}: (11, {})} | custom-call | tf_op jit(solution)/shard_map/expert/pallas_call | solution.py:641
  229.2 0.9 all-to-all-done.9.refs_2_
  230.1 6.1 %all-to-all-start.10 = ((bf16[16,56,512]{2,1,0:T(8,128)(2,1)}), bf16[16,56,512]{2,1,0:T(8,128)(2,1)S(1)}, u32[]{:S(2)}, u32[]{:S(2)}) async-start(bf16[16,56,512]{2,1,0:T(8,128)(2,1)} %get-tuple-element.137), calls=%async_computation.10 | async-start | bytes 1835008 | tf_op jit(solution)/shard_map/all_to_all | solution.py:550
  236.2 19.9 %expert.5 = (bf16[16,56,512]{2,1,0:T(8,128)(2,1)}, bf16[16,56,512]{2,1,0:T(8,128)(2,1)}, f32[512,2048]{1,0:T(8,128)}, f32[512,2048]{1,0:T(8,128)}, f32[1,2048]{1,0:T(1,128)}, /*index=5*/f32[1,512]{1,0:T(1,128)}) custom-call(s32[2]{0:T(128)} %pad_add_fusion.meta_ref.refs_0_, ...), custom_call_target="tpu_custom_call", output_to_operand_aliasing={{2}: (8, {}), {3}: (9, {}), {4}: (10, {}), {5}: (11, {})} | custom-call | tf_op jit(solution)/shard_map/expert/pallas_call | solution.py:641
  256.1 0.9 all-to-all-done.10.refs_2_
  257.0 28.6 %all_to_all.60.refs_2_ = bf16[16,56,512]{2,1,0:T(8,128)(2,1)} all-to-all(bf16[16,56,512]{2,1,0:T(8,128)(2,1)} %get-tuple-element.152), channel_id=1, replica_groups=mesh['dp'=16,'seq'=2] {'dp'}, dimensions={0} | all-to-all | bytes 1835008 | tf_op jit(solution)/shard_map/all_to_all | solution.py:550
  285.6 4.7 all-to-all-start.2
  290.2 15.9 %backward.3 = (f32[320,512]{1,0:T(8,128)}, bf16[1,320,512]{2,1,0:T(8,128)(2,1)}, f32[320,512]{1,0:T(8,128)}, f32[512,2048]{1,0:T(8,128)}, f32[128,512]{1,0:T(8,128)}) custom-call(s32[2]{0:T(128)} %pad_add_fusion.meta_ref.refs_0_, s32[3]{0:T(128)} %refs_1_.5, bf16[16,56,512]{2,1,0:T(8,128)(2,1)} %copy-done.3, s32[320,8]{1,0:T(8,128)} %get-tuple-element.99.pcol_ref.refs_3_, ...), custom_call_target="tpu_custom_call" | custom-call | tf_op jit(solution)/shard_map/backward/pallas_call | solution.py:703
  306.1 1.6 collective-permute-start.1
  307.7 8.8 %collective-permute-done.1 = bf16[320,512]{1,0:T(8,128)(2,1)S(1)} collective-permute-done((bf16[320,512]{1,0:T(8,128)(2,1)}, bf16[320,512]{1,0:T(8,128)(2,1)S(1)}, u32[]{:S(2)}, u32[]{:S(2)}) %collective-permute-start.1) | collective-permute-done | bytes 327712 | tf_op jit(solution)/shard_map/ppermute | solution.py:773
  317.2 2.9 finish.3
  320.2 17.3 %backward.4 = (f32[320,512]{1,0:T(8,128)}, bf16[1,320,512]{2,1,0:T(8,128)(2,1)}, f32[320,512]{1,0:T(8,128)}, f32[512,2048]{1,0:T(8,128)}, f32[128,512]{1,0:T(8,128)}) custom-call(s32[2]{0:T(128)} %pad_add_fusion.meta_ref.refs_0_, s32[3]{0:T(128)} %refs_1_.5, bf16[16,56,512]{2,1,0:T(8,128)(2,1)} %copy-done.8, ...), custom_call_target="tpu_custom_call", output_to_operand_aliasing={{3}: (15, {}), {4}: (16, {})} | custom-call | tf_op jit(solution)/shard_map/backward/pallas_call | solution.py:703
  337.5 1.6 collective-permute-start.2
  339.1 8.0 %collective-permute-done.2 = bf16[320,512]{1,0:T(8,128)(2,1)S(1)} collective-permute-done((bf16[320,512]{1,0:T(8,128)(2,1)}, bf16[320,512]{1,0:T(8,128)(2,1)S(1)}, u32[]{:S(2)}, u32[]{:S(2)}) %collective-permute-start.2) | collective-permute-done | bytes 327712 | tf_op jit(solution)/shard_map/ppermute | solution.py:773
  347.8 2.9 finish.4
  350.7 17.1 %backward.5 = (f32[320,512]{1,0:T(8,128)}, bf16[1,320,512]{2,1,0:T(8,128)(2,1)}, f32[320,512]{1,0:T(8,128)}, f32[512,2048]{1,0:T(8,128)}, f32[128,512]{1,0:T(8,128)}) custom-call(s32[2]{0:T(128)} %pad_add_fusion.meta_ref.refs_0_, s32[3]{0:T(128)} %refs_1_.5, ...), custom_call_target="tpu_custom_call", output_to_operand_aliasing={{3}: (15, {}), {4}: (16, {})} | custom-call | tf_op jit(solution)/shard_map/backward/pallas_call | solution.py:703
  367.9 1.6 collective-permute-start.3
  369.4 2.5 convert.7
  371.9 4.6 collective-permute-done.3
  377.3 2.9 finish.5
  380.2 1.0 convert_bitcast_fusion
  381.3 5.0 all-to-all-start.5
  386.4 1.6 pad_maximum_fusion
  388.0 2.7 convert_element_type.30
  391.4 1.6 convert_element_type.31
  393.1 1.5 collective-permute-start.6
  395.1 12.1 %all-to-all-done.5.back_ref = bf16[16,56,512]{2,1,0:T(8,128)(2,1)} async-done(((bf16[16,56,512]{2,1,0:T(8,128)(2,1)}), bf16[16,56,512]{2,1,0:T(8,128)(2,1)}, u32[]{:S(2)}, u32[]{:S(2)}) %all-to-all-start.5) | async-done | bytes 917536 | tf_op jit(solution)/shard_map/all_to_all | solution.py:550
  407.2 6.3 %all-to-all-start.8 = ((bf16[16,56,512]{2,1,0:T(8,128)(2,1)}), bf16[16,56,512]{2,1,0:T(8,128)(2,1)S(1)}, u32[]{:S(2)}, u32[]{:S(2)}) async-start(bf16[16,56,512]{2,1,0:T(8,128)(2,1)} %get-tuple-element.120), calls=%async_computation.8 | async-start | bytes 1835008 | tf_op jit(solution)/shard_map/all_to_all | solution.py:550
  413.6 1.6 collective-permute-start.7
  415.1 71.2 %collective-permute-done.7 = bf16[1,2560]{1,0:T(2,128)(2,1)S(1)} collective-permute-done((bf16[1,2560]{1,0:T(2,128)(2,1)S(1)}, bf16[1,2560]{1,0:T(2,128)(2,1)S(1)}, u32[]{:S(2)}, u32[]{:S(2)}) %collective-permute-start.7) | collective-permute-done | bytes 5152 | tf_op jit(solution)/shard_map/ppermute | solution.py:791
  487.5 3.1 mix.3
  490.6 3.2 mix.4
  493.8 0.9 copy-done.5
  494.7 3.1 mix.5
  497.9 1.5 collective-permute-start.4
  499.3 2.1 pad_maximum_fusion.1
  501.5 8.3 %sum_experts.1 = (f32[1,512,2048]{2,1,0:T(8,128)}, f32[1,2048,512]{2,1,0:T(8,128)}) custom-call(f32[512,2048]{1,0:T(8,128)} %get-tuple-element.169.gup_ref, f32[512,2048]{1,0:T(8,128)} %get-tuple-element.170.gdn_ref, bf16[512,2048]{1,0:T(8,128)(2,1)} %collective-permute-done.5.got_up, bf16[512,2048]{1,0:T(8,128)(2,1)} %collective-permute-done.6.got_dn), custom_call_target="tpu_custom_call" | custom-call | tf_op jit(solution)/shard_map/sum_experts/pallas_call | solution.py:798
  509.9 1.1 pad_maximum_fusion.2
  511.0 0.8 slice_reduce_fusion
  (78 shorter events, 13.6 us)
Async XLA Ops:
  11.8 74.3 %copy-start.1 = (bf16[3,320,512]{2,1,0:T(8,128)(2,1)S(1)}, bf16[3,320,512]{2,1,0:T(8,128)(2,1)}, u32[]{:S(2)}) copy-start(bf16[3,320,512]{2,1,0:T(8,128)(2,1)} %x_ref.5) | copy-start | bytes 2949124
  11.8 28.4 %all-to-all-start.7 = ((bf16[16,56,512]{2,1,0:T(8,128)(2,1)}), bf16[16,56,512]{2,1,0:T(8,128)(2,1)S(1)}, u32[]{:S(2)}, u32[]{:S(2)}) async-start(bf16[16,56,512]{2,1,0:T(8,128)(2,1)} %get-tuple-element.115), calls=%async_computation.7 | async-start | bytes 1835008 | tf_op jit(solution)/shard_map/all_to_all | solution.py:550
  19.3 90.9 %all-gather.2.cloned.1.call-start = ((), (), s32[]{:S(2)}) async-start(), calls=%async_computation.13 | async-start | bytes 2367488 | tf_op jit(solution)/shard_map/all_gather | solution.py:535
  40.2 82.0 %copy-start.6 = (bf16[16,56,512]{2,1,0:T(8,128)(2,1)}, bf16[16,56,512]{2,1,0:T(8,128)(2,1)S(1)}, u32[]{:S(2)}) copy-start(bf16[16,56,512]{2,1,0:T(8,128)(2,1)S(1)} %all-to-all-done.7.refs_2_) | copy-start | bytes 2752516
  40.2 38.9 %all-to-all-start.4 = ((bf16[16,56,512]{2,1,0:T(8,128)(2,1)}), bf16[16,56,512]{2,1,0:T(8,128)(2,1)S(1)}, u32[]{:S(2)}, u32[]{:S(2)}) async-start(bf16[16,56,512]{2,1,0:T(8,128)(2,1)} %get-tuple-element.104), calls=%async_computation.4 | async-start | bytes 1835008 | tf_op jit(solution)/shard_map/all_to_all | solution.py:550
  79.0 0.9 copy-start.7
  80.0 42.2 %all-to-all-start.1 = ((bf16[16,56,512]{2,1,0:T(8,128)(2,1)}), bf16[16,56,512]{2,1,0:T(8,128)(2,1)}, u32[]{:S(2)}, u32[]{:S(2)}) async-start(bf16[16,56,512]{2,1,0:T(8,128)(2,1)} %get-tuple-element.97), calls=%async_computation.1 | async-start | bytes 1835008 | tf_op jit(solution)/shard_map/all_to_all | solution.py:550
  86.1 24.1 %collective-permute-start = (bf16[3,320,512]{2,1,0:T(8,128)(2,1)S(1)}, bf16[3,320,512]{2,1,0:T(8,128)(2,1)S(1)}, u32[]{:S(2)}, u32[]{:S(2)}) collective-permute-start(bf16[3,320,512]{2,1,0:T(8,128)(2,1)S(1)} %copy-done.1), channel_id=1, source_target_pairs={{1,0},{0,1},{3,2},{2,3},{5,4},{4,5},{7,6},{6,7},{9,8},{8,9},{11,10... | collective-permute-start | bytes 2949128 | tf_op jit(solution)/shard_map/ppermute | solution.py:540
  110.2 0.9 copy-start.2
  122.2 26.5 %all-to-all-start = ((bf16[16,56,512]{2,1,0:T(8,128)(2,1)}), bf16[16,56,512]{2,1,0:T(8,128)(2,1)S(1)}, u32[]{:S(2)}, u32[]{:S(2)}) async-start(bf16[16,56,512]{2,1,0:T(8,128)(2,1)} %get-tuple-element.96), calls=%async_computation | async-start | bytes 1835008 | tf_op jit(solution)/shard_map/all_to_all | solution.py:550
  148.7 33.2 %copy-start.9 = (bf16[16,56,512]{2,1,0:T(8,128)(2,1)}, bf16[16,56,512]{2,1,0:T(8,128)(2,1)S(1)}, u32[]{:S(2)}) copy-start(bf16[16,56,512]{2,1,0:T(8,128)(2,1)S(1)} %all-to-all-done.refs_1_) | copy-start | bytes 2752516
  148.7 27.1 %all-to-all-start.3 = ((bf16[16,56,512]{2,1,0:T(8,128)(2,1)}), bf16[16,56,512]{2,1,0:T(8,128)(2,1)S(1)}, u32[]{:S(2)}, u32[]{:S(2)}) async-start(bf16[16,56,512]{2,1,0:T(8,128)(2,1)} %get-tuple-element.103), calls=%async_computation.3 | async-start | bytes 1835008 | tf_op jit(solution)/shard_map/all_to_all | solution.py:550
  175.8 24.8 %copy-start.10 = (bf16[16,56,512]{2,1,0:T(8,128)(2,1)}, bf16[16,56,512]{2,1,0:T(8,128)(2,1)S(1)}, u32[]{:S(2)}) copy-start(bf16[16,56,512]{2,1,0:T(8,128)(2,1)S(1)} %all-to-all-done.3.refs_1_) | copy-start | bytes 2752516
  175.8 26.9 %all-to-all-start.6 = ((bf16[16,56,512]{2,1,0:T(8,128)(2,1)}), bf16[16,56,512]{2,1,0:T(8,128)(2,1)S(1)}, u32[]{:S(2)}, u32[]{:S(2)}) async-start(bf16[16,56,512]{2,1,0:T(8,128)(2,1)} %get-tuple-element.114), calls=%async_computation.6 | async-start | bytes 1835008 | tf_op jit(solution)/shard_map/all_to_all | solution.py:550
  202.7 26.5 %copy-start.11 = (bf16[16,56,512]{2,1,0:T(8,128)(2,1)}, bf16[16,56,512]{2,1,0:T(8,128)(2,1)S(1)}, u32[]{:S(2)}) copy-start(bf16[16,56,512]{2,1,0:T(8,128)(2,1)S(1)} %all-to-all-done.6.refs_1_) | copy-start | bytes 2752516
  202.7 27.4 %all-to-all-start.9 = ((bf16[16,56,512]{2,1,0:T(8,128)(2,1)}), bf16[16,56,512]{2,1,0:T(8,128)(2,1)S(1)}, u32[]{:S(2)}, u32[]{:S(2)}) async-start(bf16[16,56,512]{2,1,0:T(8,128)(2,1)} %get-tuple-element.124), calls=%async_computation.9 | async-start | bytes 1835008 | tf_op jit(solution)/shard_map/all_to_all | solution.py:550
  230.1 26.0 %copy-start.3 = (bf16[16,56,512]{2,1,0:T(8,128)(2,1)}, bf16[16,56,512]{2,1,0:T(8,128)(2,1)S(1)}, u32[]{:S(2)}) copy-start(bf16[16,56,512]{2,1,0:T(8,128)(2,1)S(1)} %all-to-all-done.9.refs_2_) | copy-start | bytes 2752516
  230.1 26.9 %all-to-all-start.10 = ((bf16[16,56,512]{2,1,0:T(8,128)(2,1)}), bf16[16,56,512]{2,1,0:T(8,128)(2,1)S(1)}, u32[]{:S(2)}, u32[]{:S(2)}) async-start(bf16[16,56,512]{2,1,0:T(8,128)(2,1)} %get-tuple-element.137), calls=%async_computation.10 | async-start | bytes 1835008 | tf_op jit(solution)/shard_map/all_to_all | solution.py:550
  257.0 49.2 %copy-start.8 = (bf16[16,56,512]{2,1,0:T(8,128)(2,1)}, bf16[16,56,512]{2,1,0:T(8,128)(2,1)S(1)}, u32[]{:S(2)}) copy-start(bf16[16,56,512]{2,1,0:T(8,128)(2,1)S(1)} %all-to-all-done.10.refs_2_) | copy-start | bytes 2752516
  285.6 95.7 %all-to-all-start.2 = ((bf16[16,56,512]{2,1,0:T(8,128)(2,1)}), bf16[16,56,512]{2,1,0:T(8,128)(2,1)S(1)}, u32[]{:S(2)}, u32[]{:S(2)}) async-start(bf16[16,56,512]{2,1,0:T(8,128)(2,1)} %get-tuple-element.98), calls=%async_computation.2 | async-start | bytes 1835008 | tf_op jit(solution)/shard_map/all_to_all | solution.py:550
  306.1 10.4 %collective-permute-start.1 = (bf16[320,512]{1,0:T(8,128)(2,1)}, bf16[320,512]{1,0:T(8,128)(2,1)S(1)}, u32[]{:S(2)}, u32[]{:S(2)}) collective-permute-start(bf16[320,512]{1,0:T(8,128)(2,1)} %bitcast.44), channel_id=1, source_target_pairs={{0,1},{1,0},{2,3},{3,2},{4,5},{5,4},{6,7},{7,6},{8,9},{9,8},{10,11... | collective-permute-start | bytes 983048 | tf_op jit(solution)/shard_map/ppermute | solution.py:773
  316.5 0.7 copy-start.14
  337.5 9.5 %collective-permute-start.2 = (bf16[320,512]{1,0:T(8,128)(2,1)}, bf16[320,512]{1,0:T(8,128)(2,1)S(1)}, u32[]{:S(2)}, u32[]{:S(2)}) collective-permute-start(bf16[320,512]{1,0:T(8,128)(2,1)} %bitcast.43), channel_id=1, source_target_pairs={{0,1},{1,0},{2,3},{3,2},{4,5},{5,4},{6,7},{7,6},{8,9},{9,8},{10,11... | collective-permute-start | bytes 983048 | tf_op jit(solution)/shard_map/ppermute | solution.py:773
  347.1 0.7 copy-start.15
  367.9 8.7 %collective-permute-start.3 = (bf16[320,512]{1,0:T(8,128)(2,1)}, bf16[320,512]{1,0:T(8,128)(2,1)S(1)}, u32[]{:S(2)}, u32[]{:S(2)}) collective-permute-start(bf16[320,512]{1,0:T(8,128)(2,1)} %bitcast.42), channel_id=1, source_target_pairs={{0,1},{1,0},{2,3},{3,2},{4,5},{5,4},{6,7},{7,6},{8,9},{9,8},{10,11... | collective-permute-start | bytes 983048 | tf_op jit(solution)/shard_map/ppermute | solution.py:773
  376.5 0.7 copy-start.13
  381.3 6.7 %copy-start.4 = (bf16[16,56,512]{2,1,0:T(8,128)(2,1)}, bf16[16,56,512]{2,1,0:T(8,128)(2,1)S(1)}, u32[]{:S(2)}) copy-start(bf16[16,56,512]{2,1,0:T(8,128)(2,1)S(1)} %all-to-all-done.2.back_ref) | copy-start | bytes 2752516
  381.3 25.9 %all-to-all-start.5 = ((bf16[16,56,512]{2,1,0:T(8,128)(2,1)}), bf16[16,56,512]{2,1,0:T(8,128)(2,1)}, u32[]{:S(2)}, u32[]{:S(2)}) async-start(bf16[16,56,512]{2,1,0:T(8,128)(2,1)} %get-tuple-element.109), calls=%async_computation.5 | async-start | bytes 1835008 | tf_op jit(solution)/shard_map/all_to_all | solution.py:550
  386.3 111.5 %reduce-scatter.2.cloned.1.call-start = ((), (), s32[]{:S(2)}) async-start(), calls=%async_computation.14 | async-start | bytes 2367488 | tf_op jit(solution)/shard_map/reduce_scatter | solution.py:818
  388.0 3.5 copy-start
  390.7 22.9 %copy-start.20 = (f32[1,2048]{1,0:T(1,128)S(1)}, f32[1,2048]{1,0:T(1,128)}, u32[]{:S(2)}) copy-start(f32[1,2048]{1,0:T(1,128)} %get-tuple-element.172) | copy-start | bytes 24580
  390.7 22.9 %copy-start.21 = (f32[1,512]{1,0:T(1,128)S(1)}, f32[1,512]{1,0:T(1,128)}, u32[]{:S(2)}) copy-start(f32[1,512]{1,0:T(1,128)} %get-tuple-element.173) | copy-start | bytes 6148
  393.1 108.4 %collective-permute-start.6 = (bf16[512,2048]{1,0:T(8,128)(2,1)}, bf16[512,2048]{1,0:T(8,128)(2,1)}, u32[]{:S(2)}, u32[]{:S(2)}) collective-permute-start(bf16[512,2048]{1,0:T(8,128)(2,1)} %convert_element_type.31), channel_id=1, source_target_pairs={{0,1},{1,0},{2,3},{3,2},{4,5},{5,4},{6,7},{7,6},{8,9},{9,8},{10,11... | collective-permute-start | bytes 6291464 | tf_op jit(solution)/shard_map/ppermute | solution.py:796
  394.6 106.9 %collective-permute-start.5 = (bf16[512,2048]{1,0:T(8,128)(2,1)S(1)}, bf16[512,2048]{1,0:T(8,128)(2,1)}, u32[]{:S(2)}, u32[]{:S(2)}) collective-permute-start(bf16[512,2048]{1,0:T(8,128)(2,1)S(1)} %convert_element_type.30), channel_id=1, source_target_pairs={{0,1},{1,0},{2,3},{3,2},{4,5},{5,4},{6,7},{7,6},{8,9},{9,8},{10,11... | collective-permute-start | bytes 6291464 | tf_op jit(solution)/shard_map/ppermute | solution.py:795
  407.2 86.6 %all-to-all-start.8 = ((bf16[16,56,512]{2,1,0:T(8,128)(2,1)}), bf16[16,56,512]{2,1,0:T(8,128)(2,1)S(1)}, u32[]{:S(2)}, u32[]{:S(2)}) async-start(bf16[16,56,512]{2,1,0:T(8,128)(2,1)} %get-tuple-element.120), calls=%async_computation.8 | async-start | bytes 1835008 | tf_op jit(solution)/shard_map/all_to_all | solution.py:550
  413.6 72.7 %collective-permute-start.7 = (bf16[1,2560]{1,0:T(2,128)(2,1)S(1)}, bf16[1,2560]{1,0:T(2,128)(2,1)S(1)}, u32[]{:S(2)}, u32[]{:S(2)}) collective-permute-start(bf16[1,2560]{1,0:T(2,128)(2,1)S(1)} %convert_element_type.32), channel_id=1, source_target_pairs={{0,1},{1,0},{2,3},{3,2},{4,5},{5,4},{6,7},{7,6},{8,9},{9,8},{10,11... | collective-permute-start | bytes 15368 | tf_op jit(solution)/shard_map/ppermute | solution.py:791
  490.6 8.7 %copy-start.12 = (bf16[1,320,512]{2,1,0:T(8,128)(2,1)S(1)}, bf16[1,320,512]{2,1,0:T(8,128)(2,1)}, u32[]{:S(2)}) copy-start(bf16[1,320,512]{2,1,0:T(8,128)(2,1)} %mix.3) | copy-start | bytes 983044
  493.8 0.9 copy-start.5
  497.9 13.1 %collective-permute-start.4 = (bf16[32,2176]{1,0:T(8,128)(2,1)}, bf16[32,2176]{1,0:T(8,128)(2,1)S(1)}, u32[]{:S(2)}, u32[]{:S(2)}) collective-permute-start(bf16[32,2176]{1,0:T(8,128)(2,1)} %reduce-scatter.2.cloned.1.call-done), channel_id=1, source_target_pairs={{0,1},{1,0},{2,3},{3,2},{4,5},{5,4},{6,7},{7,6},{8,9},{9,8},{10,11... | collective-permute-start | bytes 417800 | tf_op jit(solution)/shard_map/ppermute | solution.py:791
  501.5 8.4 %copy-start.16 = (bf16[1,320,512]{2,1,0:T(8,128)(2,1)S(1)}, bf16[1,320,512]{2,1,0:T(8,128)(2,1)}, u32[]{:S(2)}) copy-start(bf16[1,320,512]{2,1,0:T(8,128)(2,1)} %get-tuple-element.136) | copy-start | bytes 983044
  501.5 8.4 %copy-start.17 = (bf16[1,320,512]{2,1,0:T(8,128)(2,1)S(1)}, bf16[1,320,512]{2,1,0:T(8,128)(2,1)}, u32[]{:S(2)}) copy-start(bf16[1,320,512]{2,1,0:T(8,128)(2,1)} %get-tuple-element.151) | copy-start | bytes 983044
  501.5 8.4 %copy-start.18 = (bf16[1,320,512]{2,1,0:T(8,128)(2,1)S(1)}, bf16[1,320,512]{2,1,0:T(8,128)(2,1)}, u32[]{:S(2)}) copy-start(bf16[1,320,512]{2,1,0:T(8,128)(2,1)} %get-tuple-element.166) | copy-start | bytes 983044
  501.5 9.4 %copy-start.19 = (bf16[32,2176]{1,0:T(8,128)(2,1)S(1)}, bf16[32,2176]{1,0:T(8,128)(2,1)}, u32[]{:S(2)}) copy-start(bf16[32,2176]{1,0:T(8,128)(2,1)} %reduce-scatter.2.cloned.1.call-done) | copy-start | bytes 417796
Sparse Core Ops, SparseCore 0:
  26.6 52.5 all-gather.1
  391.5 69.8 reduce-scatter.1

commit v2 on v1

--- a/solution.py
+++ b/solution.py
@@ -14,7 +14,7 @@
 F32 = jnp.float32
 EPS = 1e-06
 LANES = 128
-VEC = 7
+VEC = 8
 FF_BLOCK = 512
 VMEM_LIMIT = 60 * 1024 * 1024
 
@@ -52,11 +52,26 @@
     return jnp.transpose(w_ref[:, start : start + LANES].astype(F32))
 
 
-def place_kernel(experts, room, cols_ref, rows_ref, dy_ref, send_ref, prow_ref, pcol_ref):
-    tokens = cols_ref.shape[1]
+def pack_kernel(experts, qkv_ref, proj_ref, router_ref, vec_ref, out_ref):
+    width = proj_ref.shape[1]
+    shard = proj_ref.shape[0]
+    out_ref[:, : 3 * width] = qkv_ref[...]
+    out_ref[:, 3 * width : 4 * width] = proj_ref[...]
+    columns = jnp.transpose(vec_ref[...].astype(F32))
+    tail = jnp.zeros((shard, LANES - experts - columns.shape[1]), F32)
+    out_ref[:, 4 * width :] = jnp.concatenate(
+        [router_ref[...].astype(F32), columns, tail], axis=1
+    ).astype(BF)
+
+
+def place_kernel(experts, room, routes_ref, dy_ref, send_ref, prow_ref, pcol_ref):
+    tokens = routes_ref.shape[3]
     slots = experts * room
-    first_row = rows_ref[0, 0:1, :]
-    second_row = rows_ref[0, 1:2, :]
+    cols = routes_ref[0, 0, 0]
+    wide = jnp.concatenate([cols.astype(F32), jnp.zeros((tokens, LANES - TOP), F32)], axis=1)
+    across = jnp.transpose(wide)[0:8, :].astype(jnp.int32)
+    first_row = across[0:1, :]
+    second_row = across[1:2, :]
     hot_first = (iota((experts, tokens), 0) == first_row).astype(F32)
     hot_second = (iota((experts, tokens), 0) == second_row).astype(F32)
     earlier = (iota((tokens, tokens), 0) < iota((tokens, tokens), 1)).astype(BF)
@@ -65,16 +80,16 @@
     in_second = jnp.sum((before + hot_first) * hot_second, axis=0, keepdims=True).astype(jnp.int32)
     place_first = first_row * room + in_first
     place_second = second_row * room + in_second
-    prow_ref[0:1, :] = place_first
-    prow_ref[1:2, :] = place_second
+    prow_ref[0, 0:1, :] = place_first
+    prow_ref[0, 1:2, :] = place_second
     slot_of = iota((slots, tokens), 0)
     hot = jnp.where((slot_of == place_first) | (slot_of == place_second), 1.0, 0.0).astype(BF)
     flat = dy_ref[...].reshape(tokens, dy_ref.shape[-1])
     rows = mm(hot, flat)
     for e in range(experts):
         send_ref[e] = rows[e * room : (e + 1) * room].astype(BF)
-    first_col = cols_ref[0, :, 0:1]
-    second_col = cols_ref[0, :, 1:2]
+    first_col = cols[:, 0:1]
+    second_col = cols[:, 1:2]
     hot_first = (iota((tokens, experts), 1) == first_col).astype(F32)
     hot_second = (iota((tokens, experts), 1) == second_col).astype(F32)
     later = (iota((tokens, tokens), 1) < iota((tokens, tokens), 0)).astype(BF)
@@ -94,7 +109,7 @@
         )
     ):
         table = jnp.where(lane == at, col, table)
-    pcol_ref[...] = table
+    pcol_ref[0] = table
 
 
 def forward_kernel(
@@ -186,7 +201,7 @@
     gate_ref[...] = gates(mm(second, w_ref[:, misc_at : misc_at + LANES]), experts)
     slot_of = iota((slots, tokens), 0)
     hot = jnp.where(
-        (slot_of == prow_ref[0:1, :]) | (slot_of == prow_ref[1:2, :]), 1.0, 0.0
+        (slot_of == prow_ref[0, 0:1, :]) | (slot_of == prow_ref[0, 1:2, :]), 1.0, 0.0
     ).astype(BF)
     sent = mm(hot, second)
     for e in range(experts):
@@ -200,20 +215,19 @@
     return powers / jnp.sum(powers, axis=1, keepdims=True)
 
 
-def expert_kernel(cfg, first, *refs):
+def expert_kernel(cfg, first, last, *refs):
     groups, room, capacity, width = cfg
     meta_ref, buf_ref, dyb_ref, wm_ref, up_ref, ub_ref, down_ref, db_ref = refs[:8]
     refs = refs[8:]
     if not first:
-        gup_in, gdn_in, gb_in, gdb_in = refs[:4]
+        _, gup_in, gdn_in, gb_in, gdb_in = refs[:5]
+        refs = refs[5:]
+    r_ref, dbuf_ref, gup_ref, gdn_ref, gb_ref, gdb_ref = refs[:6]
+    refs = refs[6:]
+    if last:
+        lows = refs[:4]
         refs = refs[4:]
     (
-        r_ref,
-        dbuf_ref,
-        gup_ref,
-        gdn_ref,
-        gb_ref,
-        gdb_ref,
         flat_s,
         flatT_s,
         dr_s,
@@ -254,14 +268,25 @@
     gup = mm(flatT_s[...], low_pre)
     gdn = mm(drT_s[...], active)
     gbias = jnp.sum(low_pre.astype(F32), axis=0, keepdims=True)
-    if first:
-        gup_ref[...] = gup
-        gdn_ref[...] = gdn
-        gb_ref[...] = gbias
-    else:
-        gup_ref[...] = gup_in[...] + gup
-        gdn_ref[...] = gdn_in[...] + gdn
-        gb_ref[...] = gb_in[...] + gbias
+    if not first:
+        gup = gup_in[...] + gup
+        gdn = gdn_in[...] + gdn
+        gbias = gb_in[...] + gbias
+    gup_ref[...] = gup
+    gdn_ref[...] = gdn
+    gb_ref[...] = gbias
+    if last:
+        early = step < pl.num_programs(0) // 2
+
+        @pl.when(early)
+        def _():
+            lows[0][...] = gup.astype(BF)
+            lows[2][...] = gdn.astype(BF)
+
+        @pl.when(jnp.logical_not(early))
+        def _():
+            lows[1][...] = gup.astype(BF)
+            lows[3][...] = gdn.astype(BF)
 
     @pl.when(step == pl.num_programs(0) - 1)
     def _():
@@ -283,7 +308,7 @@
             dbuf_ref[e] = back[e]
 
 
-def backward_kernel(cfg, mb, first, *refs):
+def backward_kernel(cfg, mb, first, last, *refs):
     images, local_len, seq_count, width, experts, room, capacity = cfg
     (
         meta_ref,
@@ -301,12 +326,31 @@
         v_ref,
         lse_ref,
         n1T_ref,
-    ) = refs[:15]
-    refs = refs[15:]
+        own_ref,
+        oth_ref,
+    ) = refs[:17]
+    refs = refs[17:]
     if not first:
         g_in, mrow_in = refs[:2]
         refs = refs[2:]
-    down_own, down_oth, dm_ref, g_ref, mrow_ref, do_s, dqT_s, dkv_s = refs
+    down_own, down_oth, dm_ref = refs[:3]
+    refs = refs[3:]
+    if last:
+        low_ref = refs[0]
+        refs = refs[1:]
+    else:
+        g_ref = refs[0]
+        refs = refs[1:]
+    mrow_ref, do_s, dqT_s, dkv_s = refs
+
+    def add_dense(at, value):
+        if not first:
+            value = g_in[:, at] + value
+        if last:
+            low_ref[:, at] = value.astype(BF)
+        else:
+            g_ref[:, at] = value
+
     full_len = local_len * seq_count
     tokens = images * local_len
     slots = experts * room
@@ -321,7 +365,7 @@
     back_rows = dback.reshape(slots, width).astype(BF)
     slot_of = iota((tokens, slots), 1)
     hot = jnp.where(
-        (slot_of == pcol_ref[:, 0:1]) | (slot_of == pcol_ref[:, 1:2]), 1.0, 0.0
+        (slot_of == pcol_ref[0, :, 0:1]) | (slot_of == pcol_ref[0, :, 1:2]), 1.0, 0.0
     ).astype(BF)
     from_experts = mm(hot, back_rows)
     spare = jnp.where(iota((experts, room, 1), 1) == capacity, dback[:, :, : 2 * LANES], 0.0)
@@ -332,9 +376,9 @@
     lane = iota((tokens, LANES), 1)
     pulled = jnp.zeros((tokens, LANES), F32)
     for k in range(TOP):
-        within = jnp.where(lane == pcol_ref[:, 4 + k : 5 + k], 1.0, 0.0).astype(BF)
+        within = jnp.where(lane == pcol_ref[0, :, 4 + k : 5 + k], 1.0, 0.0).astype(BF)
         found = mm_nt(jnp.concatenate([within, within], axis=1), spare)
-        pulled = pulled + jnp.where(lane == pcol_ref[:, 2 + k : 3 + k], found, 0.0)
+        pulled = pulled + jnp.where(lane == pcol_ref[0, :, 2 + k : 3 + k], found, 0.0)
     gate = gate_ref[...]
     dlogit = gate * (pulled - jnp.sum(gate * pulled, axis=1, keepdims=True))
     dlogit_low = dlogit.astype(BF)
@@ -347,10 +391,7 @@
     da = dm.astype(BF)
     gproj = mm(oT_ref[...], da)
     proj = slice(3 * width, 4 * width)
-    if first:
-        g_ref[:, proj] = gproj
-    else:
-        g_ref[:, proj] = g_in[:, proj] + gproj
+    add_dense(proj, gproj)
     do_s[...] = mm_nt(da, w_ref[:, proj]).astype(BF)
     half_lane = iota((1, LANES), 1)
     low_half = (half_lane < HD).astype(BF)
@@ -358,6 +399,8 @@
     gqkv = [None, None]
     bias_q = jnp.zeros((1, width), F32)
     bias_v = jnp.zeros((1, width), F32)
+    gain_sum = jnp.zeros((1, width), F32)
+    shift_sum = jnp.zeros((1, width), F32)
     for b in range(images):
         span = slice(b * local_len, (b + 1) * local_len)
         wide = slice(b * full_len, (b + 1) * full_len)
@@ -408,17 +451,21 @@
         down = mm_nt(dkv, w_ref[:, width : 3 * width])
         down_own[span, :] = mm_nt(dq, w_ref[:, :width])
         down_own[span, :] += down[:local_len]
-        for j in range(seq_count - 1):
-            down_oth[j, span, :] = down[(j + 1) * local_len : (j + 2) * local_len].astype(BF)
-    if first:
-        g_ref[:, :width] = gqkv[0]
-        g_ref[:, width : 3 * width] = gqkv[1]
-    else:
-        g_ref[:, :width] = g_in[:, :width] + gqkv[0]
-        g_ref[:, width : 3 * width] = g_in[:, width : 3 * width] + gqkv[1]
+        for j in range(seq_count):
+            part = down_own[span, :] if j == 0 else down[j * local_len : (j + 1) * local_len]
+            tokens_in = own_ref[b] if j == 0 else oth_ref[j - 1, b]
+            first_unit, _ = norm_parts(tokens_in.astype(F32))
+            gain_sum = gain_sum + jnp.sum(part * first_unit, axis=0, keepdims=True)
+            shift_sum = shift_sum + jnp.sum(part, axis=0, keepdims=True)
+            if j > 0:
+                down_oth[j - 1, span, :] = part.astype(BF)
+    add_dense(slice(0, width), gqkv[0])
+    add_dense(slice(width, 3 * width), gqkv[1])
     row = iota((LANES, 1), 0)
     mrow = jnp.where(row < experts, mrow_ref[...], 0.0)
     sums = (
+        gain_sum,
+        shift_sum,
         bias_q,
         bias_v,
         jnp.sum(da.astype(F32), axis=0, keepdims=True),
@@ -426,11 +473,16 @@
         jnp.sum(dn2, axis=0, keepdims=True),
     )
     for j, value in enumerate(sums):
-        mrow = jnp.where(row == experts + 2 + j, value, mrow)
-    mrow_ref[...] = mrow if first else mrow_in[...] + mrow
-
-
-def input_kernel(cfg, own_ref, got_ref, x_ref, dm_ref, wm_ref, mrow_in, out_ref, mrow_ref):
+        mrow = jnp.where(row == experts + j, value, mrow)
+    if not first:
+        mrow = mrow_in[...] + mrow
+    mrow_ref[...] = mrow
+    if last:
+        low_ref[:, misc_at : misc_at + LANES] = jnp.transpose(mrow).astype(BF)
+
+
+def input_kernel(cfg, own_ref, got_ref, x_ref, dm_ref, wm_ref, *refs):
+    out_ref = refs[-1]
     images, local_len, seq_count, width, experts = cfg
     tokens = images * local_len
     rows = jnp.transpose(wm_ref[...].astype(F32))
@@ -440,13 +492,10 @@
     unit, scale = norm_parts(x_ref[...].reshape(tokens, width).astype(F32))
     grad = dm_ref[...] + norm_pull(unit, scale, rows[experts : experts + 1, :], dn1)
     out_ref[...] = grad.astype(BF).reshape(images, local_len, width)
-    row = iota((LANES, 1), 0)
-    mrow = jnp.where(row == experts, jnp.sum(dn1 * unit, axis=0, keepdims=True), 0.0)
-    mrow = jnp.where(row == experts + 1, jnp.sum(dn1, axis=0, keepdims=True), mrow)
-    mrow_ref[...] = mrow_in[...] + mrow
-
-
-def mix_kernel(cfg, back_ref, pcol_ref, gate_ref, middle_ref, out_ref):
+
+
+def mix_kernel(cfg, back_ref, pcol_ref, gate_ref, middle_ref, *refs):
+    out_ref = refs[-1]
     images, local_len, width, experts, room = cfg
     tokens = images * local_len
     slots = experts * room
@@ -456,19 +505,18 @@
     gate = gate_ref[...]
     total = middle_ref[...]
     for k in range(TOP):
-        hot = jnp.where(slot_of == pcol_ref[:, k : k + 1], 1.0, 0.0).astype(BF)
-        chosen = jnp.where(lane == pcol_ref[:, 2 + k : 3 + k], gate, 0.0)
+        hot = jnp.where(slot_of == pcol_ref[0, :, k : k + 1], 1.0, 0.0).astype(BF)
+        chosen = jnp.where(lane == pcol_ref[0, :, 2 + k : 3 + k], gate, 0.0)
         total = total + jnp.sum(chosen, axis=1, keepdims=True) * mm(hot, back)
     out_ref[...] = total.astype(BF).reshape(images, local_len, width)
 
 
-def sum_kernel(gup_ref, gdn_ref, got_up, got_dn, up_ref, dn_ref):
-    up_ref[0] = gup_ref[...] + got_up[...].astype(F32)
-    dn_ref[0] = jnp.transpose(gdn_ref[...] + got_dn[...].astype(F32))
-
-
-def whole_spec():
-    return pl.BlockSpec(memory_space=pltpu.VMEM)
+def sum_kernel(gup_ref, gdn_ref, up_early, up_late, dn_early, dn_late, up_ref, dn_ref):
+    late = pl.program_id(0) >= pl.num_programs(0) // 2
+    got_up = jnp.where(late, up_late[...], up_early[...])
+    got_dn = jnp.where(late, dn_late[...], dn_early[...])
+    up_ref[0] = gup_ref[...] + got_up.astype(F32)
+    dn_ref[0] = jnp.transpose(gdn_ref[...] + got_dn.astype(F32))
 
 
 def smem_spec():
@@ -479,8 +527,18 @@
     return pltpu.CompilerParams(vmem_limit_bytes=VMEM_LIMIT)
 
 
+def cost(micros):
+    return pl.CostEstimate(
+        flops=int(micros * 1e9), transcendentals=0, bytes_accessed=int(micros * 2e6)
+    )
+
+
 def struct(shape, kind):
     return jax.ShapeDtypeStruct(shape, kind)
+
+
+def after(value, *others):
+    return lax.optimization_barrier((value, *others))[0]
 
 
 def on_device(
@@ -517,23 +575,34 @@
     assert up_weight.shape[0] == 1 and experts == dp_count
     assert experts + VEC <= LANES and capacity <= LANES
     meta = jnp.stack([lax.axis_index("dp"), lax.axis_index("seq")]).astype(jnp.int32)
-
-    shard = router_weight.shape[0]
-    pieces = [
-        qkv_weight,
-        proj_weight,
-        router_weight,
-        attn_norm_gain[:, None],
-        attn_norm_bias[:, None],
-        query_value_bias[0][:, None],
-        query_value_bias[1][:, None],
-        proj_bias[:, None],
-        moe_norm_gain[:, None],
-        moe_norm_bias[:, None],
-        jnp.zeros((shard, LANES - experts - VEC), BF),
-    ]
-    packed = lax.all_gather(jnp.concatenate(pieces, axis=1), "dp", axis=0, tiled=True)
     packed_width = 4 * width + LANES
+
+    def full(shape):
+        return pl.BlockSpec(shape, lambda i: (0,) * len(shape))
+
+    def token_spec(mb):
+        return pl.BlockSpec((count, local_len, width), lambda i: (mb, 0, 0))
+
+    def table_spec(mb, shape):
+        return pl.BlockSpec((1, *shape), lambda i: (mb, 0, 0))
+
+    def block_spec(mb):
+        return pl.BlockSpec((experts, room, width), lambda i: (0, mb, 0))
+
+    any_spec = pl.BlockSpec(memory_space=pl.ANY)
+    other_spec = lambda mb: pl.BlockSpec(
+        (seq_count - 1, count, local_len, width), lambda i: (0, mb, 0, 0)
+    )
+    halved = hidden // FF_BLOCK // 2
+    early_spec = lambda: pl.BlockSpec(
+        (width, FF_BLOCK), lambda i: (0, jnp.minimum(i, halved - 1))
+    )
+    late_spec = lambda: pl.BlockSpec(
+        (width, FF_BLOCK), lambda i: (0, jnp.maximum(i - halved, 0))
+    )
+    misc_spec = pl.BlockSpec((width, LANES), lambda i: (0, 4 * width // LANES))
+    moved = struct((experts, room, width), BF)
+    merged = struct((experts, MICRO * room, width), BF)
 
     others = jnp.stack(
         [
@@ -543,45 +612,54 @@
             for j in range(1, seq_count)
         ]
     )
-    cols = routes.reshape(MICRO, tokens, TOP)
-    rows = jnp.swapaxes(cols, 1, 2)
+    vectors = jnp.concatenate(
+        [
+            jnp.stack([attn_norm_gain, attn_norm_bias]),
+            query_value_bias,
+            jnp.stack([proj_bias, moe_norm_gain, moe_norm_bias, jnp.zeros_like(proj_bias)]),
+        ],
+        axis=0,
+    )
+    shard = router_weight.shape[0]
+    pack_args = (qkv_weight, proj_weight, router_weight, vectors)
+    packed_shard = pl.pallas_call(
+        functools.partial(pack_kernel, experts),
+        grid=(1,),
+        in_specs=[full(a.shape) for a in pack_args],
+        out_specs=full((shard, packed_width)),
+        out_shape=struct((shard, packed_width), BF),
+        compiler_params=params(),
+        cost_estimate=cost(1),
+        name="pack",
+    )(*pack_args)
+    packed = lax.all_gather(packed_shard, "dp", axis=0, tiled=True)
 
     def exchange(array):
         return lax.all_to_all(array, "dp", split_axis=0, concat_axis=0, tiled=True)
 
-    def token_spec(mb):
-        return pl.BlockSpec((count, local_len, width), lambda i: (mb, 0, 0))
-
-    def full(shape):
-        return pl.BlockSpec(shape, lambda i: (0,) * len(shape))
-
-    misc_spec = pl.BlockSpec((width, LANES), lambda i: (0, 4 * width // LANES))
-    moved = struct((experts, room, width), BF)
-
-    def place(mb):
-        return pl.pallas_call(
-            functools.partial(place_kernel, experts, room),
-            grid=(1,),
-            in_specs=[
-                pl.BlockSpec((1, tokens, TOP), lambda i: (mb, 0, 0)),
-                pl.BlockSpec((1, TOP, tokens), lambda i: (mb, 0, 0)),
-                token_spec(mb),
-            ],
-            out_specs=[
-                full((experts, room, width)),
-                full((TOP, tokens)),
-                full((tokens, 8)),
-            ],
-            out_shape=[
-                moved,
-                struct((TOP, tokens), jnp.int32),
-                struct((tokens, 8), jnp.int32),
-            ],
-            compiler_params=params(),
-            name="place",
-        )(cols, rows, cotangent)
-
-    def forward(mb, prow):
+    sent_dy, prow, pcol = pl.pallas_call(
+        functools.partial(place_kernel, experts, room),
+        grid=(MICRO,),
+        in_specs=[
+            pl.BlockSpec((1, 1, 1, tokens, TOP), lambda i: (0, i, 0, 0, 0)),
+            pl.BlockSpec((count, local_len, width), lambda i: (i, 0, 0)),
+        ],
+        out_specs=[
+            pl.BlockSpec((experts, room, width), lambda i: (0, i, 0)),
+            pl.BlockSpec((1, TOP, tokens), lambda i: (i, 0, 0)),
+            pl.BlockSpec((1, tokens, 8), lambda i: (i, 0, 0)),
+        ],
+        out_shape=[
+            merged,
+            struct((MICRO, TOP, tokens), jnp.int32),
+            struct((MICRO, tokens, 8), jnp.int32),
+        ],
+        compiler_params=params(),
+        cost_estimate=cost(8),
+        name="place",
+    )(after(routes, packed_shard), cotangent)
+
+    def forward(mb):
         cfg = (count, local_len, seq_count, width, experts, room)
         outs = [
             ((experts, room, width), BF),
@@ -602,9 +680,9 @@
                 smem_spec(),
                 smem_spec(),
                 token_spec(mb),
-                pl.BlockSpec((seq_count - 1, count, local_len, width), lambda i: (0, mb, 0, 0)),
+                other_spec(mb),
                 full((width, packed_width)),
-                full((TOP, tokens)),
+                table_spec(mb, (TOP, tokens)),
             ],
             out_specs=[full(s) for s, _ in outs],
             out_shape=[struct(s, k) for s, k in outs],
@@ -613,18 +691,20 @@
                 pltpu.VMEM((local_len, LANES), F32),
             ],
             compiler_params=params(),
+            cost_estimate=cost(11),
             name="forward",
         )(meta, lengths, images, others, packed, prow)
 
-    def expert(buf, dyb, totals):
-        first = totals is None
+    def expert(mb, buf, results, totals):
+        first = mb == 0
+        last = mb == MICRO - 1
         cfg = (experts, room, capacity, width)
         wide = lambda: pl.BlockSpec((width, FF_BLOCK), lambda i: (0, i))
         thin = lambda: pl.BlockSpec((1, FF_BLOCK), lambda i: (0, i))
         in_specs = [
             smem_spec(),
             full((experts, room, width)),
-            full((experts, room, width)),
+            block_spec(mb),
             misc_spec,
             pl.BlockSpec((1, width, FF_BLOCK), lambda i: (0, 0, i)),
             thin(),
@@ -635,22 +715,25 @@
         args = [meta, buf, dyb, packed, up_weight, up_bias, down_weight, down_bias]
         aliases = {}
         if not first:
-            aliases = {len(args) + j: 2 + j for j in range(4)}
-            in_specs += total_specs
-            args += list(totals)
+            aliases = {len(args): 0}
+            aliases.update({len(args) + 1 + j: 2 + j for j in range(4)})
+            in_specs += [any_spec, *total_specs]
+            args += [results, *totals]
         outs = pl.pallas_call(
-            functools.partial(expert_kernel, cfg, first),
+            functools.partial(expert_kernel, cfg, first, last),
             grid=(hidden // FF_BLOCK,),
             in_specs=in_specs,
-            out_specs=[full((experts, room, width))] * 2 + total_specs,
+            out_specs=[block_spec(mb), full((experts, room, width)), *total_specs]
+            + ([early_spec(), late_spec()] * 2 if last else []),
             out_shape=[
-                moved,
+                merged,
                 moved,
                 struct((width, hidden), F32),
                 struct((width, hidden), F32),
                 struct((1, hidden), F32),
                 struct((1, width), F32),
-            ],
+            ]
+            + ([struct((width, hidden // 2), BF)] * 4 if last else []),
             scratch_shapes=[
                 pltpu.VMEM((slots, width), BF),
                 pltpu.VMEM((width, slots), BF),
@@ -661,47 +744,45 @@
             ],
             input_output_aliases=aliases,
             compiler_params=params(),
+            cost_estimate=cost(19),
             name="expert",
         )(*args)
         return outs[0], outs[1], tuple(outs[2:])
 
-    def backward(mb, dback, pcol, saved, totals):
-        first = totals is None
+    def backward(mb, dback, saved, totals):
+        first = mb == 0
+        last = mb == MICRO - 1
         cfg = (count, local_len, seq_count, width, experts, room, capacity)
         middle, gate, second, oT, q, k, v, lse, n1T = saved
-        args = [
-            meta,
-            lengths,
-            dback,
-            pcol,
-            gate,
-            middle,
-            second,
-            cotangent,
-            oT,
-            packed,
-            q,
-            k,
-            v,
-            lse,
-            n1T,
+        whole = [gate, middle, second]
+        heads = [oT, packed, q, k, v, lse, n1T]
+        args = [meta, lengths, dback, pcol, *whole, cotangent, *heads, images, others]
+        in_specs = [
+            smem_spec(),
+            smem_spec(),
+            full(dback.shape),
+            table_spec(mb, (tokens, 8)),
+            *[full(a.shape) for a in whole],
+            token_spec(mb),
+            *[full(a.shape) for a in heads],
+            token_spec(mb),
+            other_spec(mb),
         ]
-        in_specs = [smem_spec(), smem_spec()]
-        in_specs += [token_spec(mb) if a is cotangent else full(a.shape) for a in args[2:]]
         aliases = {}
         if not first:
-            aliases = {len(args) + j: 3 + j for j in range(2)}
             in_specs += [full(a.shape) for a in totals]
             args += list(totals)
+            if not last:
+                aliases = {len(args) - 2: 3, len(args) - 1: 4}
         outs = [
             ((tokens, width), F32),
             ((seq_count - 1, tokens, width), BF),
             ((tokens, width), F32),
-            ((width, 4 * width), F32),
+            ((width, packed_width), BF) if last else ((width, 4 * width), F32),
             ((LANES, width), F32),
         ]
         return pl.pallas_call(
-            functools.partial(backward_kernel, cfg, mb, first),
+            functools.partial(backward_kernel, cfg, mb, first, last),
             grid=(1,),
             in_specs=in_specs,
             out_specs=[full(s) for s, _ in outs],
@@ -713,61 +794,99 @@
             ],
             input_output_aliases=aliases,
             compiler_params=params(),
+            cost_estimate=cost(17),
             name="backward",
         )(*args)
 
-    def finish(mb, own, got, dm, mrow):
+    def into(kernel, mb, args, specs, previous, micros, name):
+        aliases = {}
+        if previous is not None:
+            aliases = {len(args): 0}
+            args = [*args, previous]
+            specs = [*specs, any_spec]
+        return pl.pallas_call(
+            kernel,
+            grid=(1,),
+            in_specs=specs,
+            out_specs=token_spec(mb),
+            out_shape=struct(images.shape, BF),
+            input_output_aliases=aliases,
+            compiler_params=params(),
+            cost_estimate=cost(micros),
+            name=name,
+        )(*args)
+
+    def finish(mb, own, got, dm, previous):
         cfg = (count, local_len, seq_count, width, experts)
-        return pl.pallas_call(
+        specs = [full(own.shape), full(got.shape), token_spec(mb), full(dm.shape), misc_spec]
+        return into(
             functools.partial(input_kernel, cfg),
-            grid=(1,),
-            in_specs=[
-                full((tokens, width)),
-                full((seq_count - 1, tokens, width)),
-                token_spec(mb),
-                full((tokens, width)),
-                misc_spec,
-                full((LANES, width)),
-            ],
-            out_specs=[full((count, local_len, width)), full((LANES, width))],
-            out_shape=[struct((count, local_len, width), BF), struct((LANES, width), F32)],
-            compiler_params=params(),
-            name="finish",
-        )(own, got, images, dm, packed, mrow)
-
-    def mix(back, pcol, gate, middle):
+            mb,
+            [own, got, images, dm, packed],
+            specs,
+            previous,
+            3,
+            "finish",
+        )
+
+    def mix(mb, back, gate, middle, previous):
         cfg = (count, local_len, width, experts, room)
-        args = (back, pcol, gate, middle)
-        return pl.pallas_call(
+        specs = [
+            block_spec(mb),
+            table_spec(mb, (tokens, 8)),
+            full(gate.shape),
+            full(middle.shape),
+        ]
+        return into(
             functools.partial(mix_kernel, cfg),
-            grid=(1,),
-            in_specs=[full(a.shape) for a in args],
-            out_specs=full((count, local_len, width)),
-            out_shape=struct((count, local_len, width), BF),
-            compiler_params=params(),
-            name="mix",
-        )(*args)
-
-    placed = [place(mb) for mb in range(MICRO)]
-    dyb = [exchange(p[0]) for p in placed]
+            mb,
+            [back, pcol, gate, middle],
+            specs,
+            previous,
+            3,
+            "mix",
+        )
+
+    swap = [(i, (i + 1) % seq_count) for i in range(seq_count)]
+
+    def seq_sum(value):
+        if seq_count == 2:
+            return value + lax.ppermute(value.astype(BF), "seq", swap).astype(F32)
+        return lax.psum(value.astype(BF), "seq").astype(F32)
+
+    dyb = exchange(sent_dy)
     saved = []
     bufs = []
     for mb in range(MICRO):
-        outs = forward(mb, placed[mb][1])
+        outs = forward(mb)
         bufs.append(exchange(outs[0]))
         saved.append(outs[1:])
     totals = None
-    results = []
-    dbacks = []
+    results = None
+    ready = []
     for mb in range(MICRO):
-        result, dback, totals = expert(bufs[mb], dyb[mb], totals)
-        results.append(result)
-        dbacks.append(exchange(dback))
+        results, dback, totals = expert(mb, bufs[mb], results, totals)
+        ready.append(dback)
+    gup, gdn, gbias, gdbias, *pieces = totals
+    arrived = []
+    if seq_count == 2:
+        arrived = [lax.ppermute(piece, "seq", swap) for piece in pieces]
     dense = None
-    mrows = []
-    grads = []
+    grads = None
+    owns = []
     for mb in range(MICRO):
-        own, oth, dm, *dense = backward(mb, dbacks[mb], placed[mb][2], saved[mb], dense)
+        sent = ready[mb]
+        if mb == 1:
+            sent = after(sent, ready[MICRO - 1])
+        if mb >= 2:
+            sent = after(sent, owns[mb - 2])
+        dback = exchange(sent)
+        if arrived and mb >= 1:
+            dback, arrived[mb - 1] = lax.optimization_barrier((dback, arrived[mb - 1]))
+        if mb == MICRO - 1:
+            results = after(results, owns[mb - 1])
+        own, oth, dm, *dense = backward(mb, dback, saved[mb], dense)
+        owns.append(own)
         got = jnp.stack(
             [
                 lax.ppermute(
@@ -776,51 +895,43 @@
                 for j in range(1, seq_count)
             ]
         )
-        grad, dense[1] = finish(mb, own, got, dm, dense[1])
-        grads.append(grad)
-    out_blocks = []
+        if arrived and mb == MICRO - 1:
+            got, arrived[2] = lax.optimization_barrier((got, arrived[2]))
+        grads = finish(mb, own, got, dm, grads)
+    shards = lax.psum_scatter(dense[0], "dp", scatter_dimension=0, tiled=True)
+    back = exchange(after(results, dback))
+    out = None
     for mb in range(MICRO):
-        back = exchange(results[mb])
-        out_blocks.append(mix(back, placed[mb][2], saved[mb][1], saved[mb][0]))
-
-    gup, gdn, gbias, gdbias = totals
-    swap = [(i, (i + 1) % seq_count) for i in range(seq_count)]
-
-    def seq_sum(value):
-        if seq_count == 2:
-            return value + lax.ppermute(value.astype(BF), "seq", swap).astype(F32)
-        return lax.psum(value.astype(BF), "seq").astype(F32)
+        out = mix(mb, back, saved[mb][1], saved[mb][0], out)
 
     if seq_count == 2:
-        got_up = lax.ppermute(gup.astype(BF), "seq", swap)
-        got_dn = lax.ppermute(gdn.astype(BF), "seq", swap)
         wide = lambda: pl.BlockSpec((width, FF_BLOCK), lambda i: (0, i))
         final_up, final_down = pl.pallas_call(
             sum_kernel,
             grid=(hidden // FF_BLOCK,),
-            in_specs=[wide(), wide(), wide(), wide()],
+            in_specs=[wide(), wide(), *[early_spec(), late_spec()] * 2],
             out_specs=[
                 pl.BlockSpec((1, width, FF_BLOCK), lambda i: (0, 0, i)),
                 pl.BlockSpec((1, FF_BLOCK, width), lambda i: (0, i, 0)),
             ],
             out_shape=[struct((1, width, hidden), F32), struct((1, hidden, width), F32)],
             compiler_params=params(),
+            cost_estimate=cost(8),
             name="sum_experts",
-        )(gup, gdn, got_up, got_dn)
+        )(gup, gdn, *arrived)
     else:
-        final_up = seq_sum(gup)[None]
-        final_down = jnp.swapaxes(seq_sum(gdn), 0, 1)[None]
+        sums = [lax.psum(piece, "seq").astype(F32) for piece in pieces]
+        final_up = jnp.concatenate(sums[:2], axis=1)[None]
+        final_down = jnp.swapaxes(jnp.concatenate(sums[2:], axis=1), 0, 1)[None]
     biases = seq_sum(jnp.concatenate([gbias, gdbias], axis=1))
     final_up_shift = biases[:, :hidden]
     final_down_shift = biases[:, hidden:]
 
-    grand = jnp.concatenate([dense[0], jnp.transpose(dense[1])], axis=1).astype(BF)
-    shards = lax.psum_scatter(grand, "dp", scatter_dimension=0, tiled=True)
     shards = seq_sum(shards.astype(F32))
     misc = 4 * width + experts
     return (
-        jnp.concatenate(out_blocks, axis=0),
-        jnp.concatenate(grads, axis=0),
+        out,
+        grads,
         shards[:, misc],
         shards[:, misc + 1],
         shards[:, : 3 * width],

time: 531 us -> 403 us (0.76)
  waiting for transfers between devices: 188 us -> 127 us
  blocking collectives: 28.6 us -> 0 us
  starting transfers between devices: 81.1 us -> 64.7 us
  other arithmetic: 13.7 us -> 1.21 us
  local copies, waits for them, and re-layouts: 18.7 us -> 12.3 us
    ppermute x2, waiting for transfers between devices: 71.2 us -> 2.01 us  [seq_sum(): return value + lax.ppermute(value.astype(BF), 'seq', swap).astype(F32)]
    all_to_all x11 -> x8, waiting for transfers between devices: 73 us -> 5.94 us  [exchange(): return lax.all_to_all(array, 'dp', split_axis=0, concat_axis=0, tiled=True)]
    ppermute x3, waiting for transfers between devices: 21.4 us -> 57 us  [on_device(): lax.ppermute(oth[j - 1], 'seq', [(i, (i + j) % seq_count) for i in range(...]
    all_gather x1, waiting for transfers between devices: 0.01 us -> 33.7 us  [on_device(): packed = lax.all_gather(packed_shard, 'dp', axis=0, tiled=True)]
    all_to_all x1 -> x0, blocking collectives: 28.6 us -> none  [exchange(): return lax.all_to_all(array, 'dp', split_axis=0, concat_axis=0, tiled=True)]
    all_to_all x11 -> x8, starting transfers between devices: 69.7 us -> 52.9 us  [exchange(): return lax.all_to_all(array, 'dp', split_axis=0, concat_axis=0, tiled=True)]
    ppermute x2 -> x4, waiting for transfers between devices: 0.01 us -> 6.56 us  [on_device(): arrived = [lax.ppermute(piece, 'seq', swap) for piece in pieces]]
    pallas_call x15 -> x14, Pallas kernels: 136 us -> 136 us  [the longest x3 58.8 us: expert(): pl.pallas_call(functools.partial(expert_kernel, cfg, first, last), grid=(...]
  transfers between devices with their start and end apart: 21 -> 20, of which waited for: 13 -> 9; matrix products, arithmetic and copies ran while one was open for 4% -> 2% of each run, Pallas kernels for 33% -> 42%
where the time goes in v2:
time: 403 us; the launch traced here: 398 us
  Pallas kernels  177 us (44%)
  waiting for transfers between devices  127 us (32%)
  starting transfers between devices  64.7 us (16%)
  between operations  14.8 us (4%)
  local copies, waits for them, and re-layouts  12.3 us (3%)
    pallas_call x3, Pallas kernels, expert(): pl.pallas_call(functools.partial(expert_kernel, cfg, first, last), grid=(...  58.8 us
    ppermute x3, waiting for transfers between devices, on_device(): lax.ppermute(oth[j - 1], 'seq', [(i, (i + j) % seq_count) for i in range(...  57 us
    all_to_all x8, starting transfers between devices, exchange(): return lax.all_to_all(array, 'dp', split_axis=0, concat_axis=0, tiled=True)  52.9 us
    pallas_call x3, Pallas kernels, backward(): pl.pallas_call(functools.partial(backward_kernel, cfg, mb, first, last),...  51.9 us
    all_gather x1, waiting for transfers between devices, on_device(): packed = lax.all_gather(packed_shard, 'dp', axis=0, tiled=True)  33.7 us
    pallas_call x3, Pallas kernels, forward(): pl.pallas_call(functools.partial(forward_kernel, cfg, mb), grid=(1,), in_...  33.1 us
    ppermute x1, waiting for transfers between devices, on_device(): lax.ppermute(images, 'seq', [((i + j) % seq_count, i) for i in range(seq_...  22.2 us
    pallas_call x6, Pallas kernels, into(): pl.pallas_call(kernel, grid=(1,), in_specs=specs, out_specs=token_spec(mb...  17.4 us
  transfers between devices with their start and end apart: 20, of which 9 were waited for; matrix products, arithmetic and copies ran while one was open for 2% of the time, Pallas kernels for 42%

profile of v2, /device:TPU:0, one launch (start us, length us, event | category | flops | bytes accessed | tf_op | source)
XLA Modules:
  0.0 397.8 jit_solution(14548763126176531469)
XLA Ops:
  7.2 0.0 all-gather.2.cloned.1.call-start
  7.2 1.4 copy.51.router_ref
  8.6 1.3 concatenate.14.vec_ref
  9.9 1.7 pack.1
  11.6 0.0 all-gather.2.cloned.1.call-update
  11.7 1.7 copy.52.routes_ref
  13.4 6.1 %place.1 = (bf16[16,168,512]{2,1,0:T(8,128)(2,1)}, s32[3,2,320]{2,1,0:T(2,128)}, s32[3,320,8]{2,1,0:T(8,128)}) custom-call(s32[1,3,1,320,2]{4,3,2,1,0:T(8,128)} %copy.52.routes_ref, bf16[3,320,512]{2,1,0:T(8,128)(2,1)} %refs_7_.11), custom_call_target="tpu_custom_call" | custom-call | flops 8000000000 | bytes 16000000 | tf_op jit(solution)/shard_map/place/pallas_call | solution.py:640
  19.4 7.4 %all-to-all-start.1 = ((bf16[16,168,512]{2,1,0:T(8,128)(2,1)}), bf16[16,168,512]{2,1,0:T(8,128)(2,1)S(1)}, u32[]{:S(2)}, u32[]{:S(2)}) async-start(bf16[16,168,512]{2,1,0:T(8,128)(2,1)} %get-tuple-element.100), calls=%async_computation.1 | async-start | bytes 5505024 | tf_op jit(solution)/shard_map/all_to_all | solution.py:638
  26.8 1.6 collective-permute-start
  28.4 0.6 pad_add_fusion.meta_ref.refs_0_
  29.0 22.2 %collective-permute-done = bf16[3,320,512]{2,1,0:T(8,128)(2,1)} collective-permute-done((bf16[3,320,512]{2,1,0:T(8,128)(2,1)}, bf16[3,320,512]{2,1,0:T(8,128)(2,1)}, u32[]{:S(2)}, u32[]{:S(2)}) %collective-permute-start) | collective-permute-done | bytes 983072 | tf_op jit(solution)/shard_map/ppermute | solution.py:609
  51.2 33.7 %all-gather.2.cloned.1.call-done.w_ref.refs_3_.refs_9_.wm_ref = bf16[512,2176]{1,0:T(8,128)(2,1)} async-done(((bf16[32,2176]{1,0:T(8,128)(2,1)}), bf16[512,2176]{1,0:T(8,128)(2,1)}) %all-gather.2.cloned.1.call-update) | async-done | bytes 2228240 | tf_op jit(solution)/shard_map/all_gather | solution.py:635
  84.9 11.0 %forward.5 = (bf16[16,56,512]{2,1,0:T(8,128)(2,1)}, f32[320,512]{1,0:T(8,128)}, f32[320,128]{1,0:T(8,128)}, bf16[320,512]{1,0:T(8,128)(2,1)}, bf16[512,320]{1,0:...) custom-call(s32[2]{0:T(128)} %pad_add_fusion.meta_ref.refs_0_, ...), custom_call_target="tpu_custom_call" | custom-call | flops 11000000512 | bytes 22000000 | tf_op jit(solution)/shard_map/forward/pallas_call | solution.py:676
  96.0 9.0 %all-to-all-start.3 = ((bf16[16,56,512]{2,1,0:T(8,128)(2,1)}), bf16[16,56,512]{2,1,0:T(8,128)(2,1)}, u32[]{:S(2)}, u32[]{:S(2)}) async-start(bf16[16,56,512]{2,1,0:T(8,128)(2,1)} %get-tuple-element.102), calls=%async_computation.3 | async-start | bytes 1835008 | tf_op jit(solution)/shard_map/all_to_all | solution.py:638
  104.9 11.0 %forward.4 = (bf16[16,56,512]{2,1,0:T(8,128)(2,1)}, f32[320,512]{1,0:T(8,128)}, f32[320,128]{1,0:T(8,128)}, bf16[320,512]{1,0:T(8,128)(2,1)}, bf16[512,320]{1,0:...) custom-call(s32[2]{0:T(128)} %pad_add_fusion.meta_ref.refs_0_, ...), custom_call_target="tpu_custom_call" | custom-call | flops 11000000512 | bytes 22000000 | tf_op jit(solution)/shard_map/forward/pallas_call | solution.py:676
  116.0 11.0 %forward.3 = (bf16[16,56,512]{2,1,0:T(8,128)(2,1)}, f32[320,512]{1,0:T(8,128)}, f32[320,128]{1,0:T(8,128)}, bf16[320,512]{1,0:T(8,128)(2,1)}, bf16[512,320]{1,0:...) custom-call(s32[2]{0:T(128)} %pad_add_fusion.meta_ref.refs_0_, ...), custom_call_target="tpu_custom_call" | custom-call | flops 11000000512 | bytes 22000000 | tf_op jit(solution)/shard_map/forward/pallas_call | solution.py:676
  127.0 6.1 %all-to-all-start.2 = ((bf16[16,56,512]{2,1,0:T(8,128)(2,1)}), bf16[16,56,512]{2,1,0:T(8,128)(2,1)S(1)}, u32[]{:S(2)}, u32[]{:S(2)}) async-start(bf16[16,56,512]{2,1,0:T(8,128)(2,1)} %get-tuple-element.101), calls=%async_computation.2 | async-start | bytes 1835008 | tf_op jit(solution)/shard_map/all_to_all | solution.py:638
  133.1 18.7 %expert.3 = (bf16[16,168,512]{2,1,0:T(8,128)(2,1)}, bf16[16,56,512]{2,1,0:T(8,128)(2,1)}, f32[512,2048]{1,0:T(8,128)}, f32[512,2048]{1,0:T(8,128)}, f32[1,2048]{1,0:T(1,128)}, /*index=5*/f32[1,512]{1,0:T(1,128)}) custom-call(s32[2]{0:T(128)} %pad_add_fusion.meta_ref.refs_0_, bf16[16,56,512]{2,1,0:T(8,128)(2,1)} %all-to-all-done.3.refs_1_, ...), custom_call_target="tpu_custom_call" | custom-call | flops 19000000512 | bytes 38000000 | tf_op jit(solution)/shard_map/expert/pallas_call | solution.py:722
  151.8 2.1 all-to-all-done.2.refs_1_
  153.9 6.3 %all-to-all-start = ((bf16[16,56,512]{2,1,0:T(8,128)(2,1)}), bf16[16,56,512]{2,1,0:T(8,128)(2,1)S(1)}, u32[]{:S(2)}, u32[]{:S(2)}) async-start(bf16[16,56,512]{2,1,0:T(8,128)(2,1)} %get-tuple-element.99), calls=%async_computation | async-start | bytes 1835008 | tf_op jit(solution)/shard_map/all_to_all | solution.py:638
  160.2 19.4 %expert.4 = (bf16[16,168,512]{2,1,0:T(8,128)(2,1)}, bf16[16,56,512]{2,1,0:T(8,128)(2,1)}, f32[512,2048]{1,0:T(8,128)}, f32[512,2048]{1,0:T(8,128)}, f32[1,2048]{1,0:T(1,128)}, /*index=5*/f32[1,512]{1,0:T(1,128)}) custom-call(s32[2]{0:T(128)} %pad_add_fusion.meta_ref.refs_0_, ...), custom_call_target="tpu_custom_call", output_to_operand_aliasing={{0}: (8, {}), {2}: (9, {}), {3}: (10, {}), {4}: (11, {}), {... | custom-call | flops 19000000512 | bytes 38000000 | tf_op jit(solution)/shard_map/expert/pallas_call | solution.py:722
  179.6 1.4 all-to-all-done.refs_1_
  180.9 6.1 %all-to-all-start.5 = ((bf16[16,56,512]{2,1,0:T(8,128)(2,1)}), bf16[16,56,512]{2,1,0:T(8,128)(2,1)S(1)}, u32[]{:S(2)}, u32[]{:S(2)}) async-start(bf16[16,56,512]{2,1,0:T(8,128)(2,1)} %get-tuple-element.129), calls=%async_computation.5 | async-start | bytes 1835008 | tf_op jit(solution)/shard_map/all_to_all | solution.py:638
  187.0 20.7 %expert.5 = (bf16[16,168,512]{2,1,0:T(8,128)(2,1)}, bf16[16,56,512]{2,1,0:T(8,128)(2,1)}, f32[512,2048]{1,0:T(8,128)}, f32[512,2048]{1,0:T(8,128)}, f32[1,2048]{...) custom-call(s32[2]{0:T(128)} %pad_add_fusion.meta_ref.refs_0_, ...), custom_call_target="tpu_custom_call", output_to_operand_aliasing={{0}: (8, {}), {2}: (9, {}), {3}: (10, {}), {4}: (11, {}), {... | custom-call | flops 19000000512 | bytes 38000000 | tf_op jit(solution)/shard_map/expert/pallas_call | solution.py:722
  207.7 0.1 all-to-all-done.5.refs_2_
  207.8 6.3 %all-to-all-start.4 = ((bf16[16,56,512]{2,1,0:T(8,128)(2,1)}), bf16[16,56,512]{2,1,0:T(8,128)(2,1)S(1)}, u32[]{:S(2)}, u32[]{:S(2)}) async-start(bf16[16,56,512]{2,1,0:T(8,128)(2,1)} %get-tuple-element.116), calls=%async_computation.4 | async-start | bytes 1835008 | tf_op jit(solution)/shard_map/all_to_all | solution.py:638
  214.1 1.6 collective-permute-start.1
  215.7 16.8 %backward.3 = (f32[320,512]{1,0:T(8,128)}, bf16[1,320,512]{2,1,0:T(8,128)(2,1)}, f32[320,512]{1,0:T(8,128)}, f32[512,2048]{1,0:T(8,128)}, f32[128,512]{1,0:T(8,128)}) custom-call(s32[2]{0:T(128)} %pad_add_fusion.meta_ref.refs_0_, s32[3]{0:T(128)} %refs_1_.5, bf16[16,56,512]{2,1,0:T(8,128)(2,1)} %copy-done.4, ...), custom_call_target="tpu_custom_call" | custom-call | flops 16999999488 | bytes 34000000 | tf_op jit(solution)/shard_map/backward/pallas_call | solution.py:784
  232.5 2.4 all-to-all-done.4.refs_2_
  234.9 6.1 %all-to-all-start.6 = ((bf16[16,56,512]{2,1,0:T(8,128)(2,1)}), bf16[16,56,512]{2,1,0:T(8,128)(2,1)S(1)}, u32[]{:S(2)}, u32[]{:S(2)}) async-start(bf16[16,56,512]{2,1,0:T(8,128)(2,1)} %get-tuple-element.144), calls=%async_computation.6 | async-start | bytes 1835008 | tf_op jit(solution)/shard_map/all_to_all | solution.py:638
  241.0 1.6 collective-permute-start.2
  242.6 17.6 %backward.4 = (f32[320,512]{1,0:T(8,128)}, bf16[1,320,512]{2,1,0:T(8,128)(2,1)}, f32[320,512]{1,0:T(8,128)}, f32[512,2048]{1,0:T(8,128)}, f32[128,512]{1,0:T(8,128)}) custom-call(s32[2]{0:T(128)} %pad_add_fusion.meta_ref.refs_0_, s32[3]{0:T(128)} %refs_1_.5, bf16[16,56,512]{2,1,0:T(8,128)(2,1)} %copy-done.3, ...), custom_call_target="tpu_custom_call", output_to_operand_aliasing={{3}: (17, {}), {4}: (18, {})} | custom-call | flops 16999999488 | bytes 34000000 | tf_op jit(solution)/shard_map/backward/pallas_call | solution.py:784
  260.2 6.6 %collective-permute-done.2.up_late = bf16[512,1024]{1,0:T(8,128)(2,1)} collective-permute-done((bf16[512,1024]{1,0:T(8,128)(2,1)}, bf16[512,1024]{1,0:T(8,128)(2,1)}, u32[]{:S(2)}, u32[]{:S(2)}) %collective-permute-start.2) | collective-permute-done | bytes 1048608 | tf_op jit(solution)/shard_map/ppermute | solution.py:873
  266.8 0.9 copy-done.2
  267.7 5.7 %all-to-all-start.7 = ((bf16[16,168,512]{2,1,0:T(8,128)(2,1)}), bf16[16,168,512]{2,1,0:T(8,128)(2,1)S(1)}, u32[]{:S(2)}, u32[]{:S(2)}) async-start(bf16[16,168,512]{2,1,0:T(8,128)(2,1)} %get-tuple-element.147), calls=%async_computation.7 | async-start | bytes 5505024 | tf_op jit(solution)/shard_map/all_to_all | solution.py:638
  273.4 0.3 reduce-scatter.2.cloned.1.call-start
  273.8 17.5 %backward.5 = (f32[320,512]{1,0:T(8,128)}, bf16[1,320,512]{2,1,0:T(8,128)(2,1)}, f32[320,512]{1,0:T(8,128)}, bf16[512,2176]{1,0:T(8,128)(2,1)}, f32[128,512]{1,0:T(8,128)}) custom-call(s32[2]{0:T(128)} %pad_add_fusion.meta_ref.refs_0_, s32[3]{0:T(128)} %refs_1_.5, bf16[16,56,512]{2,1,0:T(8,128)(2,1)} %copy-done.2, ...), custom_call_target="tpu_custom_call" | custom-call | flops 16999999488 | bytes 34000000 | tf_op jit(solution)/shard_map/backward/pallas_call | solution.py:784
  291.3 0.0 reduce-scatter.2.cloned.1.call-update
  291.4 1.6 collective-permute-start.9
  292.9 0.5 collective-permute-start.4
  293.4 1.5 collective-permute-start.8
  295.0 0.5 collective-permute-start.5
  295.5 1.5 collective-permute-start.6
  297.0 0.6 slice.59
  297.6 0.6 slice.58
  298.2 0.5 collective-permute-start.3
  298.7 57.0 %collective-permute-done.6 = bf16[320,512]{1,0:T(8,128)(2,1)S(1)} collective-permute-done((bf16[320,512]{1,0:T(8,128)(2,1)S(1)}, bf16[320,512]{1,0:T(8,128)(2,1)S(1)}, u32[]{:S(2)}, u32[]{:S(2)}) %collective-permute-start.6) | collective-permute-done | bytes 327712 | tf_op jit(solution)/shard_map/ppermute | solution.py:892
  355.7 0.7 copy-done.14
  356.4 2.7 finish.3.refs_0_
  359.1 0.7 copy-done.13
  359.9 2.7 finish.4.refs_0_
  362.6 8.4 %sum_experts.1 = (f32[1,512,2048]{2,1,0:T(8,128)}, f32[1,2048,512]{2,1,0:T(8,128)}) custom-call(f32[512,2048]{1,0:T(8,128)} %get-tuple-element.169.gup_ref, f32[512,2048]{1,0:T(8,128)} %get-tuple-element.170.gdn_ref, bf16[512,1024]{1,0:T(8,128)(2,1)} %copy-done.10, bf16[512,1024]{1,0:T(8,128)(2,1)} %collective-permute-done.2.up_late, ...), custom_call_target="tpu_custom_call" | custom-call | flops 8000000000 | bytes 16000000 | tf_op jit(solution)/shard_map/sum_experts/pallas_call | solution.py:909
  371.0 0.6 collective-permute-start.7
  371.6 2.7 finish.5
  374.3 2.0 collective-permute-done.7
  376.4 0.6 slice.53
  377.0 0.7 slice.50
  377.7 0.7 copy.53
  378.4 0.8 slice_reduce_fusion
  379.1 0.6 pad_maximum_fusion
  379.7 1.6 copy-done
  381.3 3.1 mix.3.refs_0_
  384.3 3.1 mix.4.refs_0_
  387.4 3.1 mix.5
  (44 shorter events, 0.2 us)
Async XLA Ops:
  7.2 77.7 %all-gather.2.cloned.1.call-start = ((), (), s32[]{:S(2)}) async-start(), calls=%async_computation.9 | async-start | bytes 2367488 | tf_op jit(solution)/shard_map/all_gather | solution.py:635
  19.4 76.5 %all-to-all-start.1 = ((bf16[16,168,512]{2,1,0:T(8,128)(2,1)}), bf16[16,168,512]{2,1,0:T(8,128)(2,1)S(1)}, u32[]{:S(2)}, u32[]{:S(2)}) async-start(bf16[16,168,512]{2,1,0:T(8,128)(2,1)} %get-tuple-element.100), calls=%async_computation.1 | async-start | bytes 5505024 | tf_op jit(solution)/shard_map/all_to_all | solution.py:638
  26.8 24.4 %collective-permute-start = (bf16[3,320,512]{2,1,0:T(8,128)(2,1)}, bf16[3,320,512]{2,1,0:T(8,128)(2,1)}, u32[]{:S(2)}, u32[]{:S(2)}) collective-permute-start(bf16[3,320,512]{2,1,0:T(8,128)(2,1)} %x_ref.5), channel_id=1, source_target_pairs={{1,0},{0,1},{3,2},{2,3},{5,4},{4,5},{7,6},{6,7},{9,8},{8,9},{11,10... | collective-permute-start | bytes 2949128 | tf_op jit(solution)/shard_map/ppermute | solution.py:609
  95.9 20.0 %copy-start.1 = (bf16[16,168,512]{2,1,0:T(8,128)(2,1)}, bf16[16,168,512]{2,1,0:T(8,128)(2,1)S(1)}, u32[]{:S(2)}) copy-start(bf16[16,168,512]{2,1,0:T(8,128)(2,1)S(1)} %all-to-all-done.1.refs_2_) | copy-start | bytes 8257540
  96.0 31.1 %all-to-all-start.3 = ((bf16[16,56,512]{2,1,0:T(8,128)(2,1)}), bf16[16,56,512]{2,1,0:T(8,128)(2,1)}, u32[]{:S(2)}, u32[]{:S(2)}) async-start(bf16[16,56,512]{2,1,0:T(8,128)(2,1)} %get-tuple-element.102), calls=%async_computation.3 | async-start | bytes 1835008 | tf_op jit(solution)/shard_map/all_to_all | solution.py:638
  127.0 26.9 %all-to-all-start.2 = ((bf16[16,56,512]{2,1,0:T(8,128)(2,1)}), bf16[16,56,512]{2,1,0:T(8,128)(2,1)S(1)}, u32[]{:S(2)}, u32[]{:S(2)}) async-start(bf16[16,56,512]{2,1,0:T(8,128)(2,1)} %get-tuple-element.101), calls=%async_computation.2 | async-start | bytes 1835008 | tf_op jit(solution)/shard_map/all_to_all | solution.py:638
  153.9 6.3 %copy-start.6 = (bf16[16,56,512]{2,1,0:T(8,128)(2,1)}, bf16[16,56,512]{2,1,0:T(8,128)(2,1)S(1)}, u32[]{:S(2)}) copy-start(bf16[16,56,512]{2,1,0:T(8,128)(2,1)S(1)} %all-to-all-done.2.refs_1_) | copy-start | bytes 2752516
  153.9 27.0 %all-to-all-start = ((bf16[16,56,512]{2,1,0:T(8,128)(2,1)}), bf16[16,56,512]{2,1,0:T(8,128)(2,1)S(1)}, u32[]{:S(2)}, u32[]{:S(2)}) async-start(bf16[16,56,512]{2,1,0:T(8,128)(2,1)} %get-tuple-element.99), calls=%async_computation | async-start | bytes 1835008 | tf_op jit(solution)/shard_map/all_to_all | solution.py:638
  180.9 6.1 %copy-start.5 = (bf16[16,56,512]{2,1,0:T(8,128)(2,1)}, bf16[16,56,512]{2,1,0:T(8,128)(2,1)S(1)}, u32[]{:S(2)}) copy-start(bf16[16,56,512]{2,1,0:T(8,128)(2,1)S(1)} %all-to-all-done.refs_1_) | copy-start | bytes 2752516
  180.9 26.9 %all-to-all-start.5 = ((bf16[16,56,512]{2,1,0:T(8,128)(2,1)}), bf16[16,56,512]{2,1,0:T(8,128)(2,1)S(1)}, u32[]{:S(2)}, u32[]{:S(2)}) async-start(bf16[16,56,512]{2,1,0:T(8,128)(2,1)} %get-tuple-element.129), calls=%async_computation.5 | async-start | bytes 1835008 | tf_op jit(solution)/shard_map/all_to_all | solution.py:638
  207.8 7.9 %copy-start.4 = (bf16[16,56,512]{2,1,0:T(8,128)(2,1)}, bf16[16,56,512]{2,1,0:T(8,128)(2,1)S(1)}, u32[]{:S(2)}) copy-start(bf16[16,56,512]{2,1,0:T(8,128)(2,1)S(1)} %all-to-all-done.5.refs_2_) | copy-start | bytes 2752516
  207.8 27.1 %all-to-all-start.4 = ((bf16[16,56,512]{2,1,0:T(8,128)(2,1)}), bf16[16,56,512]{2,1,0:T(8,128)(2,1)S(1)}, u32[]{:S(2)}, u32[]{:S(2)}) async-start(bf16[16,56,512]{2,1,0:T(8,128)(2,1)} %get-tuple-element.116), calls=%async_computation.4 | async-start | bytes 1835008 | tf_op jit(solution)/shard_map/all_to_all | solution.py:638
  214.1 28.4 %collective-permute-start.1 = (bf16[512,1024]{1,0:T(8,128)(2,1)}, bf16[512,1024]{1,0:T(8,128)(2,1)S(1)}, u32[]{:S(2)}, u32[]{:S(2)}) collective-permute-start(bf16[512,1024]{1,0:T(8,128)(2,1)} %get-tuple-element.117), channel_id=1, source_target_pairs={{0,1},{1,0},{2,3},{3,2},{4,5},{5,4},{6,7},{7,6},{8,9},{9,8},{10,11... | collective-permute-start | bytes 3145736 | tf_op jit(solution)/shard_map/ppermute | solution.py:873
  234.9 7.7 %copy-start.3 = (bf16[16,56,512]{2,1,0:T(8,128)(2,1)}, bf16[16,56,512]{2,1,0:T(8,128)(2,1)S(1)}, u32[]{:S(2)}) copy-start(bf16[16,56,512]{2,1,0:T(8,128)(2,1)S(1)} %all-to-all-done.4.refs_2_) | copy-start | bytes 2752516
  234.9 31.9 %all-to-all-start.6 = ((bf16[16,56,512]{2,1,0:T(8,128)(2,1)}), bf16[16,56,512]{2,1,0:T(8,128)(2,1)S(1)}, u32[]{:S(2)}, u32[]{:S(2)}) async-start(bf16[16,56,512]{2,1,0:T(8,128)(2,1)} %get-tuple-element.144), calls=%async_computation.6 | async-start | bytes 1835008 | tf_op jit(solution)/shard_map/all_to_all | solution.py:638
  241.0 25.8 %collective-permute-start.2 = (bf16[512,1024]{1,0:T(8,128)(2,1)}, bf16[512,1024]{1,0:T(8,128)(2,1)}, u32[]{:S(2)}, u32[]{:S(2)}) collective-permute-start(bf16[512,1024]{1,0:T(8,128)(2,1)} %get-tuple-element.145), channel_id=1, source_target_pairs={{0,1},{1,0},{2,3},{3,2},{4,5},{5,4},{6,7},{7,6},{8,9},{9,8},{10,11... | collective-permute-start | bytes 3145736 | tf_op jit(solution)/shard_map/ppermute | solution.py:873
  242.6 17.6 %copy-start.10 = (bf16[512,1024]{1,0:T(8,128)(2,1)}, bf16[512,1024]{1,0:T(8,128)(2,1)S(1)}, u32[]{:S(2)}) copy-start(bf16[512,1024]{1,0:T(8,128)(2,1)S(1)} %collective-permute-done.1.up_early) | copy-start | bytes 3145732
  266.8 0.9 copy-start.2
  267.7 112.0 %all-to-all-start.7 = ((bf16[16,168,512]{2,1,0:T(8,128)(2,1)}), bf16[16,168,512]{2,1,0:T(8,128)(2,1)S(1)}, u32[]{:S(2)}, u32[]{:S(2)}) async-start(bf16[16,168,512]{2,1,0:T(8,128)(2,1)} %get-tuple-element.147), calls=%async_computation.7 | async-start | bytes 5505024 | tf_op jit(solution)/shard_map/all_to_all | solution.py:638
  273.4 97.6 %reduce-scatter.2.cloned.1.call-start = ((), (), s32[]{:S(2)}) async-start(), calls=%async_computation.10 | async-start | bytes 2367488 | tf_op jit(solution)/shard_map/reduce_scatter | solution.py:901
  273.7 17.6 %copy-start.8 = (f32[1,2048]{1,0:T(1,128)S(1)}, f32[1,2048]{1,0:T(1,128)}, u32[]{:S(2)}) copy-start(f32[1,2048]{1,0:T(1,128)} %get-tuple-element.176) | copy-start | bytes 24580
  273.7 17.6 %copy-start.9 = (f32[1,512]{1,0:T(1,128)S(1)}, f32[1,512]{1,0:T(1,128)}, u32[]{:S(2)}) copy-start(f32[1,512]{1,0:T(1,128)} %get-tuple-element.177) | copy-start | bytes 6148
  273.7 21.2 %copy-start.12 = (bf16[1,320,512]{2,1,0:T(8,128)(2,1)S(1)}, bf16[1,320,512]{2,1,0:T(8,128)(2,1)}, u32[]{:S(2)}) copy-start(bf16[1,320,512]{2,1,0:T(8,128)(2,1)} %get-tuple-element.164) | copy-start | bytes 983044
  273.7 21.7 %copy-start.11 = (bf16[1,320,512]{2,1,0:T(8,128)(2,1)S(1)}, bf16[1,320,512]{2,1,0:T(8,128)(2,1)}, u32[]{:S(2)}) copy-start(bf16[1,320,512]{2,1,0:T(8,128)(2,1)} %get-tuple-element.166) | copy-start | bytes 983044
  291.4 5.6 %collective-permute-start.9 = (bf16[1,2560]{1,0:T(2,128)(2,1)S(1)}, bf16[1,2560]{1,0:T(2,128)(2,1)S(1)}, u32[]{:S(2)}, u32[]{:S(2)}) collective-permute-start(bf16[1,2560]{1,0:T(2,128)(2,1)S(1)} %convert_element_type.23), channel_id=1, source_target_pairs={{0,1},{1,0},{2,3},{3,2},{4,5},{5,4},{6,7},{7,6},{8,9},{9,8},{10,11... | collective-permute-start | bytes 15368 | tf_op jit(solution)/shard_map/ppermute | solution.py:854
  292.9 69.6 %collective-permute-start.4 = (bf16[512,1024]{1,0:T(8,128)(2,1)}, bf16[512,1024]{1,0:T(8,128)(2,1)}, u32[]{:S(2)}, u32[]{:S(2)}) collective-permute-start(bf16[512,1024]{1,0:T(8,128)(2,1)} %get-tuple-element.161), channel_id=1, source_target_pairs={{0,1},{1,0},{2,3},{3,2},{4,5},{5,4},{6,7},{7,6},{8,9},{9,8},{10,11... | collective-permute-start | bytes 3145736 | tf_op jit(solution)/shard_map/ppermute | solution.py:873
  293.4 69.1 %collective-permute-start.8 = (bf16[512,1024]{1,0:T(8,128)(2,1)}, bf16[512,1024]{1,0:T(8,128)(2,1)}, u32[]{:S(2)}, u32[]{:S(2)}) collective-permute-start(bf16[512,1024]{1,0:T(8,128)(2,1)} %get-tuple-element.174), channel_id=1, source_target_pairs={{0,1},{1,0},{2,3},{3,2},{4,5},{5,4},{6,7},{7,6},{8,9},{9,8},{10,11... | collective-permute-start | bytes 3145736 | tf_op jit(solution)/shard_map/ppermute | solution.py:873
  295.0 64.2 %collective-permute-start.5 = (bf16[320,512]{1,0:T(8,128)(2,1)S(1)}, bf16[320,512]{1,0:T(8,128)(2,1)S(1)}, u32[]{:S(2)}, u32[]{:S(2)}) collective-permute-start(bf16[320,512]{1,0:T(8,128)(2,1)S(1)} %bitcast.24), channel_id=1, source_target_pairs={{0,1},{1,0},{2,3},{3,2},{4,5},{5,4},{6,7},{7,6},{8,9},{9,8},{10,11... | collective-permute-start | bytes 983048 | tf_op jit(solution)/shard_map/ppermute | solution.py:892
  295.5 60.2 %collective-permute-start.6 = (bf16[320,512]{1,0:T(8,128)(2,1)S(1)}, bf16[320,512]{1,0:T(8,128)(2,1)S(1)}, u32[]{:S(2)}, u32[]{:S(2)}) collective-permute-start(bf16[320,512]{1,0:T(8,128)(2,1)S(1)} %bitcast.23), channel_id=1, source_target_pairs={{0,1},{1,0},{2,3},{3,2},{4,5},{5,4},{6,7},{7,6},{8,9},{9,8},{10,11... | collective-permute-start | bytes 983048 | tf_op jit(solution)/shard_map/ppermute | solution.py:892
  298.2 64.4 %collective-permute-start.3 = (bf16[320,512]{1,0:T(8,128)(2,1)}, bf16[320,512]{1,0:T(8,128)(2,1)}, u32[]{:S(2)}, u32[]{:S(2)}) collective-permute-start(bf16[320,512]{1,0:T(8,128)(2,1)} %bitcast.25), channel_id=1, source_target_pairs={{0,1},{1,0},{2,3},{3,2},{4,5},{5,4},{6,7},{7,6},{8,9},{9,8},{10,11... | collective-permute-start | bytes 983048 | tf_op jit(solution)/shard_map/ppermute | solution.py:892
  355.7 0.7 copy-start.14
  359.1 0.7 copy-start.13
  371.0 5.3 %collective-permute-start.7 = (bf16[32,2176]{1,0:T(8,128)(2,1)}, bf16[32,2176]{1,0:T(8,128)(2,1)S(1)}, u32[]{:S(2)}, u32[]{:S(2)}) collective-permute-start(bf16[32,2176]{1,0:T(8,128)(2,1)} %reduce-scatter.2.cloned.1.call-done), channel_id=1, source_target_pairs={{0,1},{1,0},{2,3},{3,2},{4,5},{5,4},{6,7},{7,6},{8,9},{9,8},{10,11... | collective-permute-start | bytes 417800 | tf_op jit(solution)/shard_map/ppermute | solution.py:854
  371.6 4.8 %copy-start.7 = (bf16[32,2176]{1,0:T(8,128)(2,1)S(1)}, bf16[32,2176]{1,0:T(8,128)(2,1)}, u32[]{:S(2)}) copy-start(bf16[32,2176]{1,0:T(8,128)(2,1)} %reduce-scatter.2.cloned.1.call-done) | copy-start | bytes 417796
  379.7 1.6 copy-start
Sparse Core Ops, SparseCore 0:
  11.8 73.0 all-gather.1
  291.4 69.2 reduce-scatter.1

commit v3 on v2

--- a/solution.py
+++ b/solution.py
@@ -57,21 +57,28 @@
     shard = proj_ref.shape[0]
     out_ref[:, : 3 * width] = qkv_ref[...]
     out_ref[:, 3 * width : 4 * width] = proj_ref[...]
-    columns = jnp.transpose(vec_ref[...].astype(F32))
-    tail = jnp.zeros((shard, LANES - experts - columns.shape[1]), F32)
-    out_ref[:, 4 * width :] = jnp.concatenate(
-        [router_ref[...].astype(F32), columns, tail], axis=1
-    ).astype(BF)
+    rows = jnp.concatenate([router_ref[...].astype(F32), vec_ref[...].astype(F32)], axis=0)
+    columns = jnp.transpose(rows)
+    tail = jnp.zeros((shard, LANES - columns.shape[1]), F32)
+    out_ref[:, 4 * width :] = jnp.concatenate([columns, tail], axis=1).astype(BF)
+
+
+def assemble_kernel(sources, shard, meta_ref, *refs):
+    out_ref = refs[-1]
+    for ref, offsets in zip(refs[:-1], sources):
+        for at, offset in enumerate(offsets):
+            row = jnp.bitwise_xor(meta_ref[0], offset) * shard
+            out_ref[pl.ds(pl.multiple_of(row, shard), shard), :] = ref[at]
 
 
 def place_kernel(experts, room, routes_ref, dy_ref, send_ref, prow_ref, pcol_ref):
-    tokens = routes_ref.shape[3]
+    tokens = routes_ref.shape[4]
     slots = experts * room
-    cols = routes_ref[0, 0, 0]
-    wide = jnp.concatenate([cols.astype(F32), jnp.zeros((tokens, LANES - TOP), F32)], axis=1)
-    across = jnp.transpose(wide)[0:8, :].astype(jnp.int32)
-    first_row = across[0:1, :]
-    second_row = across[1:2, :]
+    rows = routes_ref[0, 0, 0]
+    first_row = rows[0:1]
+    second_row = rows[1:2]
+    tall = jnp.concatenate([rows.astype(F32), jnp.zeros((LANES - TOP, tokens), F32)], axis=0)
+    cols = jnp.transpose(tall)[:, 0:8].astype(jnp.int32)
     hot_first = (iota((experts, tokens), 0) == first_row).astype(F32)
     hot_second = (iota((experts, tokens), 0) == second_row).astype(F32)
     earlier = (iota((tokens, tokens), 0) < iota((tokens, tokens), 1)).astype(BF)
@@ -221,7 +228,7 @@
     refs = refs[8:]
     if not first:
         _, gup_in, gdn_in, gb_in, gdb_in = refs[:5]
-        refs = refs[5:]
+        refs = refs[6 if last else 5 :]
     r_ref, dbuf_ref, gup_ref, gdn_ref, gb_ref, gdb_ref = refs[:6]
     refs = refs[6:]
     if last:
@@ -494,8 +501,15 @@
     out_ref[...] = grad.astype(BF).reshape(images, local_len, width)
 
 
-def mix_kernel(cfg, back_ref, pcol_ref, gate_ref, middle_ref, *refs):
-    out_ref = refs[-1]
+def mix_kernel(cfg, back_ref, pcol_ref, *refs):
+    for mb in range(MICRO):
+
+        @pl.when(pl.program_id(0) == mb)
+        def _():
+            mix_part(cfg, back_ref, pcol_ref, refs[2 * mb], refs[2 * mb + 1], refs[-1])
+
+
+def mix_part(cfg, back_ref, pcol_ref, gate_ref, middle_ref, out_ref):
     images, local_len, width, experts, room = cfg
     tokens = images * local_len
     slots = experts * room
@@ -591,7 +605,7 @@
 
     any_spec = pl.BlockSpec(memory_space=pl.ANY)
     other_spec = lambda mb: pl.BlockSpec(
-        (seq_count - 1, count, local_len, width), lambda i: (0, mb, 0, 0)
+        (seq_count - 1, count, local_len, width), lambda i: (0, max(mb - 1, 0), 0, 0)
     )
     halved = hidden // FF_BLOCK // 2
     early_spec = lambda: pl.BlockSpec(
@@ -603,45 +617,21 @@
     misc_spec = pl.BlockSpec((width, LANES), lambda i: (0, 4 * width // LANES))
     moved = struct((experts, room, width), BF)
     merged = struct((experts, MICRO * room, width), BF)
-
-    others = jnp.stack(
-        [
-            lax.ppermute(
-                images, "seq", [((i + j) % seq_count, i) for i in range(seq_count)]
-            )
-            for j in range(1, seq_count)
-        ]
-    )
-    vectors = jnp.concatenate(
-        [
-            jnp.stack([attn_norm_gain, attn_norm_bias]),
-            query_value_bias,
-            jnp.stack([proj_bias, moe_norm_gain, moe_norm_bias, jnp.zeros_like(proj_bias)]),
-        ],
-        axis=0,
-    )
-    shard = router_weight.shape[0]
-    pack_args = (qkv_weight, proj_weight, router_weight, vectors)
-    packed_shard = pl.pallas_call(
-        functools.partial(pack_kernel, experts),
-        grid=(1,),
-        in_specs=[full(a.shape) for a in pack_args],
-        out_specs=full((shard, packed_width)),
-        out_shape=struct((shard, packed_width), BF),
-        compiler_params=params(),
-        cost_estimate=cost(1),
-        name="pack",
-    )(*pack_args)
-    packed = lax.all_gather(packed_shard, "dp", axis=0, tiled=True)
-
-    def exchange(array):
-        return lax.all_to_all(array, "dp", split_axis=0, concat_axis=0, tiled=True)
+    tailed = struct((experts, (MICRO - 1) * room, width), BF)
+
+    def seq_shift(array, j):
+        return lax.ppermute(array, "seq", [((i + j) % seq_count, i) for i in range(seq_count)])
+
+    others = []
+    for part in (images[:count], images[count:]):
+        moved_images = jnp.stack([seq_shift(part, j) for j in range(1, seq_count)])
+        others.append(moved_images)
 
     sent_dy, prow, pcol = pl.pallas_call(
         functools.partial(place_kernel, experts, room),
         grid=(MICRO,),
         in_specs=[
-            pl.BlockSpec((1, 1, 1, tokens, TOP), lambda i: (0, i, 0, 0, 0)),
+            pl.BlockSpec((1, 1, 1, TOP, tokens), lambda i: (0, i, 0, 0, 0)),
             pl.BlockSpec((count, local_len, width), lambda i: (i, 0, 0)),
         ],
         out_specs=[
@@ -657,7 +647,81 @@
         compiler_params=params(),
         cost_estimate=cost(8),
         name="place",
-    )(after(routes, packed_shard), cotangent)
+    )(jnp.swapaxes(routes, 3, 4), cotangent)
+
+    vectors = jnp.concatenate(
+        [
+            jnp.stack([attn_norm_gain, attn_norm_bias]),
+            query_value_bias,
+            jnp.stack([proj_bias, moe_norm_gain, moe_norm_bias, jnp.zeros_like(proj_bias)]),
+        ],
+        axis=0,
+    )
+    shard = router_weight.shape[0]
+    bits = dp_count.bit_length() - 1
+    assert dp_count == 1 << bits
+
+    def across(value, offset):
+        return lax.ppermute(value, "dp", [(i, i ^ offset) for i in range(dp_count)])
+
+    def gather_rows(own, gate):
+        quarter = dp_count // 4
+        held = [jnp.stack([own, *[across(own, k * quarter) for k in (1, 2, 3)]])]
+        offsets = [[0, quarter, 2 * quarter, 3 * quarter]]
+        for bit in reversed(range(bits - 2)):
+            if bit == 0:
+                held[-1] = after(held[-1], gate)
+            held += [across(h, 1 << bit) for h in held]
+            offsets += [[k ^ (1 << bit) for k in known] for known in offsets]
+        return pl.pallas_call(
+            functools.partial(assemble_kernel, offsets, shard),
+            grid=(1,),
+            in_specs=[smem_spec(), *[full(h.shape) for h in held]],
+            out_specs=full((dp_count * shard, packed_width)),
+            out_shape=struct((dp_count * shard, packed_width), BF),
+            compiler_params=params(),
+            cost_estimate=cost(3),
+            name="assemble",
+        )(meta, *held), held[0]
+
+    def scatter_rows(total, far):
+        me = lax.axis_index("dp")
+        value = total.reshape(dp_count // 2, 2, shard, packed_width)
+        for bit in range(bits - 2):
+            mine = lax.bitwise_and(lax.shift_right_logical(me, bit), 1)
+            keep = lax.dynamic_index_in_dim(value, mine, 1, keepdims=False)
+            give = lax.dynamic_index_in_dim(value, 1 - mine, 1, keepdims=False)
+            give = give.astype(BF)
+            value = keep.astype(F32) + across(give, 1 << bit).astype(F32)
+            if bit < bits - 3:
+                value = value.reshape(-1, 2, shard, packed_width)
+        value = after(value, *far)
+        high = lax.shift_right_logical(me, bits - 2)
+        result = lax.dynamic_index_in_dim(value, high, 0, keepdims=False)
+        for offset in (1, 2, 3):
+            give = lax.dynamic_index_in_dim(
+                value, lax.bitwise_xor(high, offset), 0, keepdims=False
+            )
+            result = result + across(give.astype(BF), offset << (bits - 2)).astype(F32)
+        return result, value
+
+    pack_args = (qkv_weight, proj_weight, router_weight.T, vectors)
+    packed_shard = pl.pallas_call(
+        functools.partial(pack_kernel, experts),
+        grid=(1,),
+        in_specs=[full(a.shape) for a in pack_args],
+        out_specs=full((shard, packed_width)),
+        out_shape=struct((shard, packed_width), BF),
+        compiler_params=params(),
+        cost_estimate=cost(1),
+        name="pack",
+    )(*pack_args)
+
+    def exchange(array):
+        return lax.all_to_all(array, "dp", split_axis=0, concat_axis=0, tiled=True)
+
+    packed, near = gather_rows(packed_shard, others[1])
+    dyb = exchange(after(sent_dy, near, others[0]))
 
     def forward(mb):
         cfg = (count, local_len, seq_count, width, experts, room)
@@ -693,9 +757,9 @@
             compiler_params=params(),
             cost_estimate=cost(11),
             name="forward",
-        )(meta, lengths, images, others, packed, prow)
-
-    def expert(mb, buf, results, totals):
+        )(meta, lengths, images, others[min(mb, 1)], packed, prow)
+
+    def expert(mb, buf, results, tail_back, totals):
         first = mb == 0
         last = mb == MICRO - 1
         cfg = (experts, room, capacity, width)
@@ -719,15 +783,19 @@
             aliases.update({len(args) + 1 + j: 2 + j for j in range(4)})
             in_specs += [any_spec, *total_specs]
             args += [results, *totals]
+        if mb >= 2:
+            aliases[len(args)] = 1
+            in_specs += [any_spec]
+            args += [tail_back]
         outs = pl.pallas_call(
             functools.partial(expert_kernel, cfg, first, last),
             grid=(hidden // FF_BLOCK,),
             in_specs=in_specs,
-            out_specs=[block_spec(mb), full((experts, room, width)), *total_specs]
+            out_specs=[block_spec(mb), block_spec(max(mb - 1, 0)), *total_specs]
             + ([early_spec(), late_spec()] * 2 if last else []),
             out_shape=[
                 merged,
-                moved,
+                moved if first else tailed,
                 struct((width, hidden), F32),
                 struct((width, hidden), F32),
                 struct((1, hidden), F32),
@@ -756,11 +824,11 @@
         middle, gate, second, oT, q, k, v, lse, n1T = saved
         whole = [gate, middle, second]
         heads = [oT, packed, q, k, v, lse, n1T]
-        args = [meta, lengths, dback, pcol, *whole, cotangent, *heads, images, others]
+        args = [meta, lengths, dback, pcol, *whole, cotangent, *heads, images, others[min(mb, 1)]]
         in_specs = [
             smem_spec(),
             smem_spec(),
-            full(dback.shape),
+            block_spec(max(mb - 1, 0)),
             table_spec(mb, (tokens, 8)),
             *[full(a.shape) for a in whole],
             token_spec(mb),
@@ -794,7 +862,7 @@
             ],
             input_output_aliases=aliases,
             compiler_params=params(),
-            cost_estimate=cost(17),
+            cost_estimate=cost(1 if last else 17),
             name="backward",
         )(*args)
 
@@ -829,23 +897,23 @@
             "finish",
         )
 
-    def mix(mb, back, gate, middle, previous):
+    def mix(back):
         cfg = (count, local_len, width, experts, room)
-        specs = [
-            block_spec(mb),
-            table_spec(mb, (tokens, 8)),
-            full(gate.shape),
-            full(middle.shape),
-        ]
-        return into(
+        tables = sum([[saved[mb][1], saved[mb][0]] for mb in range(MICRO)], [])
+        return pl.pallas_call(
             functools.partial(mix_kernel, cfg),
-            mb,
-            [back, pcol, gate, middle],
-            specs,
-            previous,
-            3,
-            "mix",
-        )
+            grid=(MICRO,),
+            in_specs=[
+                pl.BlockSpec((experts, room, width), lambda i: (0, i, 0)),
+                pl.BlockSpec((1, tokens, 8), lambda i: (i, 0, 0)),
+                *[full(t.shape) for t in tables],
+            ],
+            out_specs=pl.BlockSpec((count, local_len, width), lambda i: (i, 0, 0)),
+            out_shape=struct(images.shape, BF),
+            compiler_params=params(),
+            cost_estimate=cost(7),
+            name="mix",
+        )(back, pcol, *tables)
 
     swap = [(i, (i + 1) % seq_count) for i in range(seq_count)]
 
@@ -854,55 +922,55 @@
             return value + lax.ppermute(value.astype(BF), "seq", swap).astype(F32)
         return lax.psum(value.astype(BF), "seq").astype(F32)
 
-    dyb = exchange(sent_dy)
-    saved = []
+    passed = [forward(mb) for mb in range(MICRO)]
+    saved = [outs[1:] for outs in passed]
     bufs = []
     for mb in range(MICRO):
-        outs = forward(mb)
-        bufs.append(exchange(outs[0]))
-        saved.append(outs[1:])
+        first_gate = (dyb,) if mb == 0 else ()
+        bufs.append(exchange(after(passed[mb][0], *first_gate)))
     totals = None
     results = None
-    ready = []
+    ready = [None, None]
     for mb in range(MICRO):
-        results, dback, totals = expert(mb, bufs[mb], results, totals)
-        ready.append(dback)
+        results, ready[min(mb, 1)], totals = expert(mb, bufs[mb], results, ready[1], totals)
     gup, gdn, gbias, gdbias, *pieces = totals
     arrived = []
     if seq_count == 2:
         arrived = [lax.ppermute(piece, "seq", swap) for piece in pieces]
     dense = None
-    grads = None
     owns = []
+    gots = []
+    dms = []
+    dbacks = [exchange(ready[0]), exchange(ready[1])]
+    if arrived:
+        dbacks[1], arrived[0] = lax.optimization_barrier((dbacks[1], arrived[0]))
     for mb in range(MICRO):
-        sent = ready[mb]
-        if mb == 1:
-            sent = after(sent, ready[MICRO - 1])
-        if mb >= 2:
-            sent = after(sent, owns[mb - 2])
-        dback = exchange(sent)
-        if arrived and mb >= 1:
-            dback, arrived[mb - 1] = lax.optimization_barrier((dback, arrived[mb - 1]))
-        if mb == MICRO - 1:
-            results = after(results, owns[mb - 1])
+        dback = dbacks[min(mb, 1)]
+        if mb == 2 and arrived:
+            dense, arrived[1] = lax.optimization_barrier((dense, arrived[1]))
         own, oth, dm, *dense = backward(mb, dback, saved[mb], dense)
         owns.append(own)
-        got = jnp.stack(
-            [
-                lax.ppermute(
-                    oth[j - 1], "seq", [(i, (i + j) % seq_count) for i in range(seq_count)]
-                )
-                for j in range(1, seq_count)
-            ]
+        dms.append(dm)
+        gots.append(
+            jnp.stack(
+                [
+                    lax.ppermute(
+                        oth[j - 1], "seq", [(i, (i + j) % seq_count) for i in range(seq_count)]
+                    )
+                    for j in range(1, seq_count)
+                ]
+            )
         )
-        if arrived and mb == MICRO - 1:
-            got, arrived[2] = lax.optimization_barrier((got, arrived[2]))
-        grads = finish(mb, own, got, dm, grads)
-    shards = lax.psum_scatter(dense[0], "dp", scatter_dimension=0, tiled=True)
-    back = exchange(after(results, dback))
-    out = None
+    back = exchange(after(results, dbacks[1]))
+    first, far = (), ()
+    if arrived:
+        first, far = (arrived[2],), (arrived[3], gots[0], gots[1])
+    shards, late = scatter_rows(after(dense[0], *first), (*far, back))
+    owns = [after(own, late) for own in owns]
+    grads = None
     for mb in range(MICRO):
-        out = mix(mb, back, saved[mb][1], saved[mb][0], out)
+        grads = finish(mb, owns[mb], gots[mb], dms[mb], grads)
+    out = mix(back)
 
     if seq_count == 2:
         wide = lambda: pl.BlockSpec((width, FF_BLOCK), lambda i: (0, i))
@@ -927,7 +995,7 @@
     final_up_shift = biases[:, :hidden]
     final_down_shift = biases[:, hidden:]
 
-    shards = seq_sum(shards.astype(F32))
+    shards = seq_sum(shards)
     misc = 4 * width + experts
     return (
         out,

time: 403 us -> 360 us (0.89)
  waiting for transfers between devices: 127 us -> 82.6 us
  starting transfers between devices: 64.7 us -> 80.8 us
  between operations: 14.8 us -> 1.19 us
    ppermute x3, waiting for transfers between devices: 57 us -> 5.37 us  [on_device(): lax.ppermute(oth[j - 1], 'seq', [(i, (i + j) % seq_count) for i in range(...]
    all_gather x1 -> x0, waiting for transfers between devices: 33.7 us -> none  [on_device(): packed = lax.all_gather(packed_shard, 'dp', axis=0, tiled=True)]
    ppermute x1 -> x13, waiting for transfers between devices: 22.2 us -> 38.5 us  [the longest x11 24.9 us: across(): return lax.ppermute(value, 'dp', [(i, i ^ offset) for i in range(dp_count)])]
    ppermute x1 -> x13, starting transfers between devices: 1.55 us -> 17.6 us  [the longest x11 14.2 us: across(): return lax.ppermute(value, 'dp', [(i, i ^ offset) for i in range(dp_count)])]
    ppermute x4, waiting for transfers between devices: 6.56 us -> 21.8 us  [on_device(): arrived = [lax.ppermute(piece, 'seq', swap) for piece in pieces]]
    pallas_call x6 -> x3, Pallas kernels: 17.4 us -> 8.1 us  [into(): pl.pallas_call(kernel, grid=(1,), in_specs=specs, out_specs=token_spec(mb...]
    pallas_call x0 -> x2, Pallas kernels: none -> 8.92 us  [the longest x1 5.82 us: mix(): pl.pallas_call(functools.partial(mix_kernel, cfg), grid=(MICRO,), in_spec...]
    all_to_all x8 -> x7, waiting for transfers between devices: 5.94 us -> 13.4 us  [exchange(): return lax.all_to_all(array, 'dp', split_axis=0, concat_axis=0, tiled=True)]
  transfers between devices with their start and end apart: 20 -> 29, of which waited for: 9 -> 13; matrix products, arithmetic and copies ran while one was open for 2% -> 2% of each run, Pallas kernels for 42% -> 49%
where the time goes in v3:
time: 360 us; the launch traced here: 354 us
  Pallas kernels  176 us (49%)
  waiting for transfers between devices  82.6 us (23%)
  starting transfers between devices  80.8 us (22%)
  local copies, waits for them, and re-layouts  9.81 us (3%)
    pallas_call x3, Pallas kernels, expert(): pl.pallas_call(functools.partial(expert_kernel, cfg, first, last), grid=(...  58.8 us
    all_to_all x7, starting transfers between devices, exchange(): return lax.all_to_all(array, 'dp', split_axis=0, concat_axis=0, tiled=True)  53.4 us
    pallas_call x3, Pallas kernels, backward(): pl.pallas_call(functools.partial(backward_kernel, cfg, mb, first, last),...  51.5 us
    pallas_call x3, Pallas kernels, forward(): pl.pallas_call(functools.partial(forward_kernel, cfg, mb), grid=(1,), in_...  33.1 us
    ppermute x11, waiting for transfers between devices, across(): return lax.ppermute(value, 'dp', [(i, i ^ offset) for i in range(dp_count)])  24.9 us
    ppermute x4, waiting for transfers between devices, on_device(): arrived = [lax.ppermute(piece, 'seq', swap) for piece in pieces]  21.8 us
    ppermute x11, starting transfers between devices, across(): return lax.ppermute(value, 'dp', [(i, i ^ offset) for i in range(dp_count)])  14.2 us
    ppermute x2, waiting for transfers between devices, seq_shift(): lax.ppermute(array, 'seq', [((i + j) % seq_count, i) for i in range(seq_c...  13.6 us
  transfers between devices with their start and end apart: 29, of which 13 were waited for; matrix products, arithmetic and copies ran while one was open for 2% of the time, Pallas kernels for 49%

profile of v3, /device:TPU:0, one launch (start us, length us, event | category | flops | bytes accessed | tf_op | source)
XLA Modules:
  0.0 354.1 jit_solution(14312761914490071459)
XLA Ops:
  0.7 1.4 concatenate.14.vec_ref
  2.1 1.7 pack.1
  3.7 3.1 collective-permute-start.1
  6.8 2.6 collective-permute-start.2
  9.4 1.8 collective-permute-start.7
  11.2 5.6 %place.1 = (bf16[16,168,512]{2,1,0:T(8,128)(2,1)}, s32[3,2,320]{2,1,0:T(2,128)}, s32[3,320,8]{2,1,0:T(8,128)}) custom-call(s32[1,3,1,2,320]{4,3,2,1,0:T(2,128)} %bitcast.73, bf16[3,320,512]{2,1,0:T(8,128)(2,1)} %refs_7_.11), custom_call_target="tpu_custom_call" | custom-call | flops 8000000000 | bytes 16000000 | tf_op jit(solution)/shard_map/place/pallas_call | solution.py:630
  16.8 3.6 %collective-permute-done.2 = bf16[32,2176]{1,0:T(8,128)(2,1)S(1)} collective-permute-done((bf16[32,2176]{1,0:T(8,128)(2,1)}, bf16[32,2176]{1,0:T(8,128)(2,1)S(1)}, u32[]{:S(2)}, u32[]{:S(2)}) %collective-permute-start.2) | collective-permute-done | bytes 139296 | tf_op jit(solution)/shard_map/ppermute | solution.py:665
  20.5 0.8 copy-done.14
  21.3 5.6 %all-to-all-start.1 = ((bf16[16,168,512]{2,1,0:T(8,128)(2,1)}), bf16[16,168,512]{2,1,0:T(8,128)(2,1)}, u32[]{:S(2)}, u32[]{:S(2)}) async-start(bf16[16,168,512]{2,1,0:T(8,128)(2,1)} %get-tuple-element.104), calls=%async_computation.1 | async-start | bytes 5505024 | tf_op jit(solution)/shard_map/all_to_all | solution.py:721
  26.9 1.6 collective-permute-start
  28.5 1.9 collective-permute-start.4
  30.4 13.6 %collective-permute-done = bf16[2,320,512]{2,1,0:T(8,128)(2,1)S(1)} collective-permute-done((bf16[2,320,512]{2,1,0:T(8,128)(2,1)S(1)}, bf16[2,320,512]{2,1,0:T(8,128)(2,1)S(1)}, u32[]{:S(2)}, u32[]{:S(2)}) %collective-permute-start) | collective-permute-done | bytes 655392 | tf_op jit(solution)/shard_map/ppermute | solution.py:623
  44.0 20.0 %collective-permute-done.4.refs_1_ = bf16[4,32,2176]{2,1,0:T(8,128)(2,1)S(1)} collective-permute-done((bf16[4,32,2176]{2,1,0:T(8,128)(2,1)S(1)}, bf16[4,32,2176]{2,1,0:T(8,128)(2,1)S(1)}, u32[]{:S(2)}, u32[]{:S(2)}) %collective-permute-start.4) | collective-permute-done | bytes 557088 | tf_op jit(solution)/shard_map/ppermute | solution.py:665
  64.0 0.7 pad_add_fusion.meta_ref.refs_0_
  64.7 1.3 collective-permute-done.6.refs_3_
  66.0 0.8 copy-done.13
  66.8 3.1 assemble.1.w_ref.refs_3_.refs_9_.wm_ref
  69.9 11.0 %forward.5 = (bf16[16,56,512]{2,1,0:T(8,128)(2,1)}, f32[320,512]{1,0:T(8,128)}, f32[320,128]{1,0:T(8,128)}, bf16[320,512]{1,0:T(8,128)(2,1)}, bf16[512,320]{1,0:...) custom-call(s32[2]{0:T(128)} %pad_add_fusion.meta_ref.refs_0_, ...), custom_call_target="tpu_custom_call" | custom-call | flops 11000000512 | bytes 22000000 | tf_op jit(solution)/shard_map/forward/pallas_call | solution.py:740
  80.9 12.6 %all-to-all-start.3 = ((bf16[16,56,512]{2,1,0:T(8,128)(2,1)}), bf16[16,56,512]{2,1,0:T(8,128)(2,1)S(1)}, u32[]{:S(2)}, u32[]{:S(2)}) async-start(bf16[16,56,512]{2,1,0:T(8,128)(2,1)} %get-tuple-element.107), calls=%async_computation.3 | async-start | bytes 1835008 | tf_op jit(solution)/shard_map/all_to_all | solution.py:721
  93.5 11.0 %forward.4 = (bf16[16,56,512]{2,1,0:T(8,128)(2,1)}, f32[320,512]{1,0:T(8,128)}, f32[320,128]{1,0:T(8,128)}, bf16[320,512]{1,0:T(8,128)(2,1)}, bf16[512,320]{1,0:...) custom-call(s32[2]{0:T(128)} %pad_add_fusion.meta_ref.refs_0_, ...), custom_call_target="tpu_custom_call" | custom-call | flops 11000000512 | bytes 22000000 | tf_op jit(solution)/shard_map/forward/pallas_call | solution.py:740
  104.5 11.0 %forward.3 = (bf16[16,56,512]{2,1,0:T(8,128)(2,1)}, f32[320,512]{1,0:T(8,128)}, f32[320,128]{1,0:T(8,128)}, bf16[320,512]{1,0:T(8,128)(2,1)}, bf16[512,320]{1,0:...) custom-call(s32[2]{0:T(128)} %pad_add_fusion.meta_ref.refs_0_, ...), custom_call_target="tpu_custom_call" | custom-call | flops 11000000512 | bytes 22000000 | tf_op jit(solution)/shard_map/forward/pallas_call | solution.py:740
  115.6 6.1 %all-to-all-start.2 = ((bf16[16,56,512]{2,1,0:T(8,128)(2,1)}), bf16[16,56,512]{2,1,0:T(8,128)(2,1)S(1)}, u32[]{:S(2)}, u32[]{:S(2)}) async-start(bf16[16,56,512]{2,1,0:T(8,128)(2,1)} %get-tuple-element.105), calls=%async_computation.2 | async-start | bytes 1835008 | tf_op jit(solution)/shard_map/all_to_all | solution.py:721
  121.7 18.7 %expert.3 = (bf16[16,168,512]{2,1,0:T(8,128)(2,1)}, bf16[16,56,512]{2,1,0:T(8,128)(2,1)}, f32[512,2048]{1,0:T(8,128)}, f32[512,2048]{1,0:T(8,128)}, f32[1,2048]{1,0:T(1,128)}, /*index=5*/f32[1,512]{1,0:T(1,128)}) custom-call(s32[2]{0:T(128)} %pad_add_fusion.meta_ref.refs_0_, bf16[16,56,512]{2,1,0:T(8,128)(2,1)} %copy-done.3, ...), custom_call_target="tpu_custom_call" | custom-call | flops 19000000512 | bytes 38000000 | tf_op jit(solution)/shard_map/expert/pallas_call | solution.py:790
  140.4 2.1 all-to-all-done.2.refs_1_
  142.5 6.5 %all-to-all-start = ((bf16[16,56,512]{2,1,0:T(8,128)(2,1)}), bf16[16,56,512]{2,1,0:T(8,128)(2,1)S(1)}, u32[]{:S(2)}, u32[]{:S(2)}) async-start(bf16[16,56,512]{2,1,0:T(8,128)(2,1)} %get-tuple-element.102), calls=%async_computation | async-start | bytes 1835008 | tf_op jit(solution)/shard_map/all_to_all | solution.py:721
  149.0 19.5 %expert.4 = (bf16[16,168,512]{2,1,0:T(8,128)(2,1)}, bf16[16,112,512]{2,1,0:T(8,128)(2,1)}, f32[512,2048]{1,0:T(8,128)}, f32[512,2048]{1,0:T(8,128)}, f32[1,2048]{1,0:T(1,128)}, /*index=5*/f32[1,512]{1,0:T(1,128)}) custom-call(s32[2]{0:T(128)} %pad_add_fusion.meta_ref.refs_0_, ...), custom_call_target="tpu_custom_call", output_to_operand_aliasing={{0}: (8, {}), {2}: (9, {}), {3}: (10, {}), {4}: (11, {}), {... | custom-call | flops 19000000512 | bytes 38000000 | tf_op jit(solution)/shard_map/expert/pallas_call | solution.py:790
  168.5 1.3 all-to-all-done.refs_1_
  169.8 6.1 %all-to-all-start.6 = ((bf16[16,56,512]{2,1,0:T(8,128)(2,1)}), bf16[16,56,512]{2,1,0:T(8,128)(2,1)S(1)}, u32[]{:S(2)}, u32[]{:S(2)}) async-start(bf16[16,56,512]{2,1,0:T(8,128)(2,1)} %get-tuple-element.145), calls=%async_computation.6 | async-start | bytes 1835008 | tf_op jit(solution)/shard_map/all_to_all | solution.py:721
  175.9 20.7 %expert.5 = (bf16[16,168,512]{2,1,0:T(8,128)(2,1)}, bf16[16,112,512]{2,1,0:T(8,128)(2,1)}, f32[512,2048]{1,0:T(8,128)}, f32[512,2048]{1,0:T(8,128)}, f32[1,2048]...) custom-call(s32[2]{0:T(128)} %pad_add_fusion.meta_ref.refs_0_, ...), custom_call_target="tpu_custom_call", output_to_operand_aliasing={{0}: (8, {}), {2}: (9, {}), {3}: (10, {}), {4}: (11, {}), {... | custom-call | flops 19000000512 | bytes 38000000 | tf_op jit(solution)/shard_map/expert/pallas_call | solution.py:790
  196.7 6.1 %all-to-all-start.4 = ((bf16[16,112,512]{2,1,0:T(8,128)(2,1)}), bf16[16,112,512]{2,1,0:T(8,128)(2,1)S(1)}, u32[]{:S(2)}, u32[]{:S(2)}) async-start(bf16[16,112,512]{2,1,0:T(8,128)(2,1)} %get-tuple-element.120), calls=%async_computation.4 | async-start | bytes 3670016 | tf_op jit(solution)/shard_map/all_to_all | solution.py:721
  202.8 1.6 collective-permute-start.8
  204.9 1.5 collective-permute-start.10
  206.3 16.8 %backward.3 = (f32[320,512]{1,0:T(8,128)}, bf16[1,320,512]{2,1,0:T(8,128)(2,1)}, f32[320,512]{1,0:T(8,128)}, f32[512,2048]{1,0:T(8,128)}, f32[128,512]{1,0:T(8,128)}) custom-call(s32[2]{0:T(128)} %pad_add_fusion.meta_ref.refs_0_, s32[3]{0:T(128)} %refs_1_.5, bf16[16,56,512]{2,1,0:T(8,128)(2,1)} %copy-done.2, ...), custom_call_target="tpu_custom_call" | custom-call | flops 16999999488 | bytes 34000000 | tf_op jit(solution)/shard_map/backward/pallas_call | solution.py:852
  223.1 6.0 %collective-permute-done.8.up_early = bf16[512,1024]{1,0:T(8,128)(2,1)} collective-permute-done((bf16[512,1024]{1,0:T(8,128)(2,1)}, bf16[512,1024]{1,0:T(8,128)(2,1)}, u32[]{:S(2)}, u32[]{:S(2)}) %collective-permute-start.8) | collective-permute-done | bytes 1048608 | tf_op jit(solution)/shard_map/ppermute | solution.py:939
  229.2 10.0 %all-to-all-done.4.refs_2_ = bf16[16,112,512]{2,1,0:T(8,128)(2,1)S(1)} async-done(((bf16[16,112,512]{2,1,0:T(8,128)(2,1)}), bf16[16,112,512]{2,1,0:T(8,128)(2,1)S(1)}, u32[]{:S(2)}, u32[]{:S(2)}) %all-to-all-start.4) | async-done | bytes 1835040 | tf_op jit(solution)/shard_map/all_to_all | solution.py:721
  239.2 1.3 copy-done
  240.4 10.4 %all-to-all-start.5 = ((bf16[16,168,512]{2,1,0:T(8,128)(2,1)}), bf16[16,168,512]{2,1,0:T(8,128)(2,1)}, u32[]{:S(2)}, u32[]{:S(2)}) async-start(bf16[16,168,512]{2,1,0:T(8,128)(2,1)} %get-tuple-element.123), calls=%async_computation.5 | async-start | bytes 5505024 | tf_op jit(solution)/shard_map/all_to_all | solution.py:721
  250.8 17.3 %backward.4 = (f32[320,512]{1,0:T(8,128)}, bf16[1,320,512]{2,1,0:T(8,128)(2,1)}, f32[320,512]{1,0:T(8,128)}, f32[512,2048]{1,0:T(8,128)}, f32[128,512]{1,0:T(8,128)}) custom-call(s32[2]{0:T(128)} %pad_add_fusion.meta_ref.refs_0_, s32[3]{0:T(128)} %refs_1_.5, bf16[16,112,512]{2,1,0:T(8,128)(2,1)} %copy-done, ...), custom_call_target="tpu_custom_call", output_to_operand_aliasing={{3}: (17, {}), {4}: (18, {})} | custom-call | flops 16999999488 | bytes 34000000 | tf_op jit(solution)/shard_map/backward/pallas_call | solution.py:852
  268.1 17.5 %backward.5 = (f32[320,512]{1,0:T(8,128)}, bf16[1,320,512]{2,1,0:T(8,128)(2,1)}, f32[320,512]{1,0:T(8,128)}, bf16[512,2176]{1,0:T(8,128)(2,1)}, f32[128,512]{1,0:T(8,128)}) custom-call(s32[2]{0:T(128)} %pad_add_fusion.meta_ref.refs_0_, s32[3]{0:T(128)} %refs_1_.5, bf16[16,112,512]{2,1,0:T(8,128)(2,1)} %copy-done, ...), custom_call_target="tpu_custom_call" | custom-call | flops 1000000000 | bytes 2000000 | tf_op jit(solution)/shard_map/backward/pallas_call | solution.py:852
  285.6 1.3 dynamic-slice_bitcast_fusion
  287.5 1.6 collective-permute-start.21
  289.6 1.6 collective-permute-done.21
  291.3 0.6 slice.66
  291.9 0.6 slice.67
  292.5 1.6 collective-permute-start.14
  294.5 1.6 collective-permute-start.16
  296.1 1.8 convert_add_fusion
  298.0 1.7 collective-permute-start.12
  299.7 15.7 %collective-permute-done.13.dn_late = bf16[512,1024]{1,0:T(8,128)(2,1)} collective-permute-done((bf16[512,1024]{1,0:T(8,128)(2,1)}, bf16[512,1024]{1,0:T(8,128)(2,1)}, u32[]{:S(2)}, u32[]{:S(2)}) %collective-permute-start.13) | collective-permute-done | bytes 1048608 | tf_op jit(solution)/shard_map/ppermute | solution.py:939
  315.4 8.5 %sum_experts.1 = (f32[1,512,2048]{2,1,0:T(8,128)}, f32[1,2048,512]{2,1,0:T(8,128)}) custom-call(f32[512,2048]{1,0:T(8,128)} %get-tuple-element.177.gup_ref, f32[512,2048]{1,0:T(8,128)} %get-tuple-element.178.gdn_ref, bf16[512,1024]{1,0:T(8,128)(2,1)} %collective-permute-done.8.up_early, bf16[512,1024]{1,0:T(8,128)(2,1)} %collective-permute-done.9.up_late, ...), custom_call_target="tpu_custom_call" | custom-call | flops 8000000000 | bytes 16000000 | tf_op jit(solution)/shard_map/sum_experts/pallas_call | solution.py:977
  324.1 5.4 %collective-permute-done.15 = bf16[320,512]{1,0:T(8,128)(2,1)} collective-permute-done((bf16[320,512]{1,0:T(8,128)(2,1)}, bf16[320,512]{1,0:T(8,128)(2,1)}, u32[]{:S(2)}, u32[]{:S(2)}) %collective-permute-start.15) | collective-permute-done | bytes 327712 | tf_op jit(solution)/shard_map/ppermute | solution.py:957
  329.5 1.7 collective-permute-start.17
  331.2 2.4 collective-permute-start.18
  334.0 2.7 finish.3.refs_0_
  336.7 5.8 %mix.1 = bf16[3,320,512]{2,1,0:T(8,128)(2,1)} custom-call(bf16[16,168,512]{2,1,0:T(8,128)(2,1)} %all-to-all-done.5.back_ref, s32[3,320,8]{2,1,0:T(8,128)} %get-tuple-element.124.pcol_ref.refs_3_, f32[320,128]{1,0:T(8,128)} %get-tuple-element.125.refs_0_.refs_4_, f32[320,512]{1,0:T(8,128)} %get-tuple-element.126.refs_1_.refs_5_, ...), custom_call_target="tpu_custom_call" | custom-call | flops 7000000000 | bytes 14000000 | tf_op jit(solution)/shard_map/mix/pallas_call | solution.py:903
  342.5 2.7 finish.4.refs_0_
  345.3 0.6 collective-permute-start.20
  345.9 2.7 finish.5
  348.6 1.8 collective-permute-done.20
  350.5 0.8 slice_reduce_fusion
  351.3 0.7 slice.58
  352.0 0.6 slice.61
  352.6 0.7 copy.52
  353.3 0.6 pad_maximum_fusion.1
  (66 shorter events, 3.2 us)
Async XLA Ops:
  0.6 8.7 %copy-start.1 = (bf16[3,320,512]{2,1,0:T(8,128)(2,1)S(1)}, bf16[3,320,512]{2,1,0:T(8,128)(2,1)}, u32[]{:S(2)}) copy-start(bf16[3,320,512]{2,1,0:T(8,128)(2,1)} %x_ref.5) | copy-start | bytes 2949124
  3.7 13.1 %collective-permute-start.1 = (bf16[32,2176]{1,0:T(8,128)(2,1)}, bf16[32,2176]{1,0:T(8,128)(2,1)S(1)}, u32[]{:S(2)}, u32[]{:S(2)}) collective-permute-start(bf16[32,2176]{1,0:T(8,128)(2,1)} %pack.1), channel_id=1, source_target_pairs={{0,8},{2,10},{4,12},{6,14},{8,0},{10,2},{12,4},{14,6},{16,24},{18,... | collective-permute-start | bytes 417800 | tf_op jit(solution)/shard_map/ppermute | solution.py:665
  6.8 13.6 %collective-permute-start.2 = (bf16[32,2176]{1,0:T(8,128)(2,1)}, bf16[32,2176]{1,0:T(8,128)(2,1)S(1)}, u32[]{:S(2)}, u32[]{:S(2)}) collective-permute-start(bf16[32,2176]{1,0:T(8,128)(2,1)} %pack.1), channel_id=1, source_target_pairs={{0,16},{2,18},{4,20},{6,22},{8,24},{10,26},{12,28},{14,30},{16,0},... | collective-permute-start | bytes 417800 | tf_op jit(solution)/shard_map/ppermute | solution.py:665
  9.4 11.0 %collective-permute-start.3 = (bf16[32,2176]{1,0:T(8,128)(2,1)}, bf16[32,2176]{1,0:T(8,128)(2,1)S(1)}, u32[]{:S(2)}, u32[]{:S(2)}) collective-permute-start(bf16[32,2176]{1,0:T(8,128)(2,1)} %pack.1), channel_id=1, source_target_pairs={{0,24},{2,26},{4,28},{6,30},{8,16},{10,18},{12,20},{14,22},{16,8},... | collective-permute-start | bytes 417800 | tf_op jit(solution)/shard_map/ppermute | solution.py:665
  9.4 11.1 %collective-permute-start.7 = (bf16[1,320,512]{2,1,0:T(8,128)(2,1)S(1)}, bf16[1,320,512]{2,1,0:T(8,128)(2,1)S(1)}, u32[]{:S(2)}, u32[]{:S(2)}) collective-permute-start(bf16[1,320,512]{2,1,0:T(8,128)(2,1)S(1)} %slice.43), channel_id=1, source_target_pairs={{1,0},{0,1},{3,2},{2,3},{5,4},{4,5},{7,6},{6,7},{9,8},{8,9},{11,10... | collective-permute-start | bytes 983048 | tf_op jit(solution)/shard_map/ppermute | solution.py:623
  11.2 9.2 %copy-start.8 = (bf16[32,2176]{1,0:T(8,128)(2,1)S(1)}, bf16[32,2176]{1,0:T(8,128)(2,1)}, u32[]{:S(2)}) copy-start(bf16[32,2176]{1,0:T(8,128)(2,1)} %pack.1) | copy-start | bytes 417796
  20.5 9.9 %copy-start.7 = (bf16[4,32,2176]{2,1,0:T(8,128)(2,1)}, bf16[4,32,2176]{2,1,0:T(8,128)(2,1)S(1)}, u32[]{:S(2)}) copy-start(bf16[4,32,2176]{2,1,0:T(8,128)(2,1)S(1)} %pad_maximum_fusion.refs_0_) | copy-start | bytes 1671172
  20.5 0.8 copy-start.14
  21.3 59.6 %all-to-all-start.1 = ((bf16[16,168,512]{2,1,0:T(8,128)(2,1)}), bf16[16,168,512]{2,1,0:T(8,128)(2,1)}, u32[]{:S(2)}, u32[]{:S(2)}) async-start(bf16[16,168,512]{2,1,0:T(8,128)(2,1)} %get-tuple-element.104), calls=%async_computation.1 | async-start | bytes 5505024 | tf_op jit(solution)/shard_map/all_to_all | solution.py:721
  26.9 17.1 %collective-permute-start = (bf16[2,320,512]{2,1,0:T(8,128)(2,1)S(1)}, bf16[2,320,512]{2,1,0:T(8,128)(2,1)S(1)}, u32[]{:S(2)}, u32[]{:S(2)}) collective-permute-start(bf16[2,320,512]{2,1,0:T(8,128)(2,1)S(1)} %slice.42), channel_id=1, source_target_pairs={{1,0},{0,1},{3,2},{2,3},{5,4},{4,5},{7,6},{6,7},{9,8},{8,9},{11,10... | collective-permute-start | bytes 1966088 | tf_op jit(solution)/shard_map/ppermute | solution.py:623
  28.5 35.5 %collective-permute-start.4 = (bf16[4,32,2176]{2,1,0:T(8,128)(2,1)S(1)}, bf16[4,32,2176]{2,1,0:T(8,128)(2,1)S(1)}, u32[]{:S(2)}, u32[]{:S(2)}) collective-permute-start(bf16[4,32,2176]{2,1,0:T(8,128)(2,1)S(1)} %pad_maximum_fusion.refs_0_), channel_id=1, source_target_pairs={{0,4},{2,6},{4,0},{6,2},{8,12},{10,14},{12,8},{14,10},{16,20},{18,... | collective-permute-start | bytes 1671176 | tf_op jit(solution)/shard_map/ppermute | solution.py:665
  30.4 34.3 %collective-permute-start.5 = (bf16[4,32,2176]{2,1,0:T(8,128)(2,1)S(1)}, bf16[4,32,2176]{2,1,0:T(8,128)(2,1)S(1)}, u32[]{:S(2)}, u32[]{:S(2)}) collective-permute-start(bf16[4,32,2176]{2,1,0:T(8,128)(2,1)S(1)} %pad_maximum_fusion.refs_0_), channel_id=1, source_target_pairs={{0,2},{2,0},{4,6},{6,4},{8,10},{10,8},{12,14},{14,12},{16,18},{18,... | collective-permute-start | bytes 1671176 | tf_op jit(solution)/shard_map/ppermute | solution.py:665
  44.0 25.9 %copy-start.6 = (bf16[2,320,512]{2,1,0:T(8,128)(2,1)}, bf16[2,320,512]{2,1,0:T(8,128)(2,1)S(1)}, u32[]{:S(2)}) copy-start(bf16[2,320,512]{2,1,0:T(8,128)(2,1)S(1)} %collective-permute-done) | copy-start | bytes 1966084
  64.0 2.0 copy-start.11
  64.0 2.0 collective-permute-start.6
  64.7 1.3 copy-start.12
  66.0 0.8 copy-start.13
  80.9 34.7 %all-to-all-start.3 = ((bf16[16,56,512]{2,1,0:T(8,128)(2,1)}), bf16[16,56,512]{2,1,0:T(8,128)(2,1)S(1)}, u32[]{:S(2)}, u32[]{:S(2)}) async-start(bf16[16,56,512]{2,1,0:T(8,128)(2,1)} %get-tuple-element.107), calls=%async_computation.3 | async-start | bytes 1835008 | tf_op jit(solution)/shard_map/all_to_all | solution.py:721
  115.6 6.1 %copy-start.3 = (bf16[16,56,512]{2,1,0:T(8,128)(2,1)}, bf16[16,56,512]{2,1,0:T(8,128)(2,1)S(1)}, u32[]{:S(2)}) copy-start(bf16[16,56,512]{2,1,0:T(8,128)(2,1)S(1)} %all-to-all-done.3.refs_1_) | copy-start | bytes 2752516
  115.6 26.9 %all-to-all-start.2 = ((bf16[16,56,512]{2,1,0:T(8,128)(2,1)}), bf16[16,56,512]{2,1,0:T(8,128)(2,1)S(1)}, u32[]{:S(2)}, u32[]{:S(2)}) async-start(bf16[16,56,512]{2,1,0:T(8,128)(2,1)} %get-tuple-element.105), calls=%async_computation.2 | async-start | bytes 1835008 | tf_op jit(solution)/shard_map/all_to_all | solution.py:721
  142.5 6.6 %copy-start.5 = (bf16[16,56,512]{2,1,0:T(8,128)(2,1)}, bf16[16,56,512]{2,1,0:T(8,128)(2,1)S(1)}, u32[]{:S(2)}) copy-start(bf16[16,56,512]{2,1,0:T(8,128)(2,1)S(1)} %all-to-all-done.2.refs_1_) | copy-start | bytes 2752516
  142.5 27.3 %all-to-all-start = ((bf16[16,56,512]{2,1,0:T(8,128)(2,1)}), bf16[16,56,512]{2,1,0:T(8,128)(2,1)S(1)}, u32[]{:S(2)}, u32[]{:S(2)}) async-start(bf16[16,56,512]{2,1,0:T(8,128)(2,1)} %get-tuple-element.102), calls=%async_computation | async-start | bytes 1835008 | tf_op jit(solution)/shard_map/all_to_all | solution.py:721
  169.8 6.1 %copy-start.4 = (bf16[16,56,512]{2,1,0:T(8,128)(2,1)}, bf16[16,56,512]{2,1,0:T(8,128)(2,1)S(1)}, u32[]{:S(2)}) copy-start(bf16[16,56,512]{2,1,0:T(8,128)(2,1)S(1)} %all-to-all-done.refs_1_) | copy-start | bytes 2752516
  169.8 26.9 %all-to-all-start.6 = ((bf16[16,56,512]{2,1,0:T(8,128)(2,1)}), bf16[16,56,512]{2,1,0:T(8,128)(2,1)S(1)}, u32[]{:S(2)}, u32[]{:S(2)}) async-start(bf16[16,56,512]{2,1,0:T(8,128)(2,1)} %get-tuple-element.145), calls=%async_computation.6 | async-start | bytes 1835008 | tf_op jit(solution)/shard_map/all_to_all | solution.py:721
  196.7 9.7 %copy-start.2 = (bf16[16,56,512]{2,1,0:T(8,128)(2,1)}, bf16[16,56,512]{2,1,0:T(8,128)(2,1)S(1)}, u32[]{:S(2)}) copy-start(bf16[16,56,512]{2,1,0:T(8,128)(2,1)S(1)} %all-to-all-done.6.refs_2_) | copy-start | bytes 2752516
  196.7 42.5 %all-to-all-start.4 = ((bf16[16,112,512]{2,1,0:T(8,128)(2,1)}), bf16[16,112,512]{2,1,0:T(8,128)(2,1)S(1)}, u32[]{:S(2)}, u32[]{:S(2)}) async-start(bf16[16,112,512]{2,1,0:T(8,128)(2,1)} %get-tuple-element.120), calls=%async_computation.4 | async-start | bytes 3670016 | tf_op jit(solution)/shard_map/all_to_all | solution.py:721
  202.8 26.4 %collective-permute-start.8 = (bf16[512,1024]{1,0:T(8,128)(2,1)}, bf16[512,1024]{1,0:T(8,128)(2,1)}, u32[]{:S(2)}, u32[]{:S(2)}) collective-permute-start(bf16[512,1024]{1,0:T(8,128)(2,1)} %get-tuple-element.121), channel_id=1, source_target_pairs={{0,1},{1,0},{2,3},{3,2},{4,5},{5,4},{6,7},{7,6},{8,9},{9,8},{10,11... | collective-permute-start | bytes 3145736 | tf_op jit(solution)/shard_map/ppermute | solution.py:939
  204.3 63.8 %collective-permute-start.9 = (bf16[512,1024]{1,0:T(8,128)(2,1)}, bf16[512,1024]{1,0:T(8,128)(2,1)}, u32[]{:S(2)}, u32[]{:S(2)}) collective-permute-start(bf16[512,1024]{1,0:T(8,128)(2,1)} %get-tuple-element.157), channel_id=1, source_target_pairs={{0,1},{1,0},{2,3},{3,2},{4,5},{5,4},{6,7},{7,6},{8,9},{9,8},{10,11... | collective-permute-start | bytes 3145736 | tf_op jit(solution)/shard_map/ppermute | solution.py:939
  204.9 80.7 %collective-permute-start.10 = (bf16[512,1024]{1,0:T(8,128)(2,1)}, bf16[512,1024]{1,0:T(8,128)(2,1)}, u32[]{:S(2)}, u32[]{:S(2)}) collective-permute-start(bf16[512,1024]{1,0:T(8,128)(2,1)} %get-tuple-element.162), channel_id=1, source_target_pairs={{0,1},{1,0},{2,3},{3,2},{4,5},{5,4},{6,7},{7,6},{8,9},{9,8},{10,11... | collective-permute-start | bytes 3145736 | tf_op jit(solution)/shard_map/ppermute | solution.py:939
  239.2 1.3 copy-start
  240.4 89.0 %all-to-all-start.5 = ((bf16[16,168,512]{2,1,0:T(8,128)(2,1)}), bf16[16,168,512]{2,1,0:T(8,128)(2,1)}, u32[]{:S(2)}, u32[]{:S(2)}) async-start(bf16[16,168,512]{2,1,0:T(8,128)(2,1)} %get-tuple-element.123), calls=%async_computation.5 | async-start | bytes 5505024 | tf_op jit(solution)/shard_map/all_to_all | solution.py:721
  285.6 1.9 copy-start.9
  285.6 1.9 copy-start.10
  286.9 9.2 %collective-permute-start.11 = (bf16[8,32,2176]{2,1,0:T(8,128)(2,1)S(1)}, bf16[8,32,2176]{2,1,0:T(8,128)(2,1)}, u32[]{:S(2)}, u32[]{:S(2)}) collective-permute-start(bf16[8,32,2176]{2,1,0:T(8,128)(2,1)S(1)} %dynamic-slice_bitcast_fusion), channel_id=1, source_target_pairs={{0,2},{2,0},{4,6},{6,4},{8,10},{10,8},{12,14},{14,12},{16,18},{18,... | collective-permute-start | bytes 3342344 | tf_op jit(solution)/shard_map/ppermute | solution.py:665
  287.5 3.7 %collective-permute-start.21 = (bf16[1,2560]{1,0:T(2,128)(2,1)S(1)}, bf16[1,2560]{1,0:T(2,128)(2,1)S(1)}, u32[]{:S(2)}, u32[]{:S(2)}) collective-permute-start(bf16[1,2560]{1,0:T(2,128)(2,1)S(1)} %convert_element_type.82), channel_id=1, source_target_pairs={{0,1},{1,0},{2,3},{3,2},{4,5},{5,4},{6,7},{7,6},{8,9},{9,8},{10,11... | collective-permute-start | bytes 15368 | tf_op jit(solution)/shard_map/ppermute | solution.py:922
  289.1 26.3 %collective-permute-start.13 = (bf16[512,1024]{1,0:T(8,128)(2,1)}, bf16[512,1024]{1,0:T(8,128)(2,1)}, u32[]{:S(2)}, u32[]{:S(2)}) collective-permute-start(bf16[512,1024]{1,0:T(8,128)(2,1)} %get-tuple-element.164), channel_id=1, source_target_pairs={{0,1},{1,0},{2,3},{3,2},{4,5},{5,4},{6,7},{7,6},{8,9},{9,8},{10,11... | collective-permute-start | bytes 3145736 | tf_op jit(solution)/shard_map/ppermute | solution.py:939
  292.5 31.6 %collective-permute-start.14 = (bf16[320,512]{1,0:T(8,128)(2,1)}, bf16[320,512]{1,0:T(8,128)(2,1)}, u32[]{:S(2)}, u32[]{:S(2)}) collective-permute-start(bf16[320,512]{1,0:T(8,128)(2,1)} %bitcast.21), channel_id=1, source_target_pairs={{0,1},{1,0},{2,3},{3,2},{4,5},{5,4},{6,7},{7,6},{8,9},{9,8},{10,11... | collective-permute-start | bytes 983048 | tf_op jit(solution)/shard_map/ppermute | solution.py:957
  294.1 35.4 %collective-permute-start.15 = (bf16[320,512]{1,0:T(8,128)(2,1)}, bf16[320,512]{1,0:T(8,128)(2,1)}, u32[]{:S(2)}, u32[]{:S(2)}) collective-permute-start(bf16[320,512]{1,0:T(8,128)(2,1)} %bitcast.23), channel_id=1, source_target_pairs={{0,1},{1,0},{2,3},{3,2},{4,5},{5,4},{6,7},{7,6},{8,9},{9,8},{10,11... | collective-permute-start | bytes 983048 | tf_op jit(solution)/shard_map/ppermute | solution.py:957
  294.5 51.4 %collective-permute-start.16 = (bf16[320,512]{1,0:T(8,128)(2,1)}, bf16[320,512]{1,0:T(8,128)(2,1)}, u32[]{:S(2)}, u32[]{:S(2)}) collective-permute-start(bf16[320,512]{1,0:T(8,128)(2,1)} %bitcast.25), channel_id=1, source_target_pairs={{0,1},{1,0},{2,3},{3,2},{4,5},{5,4},{6,7},{7,6},{8,9},{9,8},{10,11... | collective-permute-start | bytes 983048 | tf_op jit(solution)/shard_map/ppermute | solution.py:957
  298.0 26.0 %collective-permute-start.12 = (bf16[4,32,2176]{2,1,0:T(8,128)(2,1)S(1)}, bf16[4,32,2176]{2,1,0:T(8,128)(2,1)S(1)}, u32[]{:S(2)}, u32[]{:S(2)}) collective-permute-start(bf16[4,32,2176]{2,1,0:T(8,128)(2,1)S(1)} %fusion), channel_id=1, source_target_pairs={{0,4},{2,6},{4,0},{6,2},{8,12},{10,14},{12,8},{14,10},{16,20},{18,... | collective-permute-start | bytes 1671176 | tf_op jit(solution)/shard_map/ppermute | solution.py:665
  329.5 15.7 %collective-permute-start.17 = (bf16[32,2176]{1,0:T(8,128)(2,1)S(1)}, bf16[32,2176]{1,0:T(8,128)(2,1)S(1)}, u32[]{:S(2)}, u32[]{:S(2)}) collective-permute-start(bf16[32,2176]{1,0:T(8,128)(2,1)S(1)} %get-tuple-element.237), channel_id=1, source_target_pairs={{0,8},{2,10},{4,12},{6,14},{8,0},{10,2},{12,4},{14,6},{16,24},{18,... | collective-permute-start | bytes 417800 | tf_op jit(solution)/shard_map/ppermute | solution.py:665
  331.2 14.0 %collective-permute-start.18 = (bf16[32,2176]{1,0:T(8,128)(2,1)S(1)}, bf16[32,2176]{1,0:T(8,128)(2,1)S(1)}, u32[]{:S(2)}, u32[]{:S(2)}) collective-permute-start(bf16[32,2176]{1,0:T(8,128)(2,1)S(1)} %get-tuple-element.239), channel_id=1, source_target_pairs={{0,16},{2,18},{4,20},{6,22},{8,24},{10,26},{12,28},{14,30},{16,0},... | collective-permute-start | bytes 417800 | tf_op jit(solution)/shard_map/ppermute | solution.py:665
  333.6 11.6 %collective-permute-start.19 = (bf16[32,2176]{1,0:T(8,128)(2,1)S(1)}, bf16[32,2176]{1,0:T(8,128)(2,1)S(1)}, u32[]{:S(2)}, u32[]{:S(2)}) collective-permute-start(bf16[32,2176]{1,0:T(8,128)(2,1)S(1)} %get-tuple-element.238), channel_id=1, source_target_pairs={{0,24},{2,26},{4,28},{6,30},{8,16},{10,18},{12,20},{14,22},{16,8},... | collective-permute-start | bytes 417800 | tf_op jit(solution)/shard_map/ppermute | solution.py:665
  345.3 5.1 %collective-permute-start.20 = (bf16[32,2176]{1,0:T(8,128)(2,1)S(1)}, bf16[32,2176]{1,0:T(8,128)(2,1)S(1)}, u32[]{:S(2)}, u32[]{:S(2)}) collective-permute-start(bf16[32,2176]{1,0:T(8,128)(2,1)S(1)} %fusion.6), channel_id=1, source_target_pairs={{0,1},{1,0},{2,3},{3,2},{4,5},{5,4},{6,7},{7,6},{8,9},{9,8},{10,11... | collective-permute-start | bytes 417800 | tf_op jit(solution)/shard_map/ppermute | solution.py:922

commit v4 on v3

--- a/solution.py
+++ b/solution.py
@@ -71,7 +71,23 @@
             out_ref[pl.ds(pl.multiple_of(row, shard), shard), :] = ref[at]
 
 
-def place_kernel(experts, room, routes_ref, dy_ref, send_ref, prow_ref, pcol_ref):
+def window(capacity, mb):
+    start = capacity * mb // 8 * 8
+    return start, capacity * mb - start
+
+
+def place_kernel(experts, room, capacity, routes_ref, dy_ref, send_ref, prow_ref, pcol_ref):
+    for mb in range(MICRO):
+
+        @pl.when(pl.program_id(0) == mb)
+        def _():
+            place_part(
+                experts, room, window(capacity, mb), routes_ref, dy_ref, send_ref, prow_ref, pcol_ref
+            )
+
+
+def place_part(experts, room, where, routes_ref, dy_ref, send_ref, prow_ref, pcol_ref):
+    start, shift = where
     tokens = routes_ref.shape[4]
     slots = experts * room
     rows = routes_ref[0, 0, 0]
@@ -85,8 +101,8 @@
     before = mm((hot_first + hot_second).astype(BF), earlier)
     in_first = jnp.sum(before * hot_first, axis=0, keepdims=True).astype(jnp.int32)
     in_second = jnp.sum((before + hot_first) * hot_second, axis=0, keepdims=True).astype(jnp.int32)
-    place_first = first_row * room + in_first
-    place_second = second_row * room + in_second
+    place_first = first_row * room + in_first + shift
+    place_second = second_row * room + in_second + shift
     prow_ref[0, 0:1, :] = place_first
     prow_ref[0, 1:2, :] = place_second
     slot_of = iota((slots, tokens), 0)
@@ -94,7 +110,12 @@
     flat = dy_ref[...].reshape(tokens, dy_ref.shape[-1])
     rows = mm(hot, flat)
     for e in range(experts):
-        send_ref[e] = rows[e * room : (e + 1) * room].astype(BF)
+        block = rows[e * room : (e + 1) * room].astype(BF)
+        if shift:
+            send_ref[e, start : start + 8] = send_ref[e, start : start + 8] + block[:8]
+            send_ref[e, start + 8 : start + room] = block[8:]
+        else:
+            send_ref[e, start : start + room] = block
     first_col = cols[:, 0:1]
     second_col = cols[:, 1:2]
     hot_first = (iota((tokens, experts), 1) == first_col).astype(F32)
@@ -107,12 +128,12 @@
     table = jnp.zeros((tokens, 8), jnp.int32)
     for at, col in enumerate(
         (
-            first_col * room + in_first,
-            second_col * room + in_second,
+            first_col * room + in_first + shift,
+            second_col * room + in_second + shift,
             first_col,
             second_col,
-            in_first,
-            in_second,
+            in_first + shift,
+            in_second + shift,
         )
     ):
         table = jnp.where(lane == at, col, table)
@@ -223,11 +244,11 @@
 
 
 def expert_kernel(cfg, first, last, *refs):
-    groups, room, capacity, width = cfg
+    groups, room, capacity, shift, width = cfg
     meta_ref, buf_ref, dyb_ref, wm_ref, up_ref, ub_ref, down_ref, db_ref = refs[:8]
     refs = refs[8:]
     if not first:
-        _, gup_in, gdn_in, gb_in, gdb_in = refs[:5]
+        r_in, gup_in, gdn_in, gb_in, gdb_in = refs[:5]
         refs = refs[6 if last else 5 :]
     r_ref, dbuf_ref, gup_ref, gdn_ref, gb_ref, gdb_ref = refs[:6]
     refs = refs[6:]
@@ -254,7 +275,10 @@
         gate = gates(mm(flat, wm_ref[...]), experts)
         mine = iota((1, LANES), 1) == meta_ref[0]
         mine_gate = jnp.sum(jnp.where(mine, gate, 0.0), axis=1, keepdims=True)
-        dr = (dyb_ref[...].astype(F32).reshape(slots, width) * mine_gate).astype(BF)
+        at = iota((groups, room, 1), 1)
+        own = (at >= shift) & (at < shift + capacity)
+        dy = jnp.where(own, dyb_ref[...].astype(F32), 0.0)
+        dr = (dy.reshape(slots, width) * mine_gate).astype(BF)
         dr_s[...] = dr
         drT_s[...] = jnp.transpose(dr)
         shift_sum = jnp.sum(dr.astype(F32), axis=0, keepdims=True)
@@ -299,7 +323,14 @@
     def _():
         result = (racc_s[...] + db_ref[...].astype(F32)).astype(BF)
         for e in range(groups):
-            r_ref[e] = result[e * room : (e + 1) * room]
+            block = result[e * room : (e + 1) * room]
+            if shift:
+                older = iota((8, 1), 0) < shift
+                head = jnp.where(older, r_in[e, :8].astype(F32), block[:8].astype(F32))
+                r_ref[e, :8] = head.astype(BF)
+                r_ref[e, 8:] = block[8:]
+            else:
+                r_ref[e] = block
         dy = dyb_ref[...].astype(F32).reshape(slots, width)
         dgate = jnp.sum(dy * result.astype(F32), axis=1, keepdims=True).reshape(groups, room, 1)
         spread = jnp.where(
@@ -310,7 +341,7 @@
         tail = jnp.zeros((groups, 1, width - 2 * LANES), F32)
         as_row = jnp.concatenate([high, as_row - high, tail], axis=2)
         back = dacc_s[...].reshape(groups, room, width)
-        back = jnp.where(iota((groups, room, 1), 1) == capacity, as_row, back).astype(BF)
+        back = jnp.where(iota((groups, room, 1), 1) == room - 1, as_row, back).astype(BF)
         for e in range(groups):
             dbuf_ref[e] = back[e]
 
@@ -375,7 +406,7 @@
         (slot_of == pcol_ref[0, :, 0:1]) | (slot_of == pcol_ref[0, :, 1:2]), 1.0, 0.0
     ).astype(BF)
     from_experts = mm(hot, back_rows)
-    spare = jnp.where(iota((experts, room, 1), 1) == capacity, dback[:, :, : 2 * LANES], 0.0)
+    spare = jnp.where(iota((experts, room, 1), 1) == room - 1, dback[:, :, : 2 * LANES], 0.0)
     spare = jnp.sum(spare, axis=1)
     spare = jnp.concatenate(
         [spare, jnp.zeros((LANES - experts, 2 * LANES), F32)], axis=0
@@ -584,7 +615,9 @@
     experts = router_weight.shape[1]
     hidden = up_weight.shape[2]
     capacity = (5 * tokens * TOP + 4 * experts - 1) // (4 * experts)
-    room = (capacity + 1 + 7) // 8 * 8
+    room = (capacity + window(capacity, MICRO - 1)[1] + 8) // 8 * 8
+    assert all(window(capacity, mb)[1] + capacity < room for mb in range(MICRO))
+    assert window(capacity, 1)[0] + room <= window(capacity, 2)[0] + 8
     slots = experts * room
     assert up_weight.shape[0] == 1 and experts == dp_count
     assert experts + VEC <= LANES and capacity <= LANES
@@ -602,6 +635,12 @@
 
     def block_spec(mb):
         return pl.BlockSpec((experts, room, width), lambda i: (0, mb, 0))
+
+    def window_spec(mb=None):
+        def at(i):
+            return (0, (capacity * (i if mb is None else mb)) // 8 * 8, 0)
+
+        return pl.BlockSpec((pl.Element(experts), pl.Element(room), pl.Element(width)), at)
 
     any_spec = pl.BlockSpec(memory_space=pl.ANY)
     other_spec = lambda mb: pl.BlockSpec(
@@ -616,7 +655,7 @@
     )
     misc_spec = pl.BlockSpec((width, LANES), lambda i: (0, 4 * width // LANES))
     moved = struct((experts, room, width), BF)
-    merged = struct((experts, MICRO * room, width), BF)
+    merged = struct((experts, window(capacity, MICRO - 1)[0] + room, width), BF)
     tailed = struct((experts, (MICRO - 1) * room, width), BF)
 
     def seq_shift(array, j):
@@ -628,14 +667,14 @@
         others.append(moved_images)
 
     sent_dy, prow, pcol = pl.pallas_call(
-        functools.partial(place_kernel, experts, room),
+        functools.partial(place_kernel, experts, room, capacity),
         grid=(MICRO,),
         in_specs=[
             pl.BlockSpec((1, 1, 1, TOP, tokens), lambda i: (0, i, 0, 0, 0)),
             pl.BlockSpec((count, local_len, width), lambda i: (i, 0, 0)),
         ],
         out_specs=[
-            pl.BlockSpec((experts, room, width), lambda i: (0, i, 0)),
+            pl.BlockSpec(merged.shape, lambda i: (0, 0, 0)),
             pl.BlockSpec((1, TOP, tokens), lambda i: (i, 0, 0)),
             pl.BlockSpec((1, tokens, 8), lambda i: (i, 0, 0)),
         ],
@@ -666,7 +705,8 @@
 
     def gather_rows(own, gate):
         quarter = dp_count // 4
-        held = [jnp.stack([own, *[across(own, k * quarter) for k in (1, 2, 3)]])]
+        pieces = [own, *[across(own, k * quarter) for k in (1, 2, 3)]]
+        held = [jnp.stack(pieces)]
         offsets = [[0, quarter, 2 * quarter, 3 * quarter]]
         for bit in reversed(range(bits - 2)):
             if bit == 0:
@@ -682,7 +722,7 @@
             compiler_params=params(),
             cost_estimate=cost(3),
             name="assemble",
-        )(meta, *held), held[0]
+        )(meta, *held), pieces[1:]
 
     def scatter_rows(total, far):
         me = lax.axis_index("dp")
@@ -693,6 +733,8 @@
             give = lax.dynamic_index_in_dim(value, 1 - mine, 1, keepdims=False)
             give = give.astype(BF)
             value = keep.astype(F32) + across(give, 1 << bit).astype(F32)
+            if bit == 0:
+                mid = value
             if bit < bits - 3:
                 value = value.reshape(-1, 2, shard, packed_width)
         value = after(value, *far)
@@ -703,7 +745,7 @@
                 value, lax.bitwise_xor(high, offset), 0, keepdims=False
             )
             result = result + across(give.astype(BF), offset << (bits - 2)).astype(F32)
-        return result, value
+        return result, mid, value
 
     pack_args = (qkv_weight, proj_weight, router_weight.T, vectors)
     packed_shard = pl.pallas_call(
@@ -721,7 +763,7 @@
         return lax.all_to_all(array, "dp", split_axis=0, concat_axis=0, tiled=True)
 
     packed, near = gather_rows(packed_shard, others[1])
-    dyb = exchange(after(sent_dy, near, others[0]))
+    dyb = exchange(after(sent_dy, *near, others[0]))
 
     def forward(mb):
         cfg = (count, local_len, seq_count, width, experts, room)
@@ -762,13 +804,13 @@
     def expert(mb, buf, results, tail_back, totals):
         first = mb == 0
         last = mb == MICRO - 1
-        cfg = (experts, room, capacity, width)
+        cfg = (experts, room, capacity, window(capacity, mb)[1], width)
         wide = lambda: pl.BlockSpec((width, FF_BLOCK), lambda i: (0, i))
         thin = lambda: pl.BlockSpec((1, FF_BLOCK), lambda i: (0, i))
         in_specs = [
             smem_spec(),
             full((experts, room, width)),
-            block_spec(mb),
+            window_spec(mb),
             misc_spec,
             pl.BlockSpec((1, width, FF_BLOCK), lambda i: (0, 0, i)),
             thin(),
@@ -781,7 +823,7 @@
         if not first:
             aliases = {len(args): 0}
             aliases.update({len(args) + 1 + j: 2 + j for j in range(4)})
-            in_specs += [any_spec, *total_specs]
+            in_specs += [window_spec(mb), *total_specs]
             args += [results, *totals]
         if mb >= 2:
             aliases[len(args)] = 1
@@ -791,7 +833,7 @@
             functools.partial(expert_kernel, cfg, first, last),
             grid=(hidden // FF_BLOCK,),
             in_specs=in_specs,
-            out_specs=[block_spec(mb), block_spec(max(mb - 1, 0)), *total_specs]
+            out_specs=[window_spec(mb), block_spec(max(mb - 1, 0)), *total_specs]
             + ([early_spec(), late_spec()] * 2 if last else []),
             out_shape=[
                 merged,
@@ -904,7 +946,7 @@
             functools.partial(mix_kernel, cfg),
             grid=(MICRO,),
             in_specs=[
-                pl.BlockSpec((experts, room, width), lambda i: (0, i, 0)),
+                window_spec(),
                 pl.BlockSpec((1, tokens, 8), lambda i: (i, 0, 0)),
                 *[full(t.shape) for t in tables],
             ],
@@ -964,9 +1006,9 @@
     back = exchange(after(results, dbacks[1]))
     first, far = (), ()
     if arrived:
-        first, far = (arrived[2],), (arrived[3], gots[0], gots[1])
-    shards, late = scatter_rows(after(dense[0], *first), (*far, back))
-    owns = [after(own, late) for own in owns]
+        first, far = (arrived[2], arrived[3]), (gots[0], gots[1])
+    shards, mid, late = scatter_rows(after(dense[0], *first), (*far, back))
+    owns = [after(own, late if mb == MICRO - 1 else mid) for mb, own in enumerate(owns)]
     grads = None
     for mb in range(MICRO):
         grads = finish(mb, owns[mb], gots[mb], dms[mb], grads)
@@ -986,7 +1028,7 @@
             compiler_params=params(),
             cost_estimate=cost(8),
             name="sum_experts",
-        )(gup, gdn, *arrived)
+        )(after(gup, mid), gdn, *arrived)
     else:
         sums = [lax.psum(piece, "seq").astype(F32) for piece in pieces]
         final_up = jnp.concatenate(sums[:2], axis=1)[None]

time: 360 us -> 384 us (1.067)
  the two profiles are of different devices: /device:TPU:0 before, /device:TPU:12 now
where the time goes in v4:
time: 384 us; the launch traced here: 377 us
  Pallas kernels  177 us (46%)
  waiting for transfers between devices  124 us (32%)
  starting transfers between devices  62 us (16%)
  local copies, waits for them, and re-layouts  8.87 us (2%)
    pallas_call x3, Pallas kernels, expert(): pl.pallas_call(functools.partial(expert_kernel, cfg, first, last), grid=(...  59.5 us
    pallas_call x3, Pallas kernels, backward(): pl.pallas_call(functools.partial(backward_kernel, cfg, mb, first, last),...  51.7 us
    all_to_all x7, waiting for transfers between devices, exchange(): return lax.all_to_all(array, 'dp', split_axis=0, concat_axis=0, tiled=True)  49.9 us
    all_to_all x7, starting transfers between devices, exchange(): return lax.all_to_all(array, 'dp', split_axis=0, concat_axis=0, tiled=True)  39.7 us
    pallas_call x3, Pallas kernels, forward(): pl.pallas_call(functools.partial(forward_kernel, cfg, mb), grid=(1,), in_...  33.1 us
    ppermute x11, waiting for transfers between devices, across(): return lax.ppermute(value, 'dp', [(i, i ^ offset) for i in range(dp_count)])  26.5 us
    ppermute x4, waiting for transfers between devices, on_device(): arrived = [lax.ppermute(piece, 'seq', swap) for piece in pieces]  20.9 us
    ppermute x2, waiting for transfers between devices, seq_shift(): lax.ppermute(array, 'seq', [((i + j) % seq_count, i) for i in range(seq_c...  14.5 us
  transfers between devices with their start and end apart: 29, of which 19 were waited for; matrix products, arithmetic and copies ran while one was open for 1% of the time, Pallas kernels for 47%

profile of v4, /device:TPU:12, one launch (start us, length us, event | category | flops | bytes accessed | tf_op | source)
XLA Modules:
  0.0 377.0 jit_solution(462698676188799479)
XLA Ops:
  0.7 1.4 concatenate.14.vec_ref
  2.1 1.7 pack.1
  4.2 2.6 collective-permute-start.2
  7.3 1.6 collective-permute-start.7
  8.8 6.0 %place.1 = (bf16[16,152,512]{2,1,0:T(8,128)(2,1)}, s32[3,2,320]{2,1,0:T(2,128)}, s32[3,320,8]{2,1,0:T(8,128)}) custom-call(s32[1,3,1,2,320]{4,3,2,1,0:T(2,128)} %bitcast.76, bf16[3,320,512]{2,1,0:T(8,128)(2,1)} %refs_7_.11), custom_call_target="tpu_custom_call" | custom-call | flops 8000000000 | bytes 16000000 | tf_op jit(solution)/shard_map/place/pallas_call | solution.py:669
  14.8 2.1 collective-permute-done.2
  16.9 2.6 collective-permute-done.3
  19.6 0.7 copy-done.15
  20.3 5.2 %all-to-all-start.1 = ((bf16[16,152,512]{2,1,0:T(8,128)(2,1)}), bf16[16,152,512]{2,1,0:T(8,128)(2,1)}, u32[]{:S(2)}, u32[]{:S(2)}) async-start(bf16[16,152,512]{2,1,0:T(8,128)(2,1)} %get-tuple-element.105), calls=%async_computation.1 | async-start | bytes 4980736 | tf_op jit(solution)/shard_map/all_to_all | solution.py:763
  25.6 1.6 collective-permute-start
  27.9 14.5 %collective-permute-done = bf16[2,320,512]{2,1,0:T(8,128)(2,1)S(1)} collective-permute-done((bf16[2,320,512]{2,1,0:T(8,128)(2,1)S(1)}, bf16[2,320,512]{2,1,0:T(8,128)(2,1)S(1)}, u32[]{:S(2)}, u32[]{:S(2)}) %collective-permute-start) | collective-permute-done | bytes 655392 | tf_op jit(solution)/shard_map/ppermute | solution.py:662
  42.4 13.6 %collective-permute-done.4.refs_1_ = bf16[4,32,2176]{2,1,0:T(8,128)(2,1)S(1)} collective-permute-done((bf16[4,32,2176]{2,1,0:T(8,128)(2,1)S(1)}, bf16[4,32,2176]{2,1,0:T(8,128)(2,1)S(1)}, u32[]{:S(2)}, u32[]{:S(2)}) %collective-permute-start.4) | collective-permute-done | bytes 557088 | tf_op jit(solution)/shard_map/ppermute | solution.py:704
  56.0 0.7 pad_add_fusion.meta_ref.refs_0_
  56.7 1.3 collective-permute-done.6.refs_3_
  58.0 0.8 copy-done.14
  58.8 3.1 assemble.1.w_ref.refs_3_.refs_9_.wm_ref
  61.9 11.0 %forward.5 = (bf16[16,56,512]{2,1,0:T(8,128)(2,1)}, f32[320,512]{1,0:T(8,128)}, f32[320,128]{1,0:T(8,128)}, bf16[320,512]{1,0:T(8,128)(2,1)}, bf16[512,320]{1,0:...) custom-call(s32[2]{0:T(128)} %pad_add_fusion.meta_ref.refs_0_, ...), custom_call_target="tpu_custom_call" | custom-call | flops 11000000512 | bytes 22000000 | tf_op jit(solution)/shard_map/forward/pallas_call | solution.py:782
  72.9 8.4 %all-to-all-done.1.refs_2_ = bf16[16,152,512]{2,1,0:T(8,128)(2,1)} async-done(((bf16[16,152,512]{2,1,0:T(8,128)(2,1)}), bf16[16,152,512]{2,1,0:T(8,128)(2,1)}, u32[]{:S(2)}, u32[]{:S(2)}) %all-to-all-start.1) | async-done | bytes 2490400 | tf_op jit(solution)/shard_map/all_to_all | solution.py:763
  81.2 5.7 %all-to-all-start.3 = ((bf16[16,56,512]{2,1,0:T(8,128)(2,1)}), bf16[16,56,512]{2,1,0:T(8,128)(2,1)S(1)}, u32[]{:S(2)}, u32[]{:S(2)}) async-start(bf16[16,56,512]{2,1,0:T(8,128)(2,1)} %get-tuple-element.108), calls=%async_computation.3 | async-start | bytes 1835008 | tf_op jit(solution)/shard_map/all_to_all | solution.py:763
  87.0 11.0 %forward.4 = (bf16[16,56,512]{2,1,0:T(8,128)(2,1)}, f32[320,512]{1,0:T(8,128)}, f32[320,128]{1,0:T(8,128)}, bf16[320,512]{1,0:T(8,128)(2,1)}, bf16[512,320]{1,0:...) custom-call(s32[2]{0:T(128)} %pad_add_fusion.meta_ref.refs_0_, ...), custom_call_target="tpu_custom_call" | custom-call | flops 11000000512 | bytes 22000000 | tf_op jit(solution)/shard_map/forward/pallas_call | solution.py:782
  98.0 11.0 %forward.3 = (bf16[16,56,512]{2,1,0:T(8,128)(2,1)}, f32[320,512]{1,0:T(8,128)}, f32[320,128]{1,0:T(8,128)}, bf16[320,512]{1,0:T(8,128)(2,1)}, bf16[512,320]{1,0:...) custom-call(s32[2]{0:T(128)} %pad_add_fusion.meta_ref.refs_0_, ...), custom_call_target="tpu_custom_call" | custom-call | flops 11000000512 | bytes 22000000 | tf_op jit(solution)/shard_map/forward/pallas_call | solution.py:782
  109.0 6.0 %all-to-all-start.2 = ((bf16[16,56,512]{2,1,0:T(8,128)(2,1)}), bf16[16,56,512]{2,1,0:T(8,128)(2,1)S(1)}, u32[]{:S(2)}, u32[]{:S(2)}) async-start(bf16[16,56,512]{2,1,0:T(8,128)(2,1)} %get-tuple-element.106), calls=%async_computation.2 | async-start | bytes 1835008 | tf_op jit(solution)/shard_map/all_to_all | solution.py:763
  115.1 18.6 %expert.3 = (bf16[16,152,512]{2,1,0:T(8,128)(2,1)}, bf16[16,56,512]{2,1,0:T(8,128)(2,1)}, f32[512,2048]{1,0:T(8,128)}, f32[512,2048]{1,0:T(8,128)}, f32[1,2048]{1,0:T(1,128)}, /*index=5*/f32[1,512]{1,0:T(1,128)}) custom-call(s32[2]{0:T(128)} %pad_add_fusion.meta_ref.refs_0_, bf16[16,56,512]{2,1,0:T(8,128)(2,1)} %copy-done.4, ...), custom_call_target="tpu_custom_call" | custom-call | flops 19000000512 | bytes 38000000 | tf_op jit(solution)/shard_map/expert/pallas_call | solution.py:832
  133.7 3.1 all-to-all-done.2.refs_1_
  136.8 5.4 %all-to-all-start = ((bf16[16,56,512]{2,1,0:T(8,128)(2,1)}), bf16[16,56,512]{2,1,0:T(8,128)(2,1)S(1)}, u32[]{:S(2)}, u32[]{:S(2)}) async-start(bf16[16,56,512]{2,1,0:T(8,128)(2,1)} %get-tuple-element.103), calls=%async_computation | async-start | bytes 1835008 | tf_op jit(solution)/shard_map/all_to_all | solution.py:763
  142.2 19.8 %expert.4 = (bf16[16,152,512]{2,1,0:T(8,128)(2,1)}, bf16[16,112,512]{2,1,0:T(8,128)(2,1)}, f32[512,2048]{1,0:T(8,128)}, f32[512,2048]{1,0:T(8,128)}, f32[1,2048]{1,0:T(1,128)}, /*index=5*/f32[1,512]{1,0:T(1,128)}) custom-call(s32[2]{0:T(128)} %pad_add_fusion.meta_ref.refs_0_, ...), custom_call_target="tpu_custom_call", output_to_operand_aliasing={{0}: (8, {}), {2}: (9, {}), {3}: (10, {}), {4}: (11, {}), {... | custom-call | flops 19000000512 | bytes 38000000 | tf_op jit(solution)/shard_map/expert/pallas_call | solution.py:832
  162.0 1.9 all-to-all-done.refs_1_
  163.9 5.1 %all-to-all-start.6 = ((bf16[16,56,512]{2,1,0:T(8,128)(2,1)}), bf16[16,56,512]{2,1,0:T(8,128)(2,1)S(1)}, u32[]{:S(2)}, u32[]{:S(2)}) async-start(bf16[16,56,512]{2,1,0:T(8,128)(2,1)} %get-tuple-element.146), calls=%async_computation.6 | async-start | bytes 1835008 | tf_op jit(solution)/shard_map/all_to_all | solution.py:763
  169.0 21.1 %expert.5 = (bf16[16,152,512]{2,1,0:T(8,128)(2,1)}, bf16[16,112,512]{2,1,0:T(8,128)(2,1)}, f32[512,2048]{1,0:T(8,128)}, f32[512,2048]{1,0:T(8,128)}, f32[1,2048]...) custom-call(s32[2]{0:T(128)} %pad_add_fusion.meta_ref.refs_0_, ...), custom_call_target="tpu_custom_call", output_to_operand_aliasing={{0}: (8, {}), {2}: (9, {}), {3}: (10, {}), {4}: (11, {}), {... | custom-call | flops 19000000512 | bytes 38000000 | tf_op jit(solution)/shard_map/expert/pallas_call | solution.py:832
  190.1 0.7 all-to-all-done.6.refs_2_
  190.7 5.7 %all-to-all-start.4 = ((bf16[16,112,512]{2,1,0:T(8,128)(2,1)}), bf16[16,112,512]{2,1,0:T(8,128)(2,1)S(1)}, u32[]{:S(2)}, u32[]{:S(2)}) async-start(bf16[16,112,512]{2,1,0:T(8,128)(2,1)} %get-tuple-element.121), calls=%async_computation.4 | async-start | bytes 3670016 | tf_op jit(solution)/shard_map/all_to_all | solution.py:763
  196.4 1.6 collective-permute-start.8
  198.5 1.5 collective-permute-start.10
  200.5 16.8 %backward.3 = (f32[320,512]{1,0:T(8,128)}, bf16[1,320,512]{2,1,0:T(8,128)(2,1)}, f32[320,512]{1,0:T(8,128)}, f32[512,2048]{1,0:T(8,128)}, f32[128,512]{1,0:T(8,128)}) custom-call(s32[2]{0:T(128)} %pad_add_fusion.meta_ref.refs_0_, s32[3]{0:T(128)} %refs_1_.5, bf16[16,56,512]{2,1,0:T(8,128)(2,1)} %copy-done.3, ...), custom_call_target="tpu_custom_call" | custom-call | flops 16999999488 | bytes 34000000 | tf_op jit(solution)/shard_map/backward/pallas_call | solution.py:894
  217.3 5.5 %collective-permute-done.8.up_early = bf16[512,1024]{1,0:T(8,128)(2,1)} collective-permute-done((bf16[512,1024]{1,0:T(8,128)(2,1)}, bf16[512,1024]{1,0:T(8,128)(2,1)}, u32[]{:S(2)}, u32[]{:S(2)}) %collective-permute-start.8) | collective-permute-done | bytes 1048608 | tf_op jit(solution)/shard_map/ppermute | solution.py:981
  222.8 15.0 %all-to-all-done.4.refs_2_ = bf16[16,112,512]{2,1,0:T(8,128)(2,1)S(1)} async-done(((bf16[16,112,512]{2,1,0:T(8,128)(2,1)}), bf16[16,112,512]{2,1,0:T(8,128)(2,1)S(1)}, u32[]{:S(2)}, u32[]{:S(2)}) %all-to-all-start.4) | async-done | bytes 1835040 | tf_op jit(solution)/shard_map/all_to_all | solution.py:763
  237.8 1.2 copy-done
  239.1 17.5 %backward.4 = (f32[320,512]{1,0:T(8,128)}, bf16[1,320,512]{2,1,0:T(8,128)(2,1)}, f32[320,512]{1,0:T(8,128)}, f32[512,2048]{1,0:T(8,128)}, f32[128,512]{1,0:T(8,128)}) custom-call(s32[2]{0:T(128)} %pad_add_fusion.meta_ref.refs_0_, s32[3]{0:T(128)} %refs_1_.5, bf16[16,112,512]{2,1,0:T(8,128)(2,1)} %copy-done, ...), custom_call_target="tpu_custom_call", output_to_operand_aliasing={{3}: (17, {}), {4}: (18, {})} | custom-call | flops 16999999488 | bytes 34000000 | tf_op jit(solution)/shard_map/backward/pallas_call | solution.py:894
  256.6 17.4 %backward.5 = (f32[320,512]{1,0:T(8,128)}, bf16[1,320,512]{2,1,0:T(8,128)(2,1)}, f32[320,512]{1,0:T(8,128)}, bf16[512,2176]{1,0:T(8,128)(2,1)}, f32[128,512]{1,0:T(8,128)}) custom-call(s32[2]{0:T(128)} %pad_add_fusion.meta_ref.refs_0_, s32[3]{0:T(128)} %refs_1_.5, bf16[16,112,512]{2,1,0:T(8,128)(2,1)} %copy-done, ...), custom_call_target="tpu_custom_call" | custom-call | flops 1000000000 | bytes 2000000 | tf_op jit(solution)/shard_map/backward/pallas_call | solution.py:894
  274.0 15.4 %collective-permute-done.11.dn_late = bf16[512,1024]{1,0:T(8,128)(2,1)} collective-permute-done((bf16[512,1024]{1,0:T(8,128)(2,1)}, bf16[512,1024]{1,0:T(8,128)(2,1)}, u32[]{:S(2)}, u32[]{:S(2)}) %collective-permute-start.11) | collective-permute-done | bytes 1048608 | tf_op jit(solution)/shard_map/ppermute | solution.py:981
  289.4 6.6 %all-to-all-start.5 = ((bf16[16,152,512]{2,1,0:T(8,128)(2,1)}), bf16[16,152,512]{2,1,0:T(8,128)(2,1)}, u32[]{:S(2)}, u32[]{:S(2)}) async-start(bf16[16,152,512]{2,1,0:T(8,128)(2,1)} %get-tuple-element.124), calls=%async_computation.5 | async-start | bytes 4980736 | tf_op jit(solution)/shard_map/all_to_all | solution.py:763
  296.7 1.6 collective-permute-start.21
  298.3 2.2 collective-permute-done.21
  301.7 1.5 collective-permute-start.14
  303.7 1.5 collective-permute-start.16
  305.2 1.5 convert_add_fusion
  307.4 5.2 %collective-permute-done.14 = bf16[320,512]{1,0:T(8,128)(2,1)} collective-permute-done((bf16[320,512]{1,0:T(8,128)(2,1)}, bf16[320,512]{1,0:T(8,128)(2,1)}, u32[]{:S(2)}, u32[]{:S(2)}) %collective-permute-start.14) | collective-permute-done | bytes 327712 | tf_op jit(solution)/shard_map/ppermute | solution.py:999
  312.6 2.7 finish.3.refs_0_
  315.3 4.3 %collective-permute-done.15 = bf16[320,512]{1,0:T(8,128)(2,1)} collective-permute-done((bf16[320,512]{1,0:T(8,128)(2,1)}, bf16[320,512]{1,0:T(8,128)(2,1)}, u32[]{:S(2)}, u32[]{:S(2)}) %collective-permute-start.15) | collective-permute-done | bytes 327712 | tf_op jit(solution)/shard_map/ppermute | solution.py:999
  319.6 2.7 finish.4.refs_0_
  322.3 8.4 %sum_experts.1 = (f32[1,512,2048]{2,1,0:T(8,128)}, f32[1,2048,512]{2,1,0:T(8,128)}) custom-call(f32[512,2048]{1,0:T(8,128)} %get-tuple-element.179.gup_ref, f32[512,2048]{1,0:T(8,128)} %get-tuple-element.180.gdn_ref, bf16[512,1024]{1,0:T(8,128)(2,1)} %collective-permute-done.8.up_early, bf16[512,1024]{1,0:T(8,128)(2,1)} %collective-permute-done.9.up_late, ...), custom_call_target="tpu_custom_call" | custom-call | flops 8000000000 | bytes 16000000 | tf_op jit(solution)/shard_map/sum_experts/pallas_call | solution.py:1019
  330.7 20.8 %all-to-all-done.5.back_ref = bf16[16,152,512]{2,1,0:T(8,128)(2,1)} async-done(((bf16[16,152,512]{2,1,0:T(8,128)(2,1)}), bf16[16,152,512]{2,1,0:T(8,128)(2,1)}, u32[]{:S(2)}, u32[]{:S(2)}) %all-to-all-start.5) | async-done | bytes 2490400 | tf_op jit(solution)/shard_map/all_to_all | solution.py:763
  351.7 1.6 collective-permute-start.18
  353.3 1.9 collective-permute-start.19
  355.2 5.8 %mix.1 = bf16[3,320,512]{2,1,0:T(8,128)(2,1)} custom-call(bf16[16,152,512]{2,1,0:T(8,128)(2,1)} %all-to-all-done.5.back_ref, s32[3,320,8]{2,1,0:T(8,128)} %get-tuple-element.125.pcol_ref.refs_3_, f32[320,128]{1,0:T(8,128)} %get-tuple-element.126.refs_0_.refs_4_, f32[320,512]{1,0:T(8,128)} %get-tuple-element.127.refs_1_.refs_5_, ...), custom_call_target="tpu_custom_call" | custom-call | flops 7000000000 | bytes 14000000 | tf_op jit(solution)/shard_map/mix/pallas_call | solution.py:945
  361.0 2.2 collective-permute-done.18
  363.2 4.7 %collective-permute-done.19 = bf16[32,2176]{1,0:T(8,128)(2,1)S(1)} collective-permute-done((bf16[32,2176]{1,0:T(8,128)(2,1)S(1)}, bf16[32,2176]{1,0:T(8,128)(2,1)S(1)}, u32[]{:S(2)}, u32[]{:S(2)}) %collective-permute-start.19) | collective-permute-done | bytes 139296 | tf_op jit(solution)/shard_map/ppermute | solution.py:704
  367.9 1.6 collective-permute-start.20
  369.5 2.7 finish.5
  372.2 0.9 collective-permute-done.20
  373.1 0.8 slice_reduce_fusion
  373.9 0.7 slice.58
  374.6 0.6 slice.61
  375.2 0.7 copy.52
  (68 shorter events, 6.9 us)
Async XLA Ops:
  0.6 6.6 %copy-start.1 = (bf16[3,320,512]{2,1,0:T(8,128)(2,1)S(1)}, bf16[3,320,512]{2,1,0:T(8,128)(2,1)}, u32[]{:S(2)}) copy-start(bf16[3,320,512]{2,1,0:T(8,128)(2,1)} %x_ref.5) | copy-start | bytes 2949124
  3.7 11.1 %collective-permute-start.1 = (bf16[32,2176]{1,0:T(8,128)(2,1)}, bf16[32,2176]{1,0:T(8,128)(2,1)S(1)}, u32[]{:S(2)}, u32[]{:S(2)}) collective-permute-start(bf16[32,2176]{1,0:T(8,128)(2,1)} %pack.1), channel_id=1, source_target_pairs={{0,8},{2,10},{4,12},{6,14},{8,0},{10,2},{12,4},{14,6},{16,24},{18,... | collective-permute-start | bytes 417800 | tf_op jit(solution)/shard_map/ppermute | solution.py:704
  4.2 12.7 %collective-permute-start.2 = (bf16[32,2176]{1,0:T(8,128)(2,1)}, bf16[32,2176]{1,0:T(8,128)(2,1)S(1)}, u32[]{:S(2)}, u32[]{:S(2)}) collective-permute-start(bf16[32,2176]{1,0:T(8,128)(2,1)} %pack.1), channel_id=1, source_target_pairs={{0,16},{2,18},{4,20},{6,22},{8,24},{10,26},{12,28},{14,30},{16,0},... | collective-permute-start | bytes 417800 | tf_op jit(solution)/shard_map/ppermute | solution.py:704
  6.8 12.8 %collective-permute-start.3 = (bf16[32,2176]{1,0:T(8,128)(2,1)}, bf16[32,2176]{1,0:T(8,128)(2,1)S(1)}, u32[]{:S(2)}, u32[]{:S(2)}) collective-permute-start(bf16[32,2176]{1,0:T(8,128)(2,1)} %pack.1), channel_id=1, source_target_pairs={{0,24},{2,26},{4,28},{6,30},{8,16},{10,18},{12,20},{14,22},{16,8},... | collective-permute-start | bytes 417800 | tf_op jit(solution)/shard_map/ppermute | solution.py:704
  7.3 12.3 %collective-permute-start.7 = (bf16[1,320,512]{2,1,0:T(8,128)(2,1)S(1)}, bf16[1,320,512]{2,1,0:T(8,128)(2,1)S(1)}, u32[]{:S(2)}, u32[]{:S(2)}) collective-permute-start(bf16[1,320,512]{2,1,0:T(8,128)(2,1)S(1)} %slice.43), channel_id=1, source_target_pairs={{1,0},{0,1},{3,2},{2,3},{5,4},{4,5},{7,6},{6,7},{9,8},{8,9},{11,10... | collective-permute-start | bytes 983048 | tf_op jit(solution)/shard_map/ppermute | solution.py:662
  19.6 0.8 copy-start.15
  19.6 7.6 %copy-start.9 = (bf16[32,2176]{1,0:T(8,128)(2,1)S(1)}, bf16[32,2176]{1,0:T(8,128)(2,1)}, u32[]{:S(2)}) copy-start(bf16[32,2176]{1,0:T(8,128)(2,1)} %pack.1) | copy-start | bytes 417796
  20.3 60.9 %all-to-all-start.1 = ((bf16[16,152,512]{2,1,0:T(8,128)(2,1)}), bf16[16,152,512]{2,1,0:T(8,128)(2,1)}, u32[]{:S(2)}, u32[]{:S(2)}) async-start(bf16[16,152,512]{2,1,0:T(8,128)(2,1)} %get-tuple-element.105), calls=%async_computation.1 | async-start | bytes 4980736 | tf_op jit(solution)/shard_map/all_to_all | solution.py:763
  25.6 16.8 %collective-permute-start = (bf16[2,320,512]{2,1,0:T(8,128)(2,1)S(1)}, bf16[2,320,512]{2,1,0:T(8,128)(2,1)S(1)}, u32[]{:S(2)}, u32[]{:S(2)}) collective-permute-start(bf16[2,320,512]{2,1,0:T(8,128)(2,1)S(1)} %slice.42), channel_id=1, source_target_pairs={{1,0},{0,1},{3,2},{2,3},{5,4},{4,5},{7,6},{6,7},{9,8},{8,9},{11,10... | collective-permute-start | bytes 1966088 | tf_op jit(solution)/shard_map/ppermute | solution.py:662
  27.2 30.7 %copy-start.8 = (bf16[4,32,2176]{2,1,0:T(8,128)(2,1)}, bf16[4,32,2176]{2,1,0:T(8,128)(2,1)S(1)}, u32[]{:S(2)}) copy-start(bf16[4,32,2176]{2,1,0:T(8,128)(2,1)S(1)} %pad_maximum_fusion.refs_0_) | copy-start | bytes 1671172
  27.2 28.8 %collective-permute-start.4 = (bf16[4,32,2176]{2,1,0:T(8,128)(2,1)S(1)}, bf16[4,32,2176]{2,1,0:T(8,128)(2,1)S(1)}, u32[]{:S(2)}, u32[]{:S(2)}) collective-permute-start(bf16[4,32,2176]{2,1,0:T(8,128)(2,1)S(1)} %pad_maximum_fusion.refs_0_), channel_id=1, source_target_pairs={{0,4},{2,6},{4,0},{6,2},{8,12},{10,14},{12,8},{14,10},{16,20},{18,... | collective-permute-start | bytes 1671176 | tf_op jit(solution)/shard_map/ppermute | solution.py:704
  27.9 28.8 %collective-permute-start.5 = (bf16[4,32,2176]{2,1,0:T(8,128)(2,1)S(1)}, bf16[4,32,2176]{2,1,0:T(8,128)(2,1)S(1)}, u32[]{:S(2)}, u32[]{:S(2)}) collective-permute-start(bf16[4,32,2176]{2,1,0:T(8,128)(2,1)S(1)} %pad_maximum_fusion.refs_0_), channel_id=1, source_target_pairs={{0,2},{2,0},{4,6},{6,4},{8,10},{10,8},{12,14},{14,12},{16,18},{18,... | collective-permute-start | bytes 1671176 | tf_op jit(solution)/shard_map/ppermute | solution.py:704
  42.4 19.5 %copy-start.7 = (bf16[2,320,512]{2,1,0:T(8,128)(2,1)}, bf16[2,320,512]{2,1,0:T(8,128)(2,1)S(1)}, u32[]{:S(2)}) copy-start(bf16[2,320,512]{2,1,0:T(8,128)(2,1)S(1)} %collective-permute-done) | copy-start | bytes 1966084
  56.0 2.0 copy-start.12
  56.0 2.0 collective-permute-start.6
  56.7 1.3 copy-start.13
  58.0 0.8 copy-start.14
  81.2 27.8 %all-to-all-start.3 = ((bf16[16,56,512]{2,1,0:T(8,128)(2,1)}), bf16[16,56,512]{2,1,0:T(8,128)(2,1)S(1)}, u32[]{:S(2)}, u32[]{:S(2)}) async-start(bf16[16,56,512]{2,1,0:T(8,128)(2,1)} %get-tuple-element.108), calls=%async_computation.3 | async-start | bytes 1835008 | tf_op jit(solution)/shard_map/all_to_all | solution.py:763
  109.0 6.1 %copy-start.4 = (bf16[16,56,512]{2,1,0:T(8,128)(2,1)}, bf16[16,56,512]{2,1,0:T(8,128)(2,1)S(1)}, u32[]{:S(2)}) copy-start(bf16[16,56,512]{2,1,0:T(8,128)(2,1)S(1)} %all-to-all-done.3.refs_1_) | copy-start | bytes 2752516
  109.0 27.8 %all-to-all-start.2 = ((bf16[16,56,512]{2,1,0:T(8,128)(2,1)}), bf16[16,56,512]{2,1,0:T(8,128)(2,1)S(1)}, u32[]{:S(2)}, u32[]{:S(2)}) async-start(bf16[16,56,512]{2,1,0:T(8,128)(2,1)} %get-tuple-element.106), calls=%async_computation.2 | async-start | bytes 1835008 | tf_op jit(solution)/shard_map/all_to_all | solution.py:763
  136.8 5.4 %copy-start.6 = (bf16[16,56,512]{2,1,0:T(8,128)(2,1)}, bf16[16,56,512]{2,1,0:T(8,128)(2,1)S(1)}, u32[]{:S(2)}) copy-start(bf16[16,56,512]{2,1,0:T(8,128)(2,1)S(1)} %all-to-all-done.2.refs_1_) | copy-start | bytes 2752516
  136.8 27.0 %all-to-all-start = ((bf16[16,56,512]{2,1,0:T(8,128)(2,1)}), bf16[16,56,512]{2,1,0:T(8,128)(2,1)S(1)}, u32[]{:S(2)}, u32[]{:S(2)}) async-start(bf16[16,56,512]{2,1,0:T(8,128)(2,1)} %get-tuple-element.103), calls=%async_computation | async-start | bytes 1835008 | tf_op jit(solution)/shard_map/all_to_all | solution.py:763
  163.9 5.1 %copy-start.5 = (bf16[16,56,512]{2,1,0:T(8,128)(2,1)}, bf16[16,56,512]{2,1,0:T(8,128)(2,1)S(1)}, u32[]{:S(2)}) copy-start(bf16[16,56,512]{2,1,0:T(8,128)(2,1)S(1)} %all-to-all-done.refs_1_) | copy-start | bytes 2752516
  163.9 26.9 %all-to-all-start.6 = ((bf16[16,56,512]{2,1,0:T(8,128)(2,1)}), bf16[16,56,512]{2,1,0:T(8,128)(2,1)S(1)}, u32[]{:S(2)}, u32[]{:S(2)}) async-start(bf16[16,56,512]{2,1,0:T(8,128)(2,1)} %get-tuple-element.146), calls=%async_computation.6 | async-start | bytes 1835008 | tf_op jit(solution)/shard_map/all_to_all | solution.py:763
  190.7 9.8 %copy-start.3 = (bf16[16,56,512]{2,1,0:T(8,128)(2,1)}, bf16[16,56,512]{2,1,0:T(8,128)(2,1)S(1)}, u32[]{:S(2)}) copy-start(bf16[16,56,512]{2,1,0:T(8,128)(2,1)S(1)} %all-to-all-done.6.refs_2_) | copy-start | bytes 2752516
  190.7 47.1 %all-to-all-start.4 = ((bf16[16,112,512]{2,1,0:T(8,128)(2,1)}), bf16[16,112,512]{2,1,0:T(8,128)(2,1)S(1)}, u32[]{:S(2)}, u32[]{:S(2)}) async-start(bf16[16,112,512]{2,1,0:T(8,128)(2,1)} %get-tuple-element.121), calls=%async_computation.4 | async-start | bytes 3670016 | tf_op jit(solution)/shard_map/all_to_all | solution.py:763
  196.4 26.4 %collective-permute-start.8 = (bf16[512,1024]{1,0:T(8,128)(2,1)}, bf16[512,1024]{1,0:T(8,128)(2,1)}, u32[]{:S(2)}, u32[]{:S(2)}) collective-permute-start(bf16[512,1024]{1,0:T(8,128)(2,1)} %get-tuple-element.122), channel_id=1, source_target_pairs={{0,1},{1,0},{2,3},{3,2},{4,5},{5,4},{6,7},{7,6},{8,9},{9,8},{10,11... | collective-permute-start | bytes 3145736 | tf_op jit(solution)/shard_map/ppermute | solution.py:981
  198.0 58.6 %collective-permute-start.9 = (bf16[512,1024]{1,0:T(8,128)(2,1)}, bf16[512,1024]{1,0:T(8,128)(2,1)}, u32[]{:S(2)}, u32[]{:S(2)}) collective-permute-start(bf16[512,1024]{1,0:T(8,128)(2,1)} %get-tuple-element.158), channel_id=1, source_target_pairs={{0,1},{1,0},{2,3},{3,2},{4,5},{5,4},{6,7},{7,6},{8,9},{9,8},{10,11... | collective-permute-start | bytes 3145736 | tf_op jit(solution)/shard_map/ppermute | solution.py:981
  198.5 75.5 %collective-permute-start.10 = (bf16[512,1024]{1,0:T(8,128)(2,1)}, bf16[512,1024]{1,0:T(8,128)(2,1)}, u32[]{:S(2)}, u32[]{:S(2)}) collective-permute-start(bf16[512,1024]{1,0:T(8,128)(2,1)} %get-tuple-element.163), channel_id=1, source_target_pairs={{0,1},{1,0},{2,3},{3,2},{4,5},{5,4},{6,7},{7,6},{8,9},{9,8},{10,11... | collective-permute-start | bytes 3145736 | tf_op jit(solution)/shard_map/ppermute | solution.py:981
  200.0 89.4 %collective-permute-start.11 = (bf16[512,1024]{1,0:T(8,128)(2,1)}, bf16[512,1024]{1,0:T(8,128)(2,1)}, u32[]{:S(2)}, u32[]{:S(2)}) collective-permute-start(bf16[512,1024]{1,0:T(8,128)(2,1)} %get-tuple-element.164), channel_id=1, source_target_pairs={{0,1},{1,0},{2,3},{3,2},{4,5},{5,4},{6,7},{7,6},{8,9},{9,8},{10,11... | collective-permute-start | bytes 3145736 | tf_op jit(solution)/shard_map/ppermute | solution.py:981
  237.8 1.2 copy-start
  289.4 6.6 %copy-start.2 = (bf16[512,2176]{1,0:T(8,128)(2,1)S(1)}, bf16[512,2176]{1,0:T(8,128)(2,1)}, u32[]{:S(2)}) copy-start(bf16[512,2176]{1,0:T(8,128)(2,1)} %get-tuple-element.165) | copy-start | bytes 6684676
  289.4 62.2 %all-to-all-start.5 = ((bf16[16,152,512]{2,1,0:T(8,128)(2,1)}), bf16[16,152,512]{2,1,0:T(8,128)(2,1)}, u32[]{:S(2)}, u32[]{:S(2)}) async-start(bf16[16,152,512]{2,1,0:T(8,128)(2,1)} %get-tuple-element.124), calls=%async_computation.5 | async-start | bytes 4980736 | tf_op jit(solution)/shard_map/all_to_all | solution.py:763
  296.0 0.7 copy-start.10
  296.0 0.7 copy-start.11
  296.1 9.1 %collective-permute-start.12 = (bf16[8,32,2176]{2,1,0:T(8,128)(2,1)S(1)}, bf16[8,32,2176]{2,1,0:T(8,128)(2,1)S(1)}, u32[]{:S(2)}, u32[]{:S(2)}) collective-permute-start(bf16[8,32,2176]{2,1,0:T(8,128)(2,1)S(1)} %dynamic-slice_bitcast_fusion), channel_id=1, source_target_pairs={{0,2},{2,0},{4,6},{6,4},{8,10},{10,8},{12,14},{14,12},{16,18},{18,... | collective-permute-start | bytes 3342344 | tf_op jit(solution)/shard_map/ppermute | solution.py:704
  296.7 3.7 collective-permute-start.21
  301.7 10.9 %collective-permute-start.14 = (bf16[320,512]{1,0:T(8,128)(2,1)}, bf16[320,512]{1,0:T(8,128)(2,1)}, u32[]{:S(2)}, u32[]{:S(2)}) collective-permute-start(bf16[320,512]{1,0:T(8,128)(2,1)} %bitcast.74), channel_id=1, source_target_pairs={{0,1},{1,0},{2,3},{3,2},{4,5},{5,4},{6,7},{7,6},{8,9},{9,8},{10,11... | collective-permute-start | bytes 983048 | tf_op jit(solution)/shard_map/ppermute | solution.py:999
  303.1 16.4 %collective-permute-start.15 = (bf16[320,512]{1,0:T(8,128)(2,1)}, bf16[320,512]{1,0:T(8,128)(2,1)}, u32[]{:S(2)}, u32[]{:S(2)}) collective-permute-start(bf16[320,512]{1,0:T(8,128)(2,1)} %bitcast.75), channel_id=1, source_target_pairs={{0,1},{1,0},{2,3},{3,2},{4,5},{5,4},{6,7},{7,6},{8,9},{9,8},{10,11... | collective-permute-start | bytes 983048 | tf_op jit(solution)/shard_map/ppermute | solution.py:999
  303.7 65.8 %collective-permute-start.16 = (bf16[320,512]{1,0:T(8,128)(2,1)}, bf16[320,512]{1,0:T(8,128)(2,1)}, u32[]{:S(2)}, u32[]{:S(2)}) collective-permute-start(bf16[320,512]{1,0:T(8,128)(2,1)} %bitcast.73), channel_id=1, source_target_pairs={{0,1},{1,0},{2,3},{3,2},{4,5},{5,4},{6,7},{7,6},{8,9},{9,8},{10,11... | collective-permute-start | bytes 983048 | tf_op jit(solution)/shard_map/ppermute | solution.py:999
  306.7 23.9 %collective-permute-start.13 = (bf16[4,32,2176]{2,1,0:T(8,128)(2,1)S(1)}, bf16[4,32,2176]{2,1,0:T(8,128)(2,1)S(1)}, u32[]{:S(2)}, u32[]{:S(2)}) collective-permute-start(bf16[4,32,2176]{2,1,0:T(8,128)(2,1)S(1)} %fusion), channel_id=1, source_target_pairs={{0,4},{2,6},{4,0},{6,2},{8,12},{10,14},{12,8},{14,10},{16,20},{18,... | collective-permute-start | bytes 1671176 | tf_op jit(solution)/shard_map/ppermute | solution.py:704
  351.6 9.4 %collective-permute-start.17 = (bf16[32,2176]{1,0:T(8,128)(2,1)S(1)}, bf16[32,2176]{1,0:T(8,128)(2,1)S(1)}, u32[]{:S(2)}, u32[]{:S(2)}) collective-permute-start(bf16[32,2176]{1,0:T(8,128)(2,1)S(1)} %get-tuple-element.239), channel_id=1, source_target_pairs={{0,8},{2,10},{4,12},{6,14},{8,0},{10,2},{12,4},{14,6},{16,24},{18,... | collective-permute-start | bytes 417800 | tf_op jit(solution)/shard_map/ppermute | solution.py:704
  351.7 11.5 %collective-permute-start.18 = (bf16[32,2176]{1,0:T(8,128)(2,1)S(1)}, bf16[32,2176]{1,0:T(8,128)(2,1)S(1)}, u32[]{:S(2)}, u32[]{:S(2)}) collective-permute-start(bf16[32,2176]{1,0:T(8,128)(2,1)S(1)} %get-tuple-element.241), channel_id=1, source_target_pairs={{0,16},{2,18},{4,20},{6,22},{8,24},{10,26},{12,28},{14,30},{16,0},... | collective-permute-start | bytes 417800 | tf_op jit(solution)/shard_map/ppermute | solution.py:704
  353.3 14.6 %collective-permute-start.19 = (bf16[32,2176]{1,0:T(8,128)(2,1)S(1)}, bf16[32,2176]{1,0:T(8,128)(2,1)S(1)}, u32[]{:S(2)}, u32[]{:S(2)}) collective-permute-start(bf16[32,2176]{1,0:T(8,128)(2,1)S(1)} %get-tuple-element.240), channel_id=1, source_target_pairs={{0,24},{2,26},{4,28},{6,30},{8,16},{10,18},{12,20},{14,22},{16,8},... | collective-permute-start | bytes 417800 | tf_op jit(solution)/shard_map/ppermute | solution.py:704
  367.9 5.1 %collective-permute-start.20 = (bf16[32,2176]{1,0:T(8,128)(2,1)S(1)}, bf16[32,2176]{1,0:T(8,128)(2,1)S(1)}, u32[]{:S(2)}, u32[]{:S(2)}) collective-permute-start(bf16[32,2176]{1,0:T(8,128)(2,1)S(1)} %fusion.6), channel_id=1, source_target_pairs={{0,1},{1,0},{2,3},{3,2},{4,5},{5,4},{6,7},{7,6},{8,9},{9,8},{10,11... | collective-permute-start | bytes 417800 | tf_op jit(solution)/shard_map/ppermute | solution.py:964

commit v5 on v4

--- a/solution.py
+++ b/solution.py
@@ -16,6 +16,9 @@
 LANES = 128
 VEC = 8
 FF_BLOCK = 512
+UP_PIECES = ((0, 2), (2, 4))
+DOWN_PIECES = ((0, 2), (2, 3), (3, 4))
+PIECES = UP_PIECES + DOWN_PIECES
 VMEM_LIMIT = 60 * 1024 * 1024
 
 
@@ -253,8 +256,8 @@
     r_ref, dbuf_ref, gup_ref, gdn_ref, gb_ref, gdb_ref = refs[:6]
     refs = refs[6:]
     if last:
-        lows = refs[:4]
-        refs = refs[4:]
+        lows = refs[: len(PIECES)]
+        refs = refs[len(PIECES) :]
     (
         flat_s,
         flatT_s,
@@ -307,17 +310,12 @@
     gdn_ref[...] = gdn
     gb_ref[...] = gbias
     if last:
-        early = step < pl.num_programs(0) // 2
-
-        @pl.when(early)
-        def _():
-            lows[0][...] = gup.astype(BF)
-            lows[2][...] = gdn.astype(BF)
-
-        @pl.when(jnp.logical_not(early))
-        def _():
-            lows[1][...] = gup.astype(BF)
-            lows[3][...] = gdn.astype(BF)
+        for at, (low, (begin, end)) in enumerate(zip(lows, PIECES)):
+            value = gup if at < len(UP_PIECES) else gdn
+
+            @pl.when((step >= begin) & (step < end))
+            def _(low=low, value=value):
+                low[...] = value.astype(BF)
 
     @pl.when(step == pl.num_programs(0) - 1)
     def _():
@@ -556,10 +554,17 @@
     out_ref[...] = total.astype(BF).reshape(images, local_len, width)
 
 
-def sum_kernel(gup_ref, gdn_ref, up_early, up_late, dn_early, dn_late, up_ref, dn_ref):
-    late = pl.program_id(0) >= pl.num_programs(0) // 2
-    got_up = jnp.where(late, up_late[...], up_early[...])
-    got_dn = jnp.where(late, dn_late[...], dn_early[...])
+def sum_kernel(gup_ref, gdn_ref, *refs):
+    up_ref, dn_ref = refs[-2:]
+    step = pl.program_id(0)
+    ups = refs[: len(UP_PIECES)]
+    downs = refs[len(UP_PIECES) : -2]
+    got_up = ups[0][...]
+    for ref, (begin, _) in zip(ups[1:], UP_PIECES[1:]):
+        got_up = jnp.where(step >= begin, ref[...], got_up)
+    got_dn = downs[0][...]
+    for ref, (begin, _) in zip(downs[1:], DOWN_PIECES[1:]):
+        got_dn = jnp.where(step >= begin, ref[...], got_dn)
     up_ref[0] = gup_ref[...] + got_up.astype(F32)
     dn_ref[0] = jnp.transpose(gdn_ref[...] + got_dn.astype(F32))
 
@@ -646,13 +651,13 @@
     other_spec = lambda mb: pl.BlockSpec(
         (seq_count - 1, count, local_len, width), lambda i: (0, max(mb - 1, 0), 0, 0)
     )
-    halved = hidden // FF_BLOCK // 2
-    early_spec = lambda: pl.BlockSpec(
-        (width, FF_BLOCK), lambda i: (0, jnp.minimum(i, halved - 1))
-    )
-    late_spec = lambda: pl.BlockSpec(
-        (width, FF_BLOCK), lambda i: (0, jnp.maximum(i - halved, 0))
-    )
+    assert hidden // FF_BLOCK == UP_PIECES[-1][1] == DOWN_PIECES[-1][1]
+
+    def piece_spec(begin, end):
+        return pl.BlockSpec(
+            (width, FF_BLOCK), lambda i: (0, jnp.clip(i - begin, 0, end - begin - 1))
+        )
+
     misc_spec = pl.BlockSpec((width, LANES), lambda i: (0, 4 * width // LANES))
     moved = struct((experts, room, width), BF)
     merged = struct((experts, window(capacity, MICRO - 1)[0] + room, width), BF)
@@ -724,28 +729,22 @@
             name="assemble",
         )(meta, *held), pieces[1:]
 
-    def scatter_rows(total, far):
-        me = lax.axis_index("dp")
-        value = total.reshape(dp_count // 2, 2, shard, packed_width)
-        for bit in range(bits - 2):
-            mine = lax.bitwise_and(lax.shift_right_logical(me, bit), 1)
-            keep = lax.dynamic_index_in_dim(value, mine, 1, keepdims=False)
-            give = lax.dynamic_index_in_dim(value, 1 - mine, 1, keepdims=False)
-            give = give.astype(BF)
-            value = keep.astype(F32) + across(give, 1 << bit).astype(F32)
-            if bit == 0:
-                mid = value
-            if bit < bits - 3:
-                value = value.reshape(-1, 2, shard, packed_width)
-        value = after(value, *far)
-        high = lax.shift_right_logical(me, bits - 2)
+    def halve(value, bit):
+        mine = lax.bitwise_and(lax.shift_right_logical(lax.axis_index("dp"), bit), 1)
+        value = value.reshape(-1, 2, shard, packed_width)
+        keep = lax.dynamic_index_in_dim(value, mine, 1, keepdims=False)
+        give = lax.dynamic_index_in_dim(value, 1 - mine, 1, keepdims=False).astype(BF)
+        return keep.astype(F32) + across(give, 1 << bit).astype(F32)
+
+    def scatter_far(value):
+        high = lax.shift_right_logical(lax.axis_index("dp"), bits - 2)
         result = lax.dynamic_index_in_dim(value, high, 0, keepdims=False)
         for offset in (1, 2, 3):
             give = lax.dynamic_index_in_dim(
                 value, lax.bitwise_xor(high, offset), 0, keepdims=False
             )
             result = result + across(give.astype(BF), offset << (bits - 2)).astype(F32)
-        return result, mid, value
+        return result
 
     pack_args = (qkv_weight, proj_weight, router_weight.T, vectors)
     packed_shard = pl.pallas_call(
@@ -834,7 +833,7 @@
             grid=(hidden // FF_BLOCK,),
             in_specs=in_specs,
             out_specs=[window_spec(mb), block_spec(max(mb - 1, 0)), *total_specs]
-            + ([early_spec(), late_spec()] * 2 if last else []),
+            + ([piece_spec(*p) for p in PIECES] if last else []),
             out_shape=[
                 merged,
                 moved if first else tailed,
@@ -843,7 +842,11 @@
                 struct((1, hidden), F32),
                 struct((1, width), F32),
             ]
-            + ([struct((width, hidden // 2), BF)] * 4 if last else []),
+            + (
+                [struct((width, (end - begin) * FF_BLOCK), BF) for begin, end in PIECES]
+                if last
+                else []
+            ),
             scratch_shapes=[
                 pltpu.VMEM((slots, width), BF),
                 pltpu.VMEM((width, slots), BF),
@@ -904,7 +907,7 @@
             ],
             input_output_aliases=aliases,
             compiler_params=params(),
-            cost_estimate=cost(1 if last else 17),
+            cost_estimate=cost(0.1 if last else 17),
             name="backward",
         )(*args)
 
@@ -935,7 +938,7 @@
             [own, got, images, dm, packed],
             specs,
             previous,
-            3,
+            0.1,
             "finish",
         )
 
@@ -953,7 +956,7 @@
             out_specs=pl.BlockSpec((count, local_len, width), lambda i: (i, 0, 0)),
             out_shape=struct(images.shape, BF),
             compiler_params=params(),
-            cost_estimate=cost(7),
+            cost_estimate=cost(0.1),
             name="mix",
         )(back, pcol, *tables)
 
@@ -1004,36 +1007,43 @@
             )
         )
     back = exchange(after(results, dbacks[1]))
-    first, far = (), ()
-    if arrived:
-        first, far = (arrived[2], arrived[3]), (gots[0], gots[1])
-    shards, mid, late = scatter_rows(after(dense[0], *first), (*far, back))
-    owns = [after(own, late if mb == MICRO - 1 else mid) for mb, own in enumerate(owns)]
+    part = halve(after(dense[0], *arrived[2:4]), 0)
+    mid = part
+    owns = [after(own, mid) for own in owns]
     grads = None
-    for mb in range(MICRO):
+    for mb in range(MICRO - 1):
         grads = finish(mb, owns[mb], gots[mb], dms[mb], grads)
-    out = mix(back)
 
     if seq_count == 2:
         wide = lambda: pl.BlockSpec((width, FF_BLOCK), lambda i: (0, i))
         final_up, final_down = pl.pallas_call(
             sum_kernel,
             grid=(hidden // FF_BLOCK,),
-            in_specs=[wide(), wide(), *[early_spec(), late_spec()] * 2],
+            in_specs=[wide(), wide(), *[piece_spec(*p) for p in PIECES]],
             out_specs=[
                 pl.BlockSpec((1, width, FF_BLOCK), lambda i: (0, 0, i)),
                 pl.BlockSpec((1, FF_BLOCK, width), lambda i: (0, i, 0)),
             ],
             out_shape=[struct((1, width, hidden), F32), struct((1, hidden, width), F32)],
             compiler_params=params(),
-            cost_estimate=cost(8),
+            cost_estimate=cost(0.1),
             name="sum_experts",
         )(after(gup, mid), gdn, *arrived)
     else:
         sums = [lax.psum(piece, "seq").astype(F32) for piece in pieces]
-        final_up = jnp.concatenate(sums[:2], axis=1)[None]
-        final_down = jnp.swapaxes(jnp.concatenate(sums[2:], axis=1), 0, 1)[None]
+        ups, downs = sums[: len(UP_PIECES)], sums[len(UP_PIECES) :]
+        final_up = jnp.concatenate(ups, axis=1)[None]
+        final_down = jnp.swapaxes(jnp.concatenate(downs, axis=1), 0, 1)[None]
     biases = seq_sum(jnp.concatenate([gbias, gdbias], axis=1))
+    for bit in range(1, bits - 2):
+        part = halve(part, bit)
+    part, grads, final_up, biases, back = lax.optimization_barrier(
+        (part, grads, final_up, biases, back)
+    )
+    shards = scatter_far(part)
+    last_own = after(owns[-1], part)
+    grads = finish(MICRO - 1, last_own, gots[-1], dms[-1], grads)
+    out = mix(back)
     final_up_shift = biases[:, :hidden]
     final_down_shift = biases[:, hidden:]
 

time: 384 us -> 369 us (0.961)
  the two profiles are of different devices: /device:TPU:12 before, /device:TPU:0 now
where the time goes in v5:
time: 369 us; the launch traced here: 361 us
  Pallas kernels  178 us (48%)
  waiting for transfers between devices  81.7 us (22%)
  starting transfers between devices  76.3 us (21%)
  local copies, waits for them, and re-layouts  15.4 us (4%)
  other arithmetic  8.61 us (2%)
    pallas_call x3, Pallas kernels, expert(): pl.pallas_call(functools.partial(expert_kernel, cfg, first, last), grid=(...  59.9 us
    pallas_call x3, Pallas kernels, backward(): pl.pallas_call(functools.partial(backward_kernel, cfg, mb, first, last),...  51.8 us
    all_to_all x7, starting transfers between devices, exchange(): return lax.all_to_all(array, 'dp', split_axis=0, concat_axis=0, tiled=True)  48.9 us
    ppermute x11, waiting for transfers between devices, across(): return lax.ppermute(value, 'dp', [(i, i ^ offset) for i in range(dp_count)])  33.7 us
    pallas_call x3, Pallas kernels, forward(): pl.pallas_call(functools.partial(forward_kernel, cfg, mb), grid=(1,), in_...  33.1 us
    ppermute x3, waiting for transfers between devices, on_device(): lax.ppermute(oth[j - 1], 'seq', [(i, (i + j) % seq_count) for i in range(...  17 us
    ppermute x11, starting transfers between devices, across(): return lax.ppermute(value, 'dp', [(i, i ^ offset) for i in range(dp_count)])  14.4 us
    all_to_all x7, waiting for transfers between devices, exchange(): return lax.all_to_all(array, 'dp', split_axis=0, concat_axis=0, tiled=True)  13.1 us
  transfers between devices with their start and end apart: 30, of which 12 were waited for; matrix products, arithmetic and copies ran while one was open for 3% of the time, Pallas kernels for 49%

profile of v5, /device:TPU:0, one launch (start us, length us, event | category | flops | bytes accessed | tf_op | source)
XLA Modules:
  0.0 361.5 jit_solution(14480575270193035162)
XLA Ops:
  0.7 1.4 concatenate.14.vec_ref
  2.1 1.7 pack.1
  3.7 3.1 collective-permute-start.1
  6.8 2.6 collective-permute-start.2
  9.4 1.8 collective-permute-start.7
  11.2 6.0 %place.1 = (bf16[16,152,512]{2,1,0:T(8,128)(2,1)}, s32[3,2,320]{2,1,0:T(2,128)}, s32[3,320,8]{2,1,0:T(8,128)}) custom-call(s32[1,3,1,2,320]{4,3,2,1,0:T(2,128)} %bitcast.72, bf16[3,320,512]{2,1,0:T(8,128)(2,1)} %refs_7_.11), custom_call_target="tpu_custom_call" | custom-call | flops 8000000000 | bytes 16000000 | tf_op jit(solution)/shard_map/place/pallas_call | solution.py:674
  17.2 3.2 collective-permute-done.2
  21.3 5.5 %all-to-all-start.1 = ((bf16[16,152,512]{2,1,0:T(8,128)(2,1)}), bf16[16,152,512]{2,1,0:T(8,128)(2,1)S(1)}, u32[]{:S(2)}, u32[]{:S(2)}) async-start(bf16[16,152,512]{2,1,0:T(8,128)(2,1)} %get-tuple-element.111), calls=%async_computation.1 | async-start | bytes 4980736 | tf_op jit(solution)/shard_map/all_to_all | solution.py:762
  26.8 1.6 collective-permute-start
  28.4 1.2 pad_maximum_fusion.refs_0_
  29.6 2.0 collective-permute-start.4
  31.6 12.5 %collective-permute-done = bf16[2,320,512]{2,1,0:T(8,128)(2,1)} collective-permute-done((bf16[2,320,512]{2,1,0:T(8,128)(2,1)S(1)}, bf16[2,320,512]{2,1,0:T(8,128)(2,1)}, u32[]{:S(2)}, u32[]{:S(2)}) %collective-permute-start) | collective-permute-done | bytes 655392 | tf_op jit(solution)/shard_map/ppermute | solution.py:667
  44.0 19.0 %collective-permute-done.4.refs_1_ = bf16[4,32,2176]{2,1,0:T(8,128)(2,1)} collective-permute-done((bf16[4,32,2176]{2,1,0:T(8,128)(2,1)S(1)}, bf16[4,32,2176]{2,1,0:T(8,128)(2,1)}, u32[]{:S(2)}, u32[]{:S(2)}) %collective-permute-start.4) | collective-permute-done | bytes 557088 | tf_op jit(solution)/shard_map/ppermute | solution.py:709
  63.6 1.7 collective-permute-done.6.refs_3_
  65.3 3.2 assemble.1.w_ref.refs_3_.refs_9_.wm_ref
  68.6 11.0 %forward.5 = (bf16[16,56,512]{2,1,0:T(8,128)(2,1)}, f32[320,512]{1,0:T(8,128)}, f32[320,128]{1,0:T(8,128)}, bf16[320,512]{1,0:T(8,128)(2,1)}, bf16[512,320]{1,0:...) custom-call(s32[2]{0:T(128)} %pad_add_fusion.meta_ref.refs_0_, ...), custom_call_target="tpu_custom_call" | custom-call | flops 11000000512 | bytes 22000000 | tf_op jit(solution)/shard_map/forward/pallas_call | solution.py:781
  79.6 8.3 %all-to-all-start.3 = ((bf16[16,56,512]{2,1,0:T(8,128)(2,1)}), bf16[16,56,512]{2,1,0:T(8,128)(2,1)S(1)}, u32[]{:S(2)}, u32[]{:S(2)}) async-start(bf16[16,56,512]{2,1,0:T(8,128)(2,1)} %get-tuple-element.114), calls=%async_computation.3 | async-start | bytes 1835008 | tf_op jit(solution)/shard_map/all_to_all | solution.py:762
  87.9 11.0 %forward.4 = (bf16[16,56,512]{2,1,0:T(8,128)(2,1)}, f32[320,512]{1,0:T(8,128)}, f32[320,128]{1,0:T(8,128)}, bf16[320,512]{1,0:T(8,128)(2,1)}, bf16[512,320]{1,0:...) custom-call(s32[2]{0:T(128)} %pad_add_fusion.meta_ref.refs_0_, ...), custom_call_target="tpu_custom_call" | custom-call | flops 11000000512 | bytes 22000000 | tf_op jit(solution)/shard_map/forward/pallas_call | solution.py:781
  99.0 11.0 %forward.3 = (bf16[16,56,512]{2,1,0:T(8,128)(2,1)}, f32[320,512]{1,0:T(8,128)}, f32[320,128]{1,0:T(8,128)}, bf16[320,512]{1,0:T(8,128)(2,1)}, bf16[512,320]{1,0:...) custom-call(s32[2]{0:T(128)} %pad_add_fusion.meta_ref.refs_0_, ...), custom_call_target="tpu_custom_call" | custom-call | flops 11000000512 | bytes 22000000 | tf_op jit(solution)/shard_map/forward/pallas_call | solution.py:781
  110.0 6.1 %all-to-all-start.2 = ((bf16[16,56,512]{2,1,0:T(8,128)(2,1)}), bf16[16,56,512]{2,1,0:T(8,128)(2,1)S(1)}, u32[]{:S(2)}, u32[]{:S(2)}) async-start(bf16[16,56,512]{2,1,0:T(8,128)(2,1)} %get-tuple-element.112), calls=%async_computation.2 | async-start | bytes 1835008 | tf_op jit(solution)/shard_map/all_to_all | solution.py:762
  116.2 18.7 %expert.3 = (bf16[16,152,512]{2,1,0:T(8,128)(2,1)}, bf16[16,56,512]{2,1,0:T(8,128)(2,1)}, f32[512,2048]{1,0:T(8,128)}, f32[512,2048]{1,0:T(8,128)}, f32[1,2048]{1,0:T(1,128)}, /*index=5*/f32[1,512]{1,0:T(1,128)}) custom-call(s32[2]{0:T(128)} %pad_add_fusion.meta_ref.refs_0_, bf16[16,56,512]{2,1,0:T(8,128)(2,1)} %copy-done.7, ...), custom_call_target="tpu_custom_call" | custom-call | flops 19000000512 | bytes 38000000 | tf_op jit(solution)/shard_map/expert/pallas_call | solution.py:831
  134.9 2.1 all-to-all-done.2.refs_1_
  136.9 6.3 %all-to-all-start = ((bf16[16,56,512]{2,1,0:T(8,128)(2,1)}), bf16[16,56,512]{2,1,0:T(8,128)(2,1)S(1)}, u32[]{:S(2)}, u32[]{:S(2)}) async-start(bf16[16,56,512]{2,1,0:T(8,128)(2,1)} %get-tuple-element.109), calls=%async_computation | async-start | bytes 1835008 | tf_op jit(solution)/shard_map/all_to_all | solution.py:762
  143.2 19.8 %expert.4 = (bf16[16,152,512]{2,1,0:T(8,128)(2,1)}, bf16[16,112,512]{2,1,0:T(8,128)(2,1)}, f32[512,2048]{1,0:T(8,128)}, f32[512,2048]{1,0:T(8,128)}, f32[1,2048]{1,0:T(1,128)}, /*index=5*/f32[1,512]{1,0:T(1,128)}) custom-call(s32[2]{0:T(128)} %pad_add_fusion.meta_ref.refs_0_, ...), custom_call_target="tpu_custom_call", output_to_operand_aliasing={{0}: (8, {}), {2}: (9, {}), {3}: (10, {}), {4}: (11, {}), {... | custom-call | flops 19000000512 | bytes 38000000 | tf_op jit(solution)/shard_map/expert/pallas_call | solution.py:831
  163.0 0.9 all-to-all-done.refs_1_
  164.0 6.1 %all-to-all-start.5 = ((bf16[16,56,512]{2,1,0:T(8,128)(2,1)}), bf16[16,56,512]{2,1,0:T(8,128)(2,1)S(1)}, u32[]{:S(2)}, u32[]{:S(2)}) async-start(bf16[16,56,512]{2,1,0:T(8,128)(2,1)} %get-tuple-element.148), calls=%async_computation.5 | async-start | bytes 1835008 | tf_op jit(solution)/shard_map/all_to_all | solution.py:762
  170.1 21.4 %expert.5 = (bf16[16,152,512]{2,1,0:T(8,128)(2,1)}, bf16[16,112,512]{2,1,0:T(8,128)(2,1)}, f32[512,2048]{1,0:T(8,128)}, f32[512,2048]{1,0:T(8,128)}, f32[1,2048]...) custom-call(s32[2]{0:T(128)} %pad_add_fusion.meta_ref.refs_0_, ...), custom_call_target="tpu_custom_call", output_to_operand_aliasing={{0}: (8, {}), {2}: (9, {}), {3}: (10, {}), {4}: (11, {}), {... | custom-call | flops 19000000512 | bytes 38000000 | tf_op jit(solution)/shard_map/expert/pallas_call | solution.py:831
  191.5 0.9 copy-done.6
  192.4 6.2 %all-to-all-start.4 = ((bf16[16,112,512]{2,1,0:T(8,128)(2,1)}), bf16[16,112,512]{2,1,0:T(8,128)(2,1)S(1)}, u32[]{:S(2)}, u32[]{:S(2)}) async-start(bf16[16,112,512]{2,1,0:T(8,128)(2,1)} %get-tuple-element.126), calls=%async_computation.4 | async-start | bytes 3670016 | tf_op jit(solution)/shard_map/all_to_all | solution.py:762
  198.6 1.6 collective-permute-start.8
  200.7 1.5 collective-permute-start.10
  202.7 16.8 %backward.3 = (f32[320,512]{1,0:T(8,128)}, bf16[1,320,512]{2,1,0:T(8,128)(2,1)}, f32[320,512]{1,0:T(8,128)}, f32[512,2048]{1,0:T(8,128)}, f32[128,512]{1,0:T(8,128)}) custom-call(s32[2]{0:T(128)} %pad_add_fusion.meta_ref.refs_0_, s32[3]{0:T(128)} %refs_1_.5, bf16[16,56,512]{2,1,0:T(8,128)(2,1)} %copy-done.6, ...), custom_call_target="tpu_custom_call" | custom-call | flops 16999999488 | bytes 34000000 | tf_op jit(solution)/shard_map/backward/pallas_call | solution.py:897
  219.5 5.4 %collective-permute-done.8.refs_0_ = bf16[512,1024]{1,0:T(8,128)(2,1)S(1)} collective-permute-done((bf16[512,1024]{1,0:T(8,128)(2,1)}, bf16[512,1024]{1,0:T(8,128)(2,1)S(1)}, u32[]{:S(2)}, u32[]{:S(2)}) %collective-permute-start.8) | collective-permute-done | bytes 1048608 | tf_op jit(solution)/shard_map/ppermute | solution.py:984
  224.9 10.1 %all-to-all-done.4.refs_2_ = bf16[16,112,512]{2,1,0:T(8,128)(2,1)S(1)} async-done(((bf16[16,112,512]{2,1,0:T(8,128)(2,1)}), bf16[16,112,512]{2,1,0:T(8,128)(2,1)S(1)}, u32[]{:S(2)}, u32[]{:S(2)}) %all-to-all-start.4) | async-done | bytes 1835040 | tf_op jit(solution)/shard_map/all_to_all | solution.py:762
  235.0 1.2 copy-done.2
  236.2 10.4 %all-to-all-start.6 = ((bf16[16,152,512]{2,1,0:T(8,128)(2,1)}), bf16[16,152,512]{2,1,0:T(8,128)(2,1)S(1)}, u32[]{:S(2)}, u32[]{:S(2)}) async-start(bf16[16,152,512]{2,1,0:T(8,128)(2,1)} %get-tuple-element.187), calls=%async_computation.6 | async-start | bytes 4980736 | tf_op jit(solution)/shard_map/all_to_all | solution.py:762
  246.6 17.3 %backward.4 = (f32[320,512]{1,0:T(8,128)}, bf16[1,320,512]{2,1,0:T(8,128)(2,1)}, f32[320,512]{1,0:T(8,128)}, f32[512,2048]{1,0:T(8,128)}, f32[128,512]{1,0:T(8,128)}) custom-call(s32[2]{0:T(128)} %pad_add_fusion.meta_ref.refs_0_, s32[3]{0:T(128)} %refs_1_.5, bf16[16,112,512]{2,1,0:T(8,128)(2,1)} %copy-done.2, ...), custom_call_target="tpu_custom_call", output_to_operand_aliasing={{3}: (17, {}), {4}: (18, {})} | custom-call | flops 16999999488 | bytes 34000000 | tf_op jit(solution)/shard_map/backward/pallas_call | solution.py:897
  263.9 17.7 %backward.5 = (f32[320,512]{1,0:T(8,128)}, bf16[1,320,512]{2,1,0:T(8,128)(2,1)}, f32[320,512]{1,0:T(8,128)}, bf16[512,2176]{1,0:T(8,128)(2,1)}, f32[128,512]{1,0:T(8,128)}) custom-call(s32[2]{0:T(128)} %pad_add_fusion.meta_ref.refs_0_, s32[3]{0:T(128)} %refs_1_.5, bf16[16,112,512]{2,1,0:T(8,128)(2,1)} %copy-done.2, ...), custom_call_target="tpu_custom_call" | custom-call | flops 100000000 | bytes 200000 | tf_op jit(solution)/shard_map/backward/pallas_call | solution.py:897
  281.7 2.3 dynamic-slice_bitcast_fusion
  284.5 1.6 collective-permute-start.17
  286.6 1.5 collective-permute-start.15
  288.7 1.8 convert_add_fusion
  290.5 1.3 copy-done.3
  291.9 1.7 collective-permute-start.13
  293.6 14.5 %collective-permute-done.15 = bf16[320,512]{1,0:T(8,128)(2,1)S(1)} collective-permute-done((bf16[320,512]{1,0:T(8,128)(2,1)}, bf16[320,512]{1,0:T(8,128)(2,1)S(1)}, u32[]{:S(2)}, u32[]{:S(2)}) %collective-permute-start.15) | collective-permute-done | bytes 327712 | tf_op jit(solution)/shard_map/ppermute | solution.py:1002
  308.1 0.7 copy-done.11
  308.9 2.7 finish.3.refs_0_
  311.6 2.5 collective-permute-done.14
  314.0 2.7 finish.4.refs_0_
  316.7 8.4 %sum_experts.1 = (f32[1,512,2048]{2,1,0:T(8,128)}, f32[1,2048,512]{2,1,0:T(8,128)}) custom-call(f32[512,2048]{1,0:T(8,128)} %get-tuple-element.178.gup_ref, f32[512,2048]{1,0:T(8,128)} %get-tuple-element.179.gdn_ref, bf16[512,1024]{1,0:T(8,128)(2,1)} %copy-done.5, bf16[512,1024]{1,0:T(8,128)(2,1)} %collective-permute-done.9.refs_1_, ...), custom_call_target="tpu_custom_call" | custom-call | flops 100000000 | bytes 200000 | tf_op jit(solution)/shard_map/sum_experts/pallas_call | solution.py:1019
  325.1 2.4 bitcast_add_fusion
  327.5 1.8 fusion.3
  329.3 2.1 collective-permute-start.19
  331.3 2.4 collective-permute-start.20
  334.4 1.5 collective-permute-done.19
  335.9 8.3 %collective-permute-done.20 = bf16[32,2176]{1,0:T(8,128)(2,1)S(1)} collective-permute-done((bf16[32,2176]{1,0:T(8,128)(2,1)S(1)}, bf16[32,2176]{1,0:T(8,128)(2,1)S(1)}, u32[]{:S(2)}, u32[]{:S(2)}) %collective-permute-start.20) | collective-permute-done | bytes 139296 | tf_op jit(solution)/shard_map/ppermute | solution.py:709
  344.2 1.0 fusion.6
  345.3 0.8 collective-permute-start.22
  347.3 5.8 %mix.1 = bf16[3,320,512]{2,1,0:T(8,128)(2,1)} custom-call(bf16[16,152,512]{2,1,0:T(8,128)(2,1)} %copy-done.1, s32[3,320,8]{2,1,0:T(8,128)} %get-tuple-element.129.refs_3_.pcol_ref, f32[320,128]{1,0:T(8,128)} %get-tuple-element.149.refs_4_.refs_0_, f32[320,512]{1,0:T(8,128)} %get-tuple-element.150.refs_5_.refs_1_, ...), custom_call_target="tpu_custom_call" | custom-call | flops 100000000 | bytes 200000 | tf_op jit(solution)/shard_map/mix/pallas_call | solution.py:948
  353.1 0.7 copy-done.12
  353.9 2.7 finish.5
  356.6 1.0 convert_add_fusion.1
  357.6 0.8 slice_reduce_fusion
  358.4 0.7 slice.58
  (76 shorter events, 8.1 us)
Async XLA Ops:
  0.6 8.7 %copy-start = (bf16[3,320,512]{2,1,0:T(8,128)(2,1)S(1)}, bf16[3,320,512]{2,1,0:T(8,128)(2,1)}, u32[]{:S(2)}) copy-start(bf16[3,320,512]{2,1,0:T(8,128)(2,1)} %x_ref.5) | copy-start | bytes 2949124
  3.7 13.5 %collective-permute-start.1 = (bf16[32,2176]{1,0:T(8,128)(2,1)}, bf16[32,2176]{1,0:T(8,128)(2,1)S(1)}, u32[]{:S(2)}, u32[]{:S(2)}) collective-permute-start(bf16[32,2176]{1,0:T(8,128)(2,1)} %pack.1), channel_id=1, source_target_pairs={{0,8},{2,10},{4,12},{6,14},{8,0},{10,2},{12,4},{14,6},{16,24},{18,... | collective-permute-start | bytes 417800 | tf_op jit(solution)/shard_map/ppermute | solution.py:709
  6.8 13.6 %collective-permute-start.2 = (bf16[32,2176]{1,0:T(8,128)(2,1)}, bf16[32,2176]{1,0:T(8,128)(2,1)S(1)}, u32[]{:S(2)}, u32[]{:S(2)}) collective-permute-start(bf16[32,2176]{1,0:T(8,128)(2,1)} %pack.1), channel_id=1, source_target_pairs={{0,16},{2,18},{4,20},{6,22},{8,24},{10,26},{12,28},{14,30},{16,0},... | collective-permute-start | bytes 417800 | tf_op jit(solution)/shard_map/ppermute | solution.py:709
  9.4 11.0 %collective-permute-start.3 = (bf16[32,2176]{1,0:T(8,128)(2,1)}, bf16[32,2176]{1,0:T(8,128)(2,1)S(1)}, u32[]{:S(2)}, u32[]{:S(2)}) collective-permute-start(bf16[32,2176]{1,0:T(8,128)(2,1)} %pack.1), channel_id=1, source_target_pairs={{0,24},{2,26},{4,28},{6,30},{8,16},{10,18},{12,20},{14,22},{16,8},... | collective-permute-start | bytes 417800 | tf_op jit(solution)/shard_map/ppermute | solution.py:709
  9.4 11.0 %collective-permute-start.7 = (bf16[1,320,512]{2,1,0:T(8,128)(2,1)S(1)}, bf16[1,320,512]{2,1,0:T(8,128)(2,1)S(1)}, u32[]{:S(2)}, u32[]{:S(2)}) collective-permute-start(bf16[1,320,512]{2,1,0:T(8,128)(2,1)S(1)} %slice.43), channel_id=1, source_target_pairs={{1,0},{0,1},{3,2},{2,3},{5,4},{4,5},{7,6},{6,7},{9,8},{8,9},{11,10... | collective-permute-start | bytes 983048 | tf_op jit(solution)/shard_map/ppermute | solution.py:667
  17.2 3.2 copy-start.13
  20.4 0.7 copy-start.14
  20.4 0.7 copy-start.15
  20.4 0.8 copy-start.18
  21.3 58.3 %all-to-all-start.1 = ((bf16[16,152,512]{2,1,0:T(8,128)(2,1)}), bf16[16,152,512]{2,1,0:T(8,128)(2,1)S(1)}, u32[]{:S(2)}, u32[]{:S(2)}) async-start(bf16[16,152,512]{2,1,0:T(8,128)(2,1)} %get-tuple-element.111), calls=%async_computation.1 | async-start | bytes 4980736 | tf_op jit(solution)/shard_map/all_to_all | solution.py:762
  26.8 17.2 %collective-permute-start = (bf16[2,320,512]{2,1,0:T(8,128)(2,1)S(1)}, bf16[2,320,512]{2,1,0:T(8,128)(2,1)}, u32[]{:S(2)}, u32[]{:S(2)}) collective-permute-start(bf16[2,320,512]{2,1,0:T(8,128)(2,1)S(1)} %slice.42), channel_id=1, source_target_pairs={{1,0},{0,1},{3,2},{2,3},{5,4},{4,5},{7,6},{6,7},{9,8},{8,9},{11,10... | collective-permute-start | bytes 1966088 | tf_op jit(solution)/shard_map/ppermute | solution.py:667
  29.6 35.8 %copy-start.10 = (bf16[4,32,2176]{2,1,0:T(8,128)(2,1)}, bf16[4,32,2176]{2,1,0:T(8,128)(2,1)S(1)}, u32[]{:S(2)}) copy-start(bf16[4,32,2176]{2,1,0:T(8,128)(2,1)S(1)} %pad_maximum_fusion.refs_0_) | copy-start | bytes 1671172
  29.6 33.5 %collective-permute-start.4 = (bf16[4,32,2176]{2,1,0:T(8,128)(2,1)S(1)}, bf16[4,32,2176]{2,1,0:T(8,128)(2,1)}, u32[]{:S(2)}, u32[]{:S(2)}) collective-permute-start(bf16[4,32,2176]{2,1,0:T(8,128)(2,1)S(1)} %pad_maximum_fusion.refs_0_), channel_id=1, source_target_pairs={{0,4},{2,6},{4,0},{6,2},{8,12},{10,14},{12,8},{14,10},{16,20},{18,... | collective-permute-start | bytes 1671176 | tf_op jit(solution)/shard_map/ppermute | solution.py:709
  31.6 32.1 %collective-permute-start.5 = (bf16[4,32,2176]{2,1,0:T(8,128)(2,1)S(1)}, bf16[4,32,2176]{2,1,0:T(8,128)(2,1)}, u32[]{:S(2)}, u32[]{:S(2)}) collective-permute-start(bf16[4,32,2176]{2,1,0:T(8,128)(2,1)S(1)} %pad_maximum_fusion.refs_0_), channel_id=1, source_target_pairs={{0,2},{2,0},{4,6},{6,4},{8,10},{10,8},{12,14},{14,12},{16,18},{18,... | collective-permute-start | bytes 1671176 | tf_op jit(solution)/shard_map/ppermute | solution.py:709
  63.0 2.3 collective-permute-start.6
  79.6 19.4 %copy-start.4 = (bf16[16,152,512]{2,1,0:T(8,128)(2,1)}, bf16[16,152,512]{2,1,0:T(8,128)(2,1)S(1)}, u32[]{:S(2)}) copy-start(bf16[16,152,512]{2,1,0:T(8,128)(2,1)S(1)} %all-to-all-done.1.refs_2_) | copy-start | bytes 7471108
  79.6 30.4 %all-to-all-start.3 = ((bf16[16,56,512]{2,1,0:T(8,128)(2,1)}), bf16[16,56,512]{2,1,0:T(8,128)(2,1)S(1)}, u32[]{:S(2)}, u32[]{:S(2)}) async-start(bf16[16,56,512]{2,1,0:T(8,128)(2,1)} %get-tuple-element.114), calls=%async_computation.3 | async-start | bytes 1835008 | tf_op jit(solution)/shard_map/all_to_all | solution.py:762
  110.0 6.1 %copy-start.7 = (bf16[16,56,512]{2,1,0:T(8,128)(2,1)}, bf16[16,56,512]{2,1,0:T(8,128)(2,1)S(1)}, u32[]{:S(2)}) copy-start(bf16[16,56,512]{2,1,0:T(8,128)(2,1)S(1)} %all-to-all-done.3.refs_1_) | copy-start | bytes 2752516
  110.0 26.9 %all-to-all-start.2 = ((bf16[16,56,512]{2,1,0:T(8,128)(2,1)}), bf16[16,56,512]{2,1,0:T(8,128)(2,1)S(1)}, u32[]{:S(2)}, u32[]{:S(2)}) async-start(bf16[16,56,512]{2,1,0:T(8,128)(2,1)} %get-tuple-element.112), calls=%async_computation.2 | async-start | bytes 1835008 | tf_op jit(solution)/shard_map/all_to_all | solution.py:762
  136.9 6.3 %copy-start.9 = (bf16[16,56,512]{2,1,0:T(8,128)(2,1)}, bf16[16,56,512]{2,1,0:T(8,128)(2,1)S(1)}, u32[]{:S(2)}) copy-start(bf16[16,56,512]{2,1,0:T(8,128)(2,1)S(1)} %all-to-all-done.2.refs_1_) | copy-start | bytes 2752516
  136.9 27.0 %all-to-all-start = ((bf16[16,56,512]{2,1,0:T(8,128)(2,1)}), bf16[16,56,512]{2,1,0:T(8,128)(2,1)S(1)}, u32[]{:S(2)}, u32[]{:S(2)}) async-start(bf16[16,56,512]{2,1,0:T(8,128)(2,1)} %get-tuple-element.109), calls=%async_computation | async-start | bytes 1835008 | tf_op jit(solution)/shard_map/all_to_all | solution.py:762
  163.9 6.1 %copy-start.8 = (bf16[16,56,512]{2,1,0:T(8,128)(2,1)}, bf16[16,56,512]{2,1,0:T(8,128)(2,1)S(1)}, u32[]{:S(2)}) copy-start(bf16[16,56,512]{2,1,0:T(8,128)(2,1)S(1)} %all-to-all-done.refs_1_) | copy-start | bytes 2752516
  164.0 27.5 %all-to-all-start.5 = ((bf16[16,56,512]{2,1,0:T(8,128)(2,1)}), bf16[16,56,512]{2,1,0:T(8,128)(2,1)S(1)}, u32[]{:S(2)}, u32[]{:S(2)}) async-start(bf16[16,56,512]{2,1,0:T(8,128)(2,1)} %get-tuple-element.148), calls=%async_computation.5 | async-start | bytes 1835008 | tf_op jit(solution)/shard_map/all_to_all | solution.py:762
  191.4 0.9 copy-start.6
  192.4 42.6 %all-to-all-start.4 = ((bf16[16,112,512]{2,1,0:T(8,128)(2,1)}), bf16[16,112,512]{2,1,0:T(8,128)(2,1)S(1)}, u32[]{:S(2)}, u32[]{:S(2)}) async-start(bf16[16,112,512]{2,1,0:T(8,128)(2,1)} %get-tuple-element.126), calls=%async_computation.4 | async-start | bytes 3670016 | tf_op jit(solution)/shard_map/all_to_all | solution.py:762
  198.6 26.3 %collective-permute-start.8 = (bf16[512,1024]{1,0:T(8,128)(2,1)}, bf16[512,1024]{1,0:T(8,128)(2,1)S(1)}, u32[]{:S(2)}, u32[]{:S(2)}) collective-permute-start(bf16[512,1024]{1,0:T(8,128)(2,1)} %get-tuple-element.127), channel_id=1, source_target_pairs={{0,1},{1,0},{2,3},{3,2},{4,5},{5,4},{6,7},{7,6},{8,9},{9,8},{10,11... | collective-permute-start | bytes 3145736 | tf_op jit(solution)/shard_map/ppermute | solution.py:984
  200.2 63.8 %collective-permute-start.9 = (bf16[512,1024]{1,0:T(8,128)(2,1)}, bf16[512,1024]{1,0:T(8,128)(2,1)}, u32[]{:S(2)}, u32[]{:S(2)}) collective-permute-start(bf16[512,1024]{1,0:T(8,128)(2,1)} %get-tuple-element.162), channel_id=1, source_target_pairs={{0,1},{1,0},{2,3},{3,2},{4,5},{5,4},{6,7},{7,6},{8,9},{9,8},{10,11... | collective-permute-start | bytes 3145736 | tf_op jit(solution)/shard_map/ppermute | solution.py:984
  200.7 81.0 %collective-permute-start.10 = (bf16[512,1024]{1,0:T(8,128)(2,1)}, bf16[512,1024]{1,0:T(8,128)(2,1)}, u32[]{:S(2)}, u32[]{:S(2)}) collective-permute-start(bf16[512,1024]{1,0:T(8,128)(2,1)} %get-tuple-element.166), channel_id=1, source_target_pairs={{0,1},{1,0},{2,3},{3,2},{4,5},{5,4},{6,7},{7,6},{8,9},{9,8},{10,11... | collective-permute-start | bytes 3145736 | tf_op jit(solution)/shard_map/ppermute | solution.py:984
  202.2 79.5 %collective-permute-start.11 = (bf16[512,512]{1,0:T(8,128)(2,1)}, bf16[512,512]{1,0:T(8,128)(2,1)}, u32[]{:S(2)}, u32[]{:S(2)}) collective-permute-start(bf16[512,512]{1,0:T(8,128)(2,1)} %get-tuple-element.167), channel_id=1, source_target_pairs={{0,1},{1,0},{2,3},{3,2},{4,5},{5,4},{6,7},{7,6},{8,9},{9,8},{10,11... | collective-permute-start | bytes 1572872 | tf_op jit(solution)/shard_map/ppermute | solution.py:984
  224.9 39.0 %copy-start.5 = (bf16[512,1024]{1,0:T(8,128)(2,1)}, bf16[512,1024]{1,0:T(8,128)(2,1)S(1)}, u32[]{:S(2)}) copy-start(bf16[512,1024]{1,0:T(8,128)(2,1)S(1)} %collective-permute-done.8.refs_0_) | copy-start | bytes 3145732
  235.0 1.2 copy-start.2
  236.2 91.3 %all-to-all-start.6 = ((bf16[16,152,512]{2,1,0:T(8,128)(2,1)}), bf16[16,152,512]{2,1,0:T(8,128)(2,1)S(1)}, u32[]{:S(2)}, u32[]{:S(2)}) async-start(bf16[16,152,512]{2,1,0:T(8,128)(2,1)} %get-tuple-element.187), calls=%async_computation.6 | async-start | bytes 4980736 | tf_op jit(solution)/shard_map/all_to_all | solution.py:762
  281.6 2.9 copy-start.16
  281.7 2.9 copy-start.17
  284.0 4.7 %collective-permute-start.12 = (bf16[8,32,2176]{2,1,0:T(8,128)(2,1)}, bf16[8,32,2176]{2,1,0:T(8,128)(2,1)}, u32[]{:S(2)}, u32[]{:S(2)}) collective-permute-start(bf16[8,32,2176]{2,1,0:T(8,128)(2,1)} %dynamic-slice_bitcast_fusion), channel_id=1, source_target_pairs={{0,2},{2,0},{4,6},{6,4},{8,10},{10,8},{12,14},{14,12},{16,18},{18,... | collective-permute-start | bytes 3342344 | tf_op jit(solution)/shard_map/ppermute | solution.py:709
  284.5 9.1 %collective-permute-start.17 = (bf16[1,2560]{1,0:T(2,128)(2,1)S(1)}, bf16[1,2560]{1,0:T(2,128)(2,1)S(1)}, u32[]{:S(2)}, u32[]{:S(2)}) collective-permute-start(bf16[1,2560]{1,0:T(2,128)(2,1)S(1)} %convert_element_type.71), channel_id=1, source_target_pairs={{0,1},{1,0},{2,3},{3,2},{4,5},{5,4},{6,7},{7,6},{8,9},{9,8},{10,11... | collective-permute-start | bytes 15368 | tf_op jit(solution)/shard_map/ppermute | solution.py:967
  286.1 30.6 %collective-permute-start.16 = (bf16[512,512]{1,0:T(8,128)(2,1)}, bf16[512,512]{1,0:T(8,128)(2,1)}, u32[]{:S(2)}, u32[]{:S(2)}) collective-permute-start(bf16[512,512]{1,0:T(8,128)(2,1)} %get-tuple-element.182), channel_id=1, source_target_pairs={{0,1},{1,0},{2,3},{3,2},{4,5},{5,4},{6,7},{7,6},{8,9},{9,8},{10,11... | collective-permute-start | bytes 1572872 | tf_op jit(solution)/shard_map/ppermute | solution.py:984
  286.6 21.5 %collective-permute-start.15 = (bf16[320,512]{1,0:T(8,128)(2,1)}, bf16[320,512]{1,0:T(8,128)(2,1)S(1)}, u32[]{:S(2)}, u32[]{:S(2)}) collective-permute-start(bf16[320,512]{1,0:T(8,128)(2,1)} %bitcast.23), channel_id=1, source_target_pairs={{0,1},{1,0},{2,3},{3,2},{4,5},{5,4},{6,7},{7,6},{8,9},{9,8},{10,11... | collective-permute-start | bytes 983048 | tf_op jit(solution)/shard_map/ppermute | solution.py:1002
  288.1 25.9 %collective-permute-start.14 = (bf16[320,512]{1,0:T(8,128)(2,1)}, bf16[320,512]{1,0:T(8,128)(2,1)}, u32[]{:S(2)}, u32[]{:S(2)}) collective-permute-start(bf16[320,512]{1,0:T(8,128)(2,1)} %bitcast.21), channel_id=1, source_target_pairs={{0,1},{1,0},{2,3},{3,2},{4,5},{5,4},{6,7},{7,6},{8,9},{9,8},{10,11... | collective-permute-start | bytes 983048 | tf_op jit(solution)/shard_map/ppermute | solution.py:1002
  290.5 1.4 copy-start.3
  291.9 33.2 %collective-permute-start.13 = (bf16[4,32,2176]{2,1,0:T(8,128)(2,1)S(1)}, bf16[4,32,2176]{2,1,0:T(8,128)(2,1)S(1)}, u32[]{:S(2)}, u32[]{:S(2)}) collective-permute-start(bf16[4,32,2176]{2,1,0:T(8,128)(2,1)S(1)} %fusion), channel_id=1, source_target_pairs={{0,4},{2,6},{4,0},{6,2},{8,12},{10,14},{12,8},{14,10},{16,20},{18,... | collective-permute-start | bytes 1671176 | tf_op jit(solution)/shard_map/ppermute | solution.py:709
  308.1 0.7 copy-start.11
  327.5 19.8 %copy-start.1 = (bf16[16,152,512]{2,1,0:T(8,128)(2,1)}, bf16[16,152,512]{2,1,0:T(8,128)(2,1)S(1)}, u32[]{:S(2)}) copy-start(bf16[16,152,512]{2,1,0:T(8,128)(2,1)S(1)} %all-to-all-done.6.back_ref) | copy-start | bytes 7471108
  329.3 6.7 %collective-permute-start.19 = (bf16[32,2176]{1,0:T(8,128)(2,1)S(1)}, bf16[32,2176]{1,0:T(8,128)(2,1)S(1)}, u32[]{:S(2)}, u32[]{:S(2)}) collective-permute-start(bf16[32,2176]{1,0:T(8,128)(2,1)S(1)} %get-tuple-element.251), channel_id=1, source_target_pairs={{0,8},{2,10},{4,12},{6,14},{8,0},{10,2},{12,4},{14,6},{16,24},{18,... | collective-permute-start | bytes 417800 | tf_op jit(solution)/shard_map/ppermute | solution.py:709
  331.3 12.9 %collective-permute-start.20 = (bf16[32,2176]{1,0:T(8,128)(2,1)S(1)}, bf16[32,2176]{1,0:T(8,128)(2,1)S(1)}, u32[]{:S(2)}, u32[]{:S(2)}) collective-permute-start(bf16[32,2176]{1,0:T(8,128)(2,1)S(1)} %get-tuple-element.253), channel_id=1, source_target_pairs={{0,16},{2,18},{4,20},{6,22},{8,24},{10,26},{12,28},{14,30},{16,0},... | collective-permute-start | bytes 417800 | tf_op jit(solution)/shard_map/ppermute | solution.py:709
  333.7 10.5 %collective-permute-start.21 = (bf16[32,2176]{1,0:T(8,128)(2,1)S(1)}, bf16[32,2176]{1,0:T(8,128)(2,1)S(1)}, u32[]{:S(2)}, u32[]{:S(2)}) collective-permute-start(bf16[32,2176]{1,0:T(8,128)(2,1)S(1)} %get-tuple-element.252), channel_id=1, source_target_pairs={{0,24},{2,26},{4,28},{6,30},{8,16},{10,18},{12,20},{14,22},{16,8},... | collective-permute-start | bytes 417800 | tf_op jit(solution)/shard_map/ppermute | solution.py:709
  333.8 19.3 %collective-permute-start.18 = (bf16[320,512]{1,0:T(8,128)(2,1)}, bf16[320,512]{1,0:T(8,128)(2,1)S(1)}, u32[]{:S(2)}, u32[]{:S(2)}) collective-permute-start(bf16[320,512]{1,0:T(8,128)(2,1)} %bitcast.71), channel_id=1, source_target_pairs={{0,1},{1,0},{2,3},{3,2},{4,5},{5,4},{6,7},{7,6},{8,9},{9,8},{10,11... | collective-permute-start | bytes 983048 | tf_op jit(solution)/shard_map/ppermute | solution.py:1002
  345.3 11.3 %collective-permute-start.22 = (bf16[32,2176]{1,0:T(8,128)(2,1)S(1)}, bf16[32,2176]{1,0:T(8,128)(2,1)S(1)}, u32[]{:S(2)}, u32[]{:S(2)}) collective-permute-start(bf16[32,2176]{1,0:T(8,128)(2,1)S(1)} %fusion.6), channel_id=1, source_target_pairs={{0,1},{1,0},{2,3},{3,2},{4,5},{5,4},{6,7},{7,6},{8,9},{9,8},{10,11... | collective-permute-start | bytes 417800 | tf_op jit(solution)/shard_map/ppermute | solution.py:967
  353.1 0.7 copy-start.12
